TPU v7x, 32 devices: a whole 2x2x4 slice. The times are simulated.
32 devices in a mesh: dp: 4 (over y, core), expert: 8 (over z, x).
Axes of the slice: x: 2, y: 2, z: 4, core: 2. Of those that a mesh axis runs over, the one named last changes fastest.
Arguments:
- tokens: bfloat16 [4096, 1024], P(('dp', 'expert')), may hold values from -6 to 6
- cotangent: bfloat16 [4096, 1024], P(('dp', 'expert')), may hold values from -2 to 2
- expert_ids: int32 [4096, 10], P(('dp', 'expert')), may hold values from 0 to 31, all different within a row; in each aligned block of 128 rows (0 to 127, 128 to 255, ...) at most 48 rows name the same one
- gate_weights: bfloat16 [4096, 10], P(('dp', 'expert')), may hold values from 0.019897461 to 0.29882812
- expert_weights: bfloat16 [32, 3, 1024, 512], P(('dp', 'expert')), may hold values from -0.1875 to 0.1875
- shared_weights: bfloat16 [3, 1024, 512], replicated, may hold values from -0.1875 to 0.1875
Outputs:
- grad_tokens: bfloat16 [4096, 1024], P(('dp', 'expert'))
- grad_gates: bfloat16 [4096, 10], P(('dp', 'expert'))
- grad_experts: bfloat16 [32, 3, 1024, 512], P(('dp', 'expert'))
- grad_shared: float32 [3, 1024, 512], P(None, 'dp')
Inputs may be any that keep to these rules, and one draw needn't show every extreme that they name: `expert_ids`: each token names 10 different experts. Among the 128 tokens of one device no expert is named more than 48 times, and in some device's tokens some expert is named exactly 48 times.
All inputs are finite; a program needn't handle non-finite values.
Results may differ from a plain program's by a relative error of at most 0.0052.
Values may be sent and summed in bfloat16 or wider, within the bound.
No kernel may reach another device: no remote copies, remote signals or barrier semaphores. Data moves between devices by JAX's collectives and lax.ppermute only.
A program may use at most 128 MiB of HBM per device.

v0:
```python
import jax
import jax.numpy as jnp
from jax import lax
from jax.sharding import PartitionSpec as P


def silu_parts(pre):
    sigma = jax.nn.sigmoid(pre)
    return (pre * sigma, sigma * (1.0 + pre * (1.0 - sigma)))


def contract_rows(left, right):
    return lax.dot_general(
        left, right, (((0,), (0,)), ((), ())), preferred_element_type=jnp.float32
    )


def expert_grads(inputs, upstream, scales, weight):
    hidden_units = weight.shape[2]
    paired = jnp.concatenate([weight[0], weight[1]], axis=1)
    gate_up = jnp.dot(inputs, paired, preferred_element_type=jnp.float32)
    pre_gate = gate_up[:, :hidden_units]
    pre_up = gate_up[:, hidden_units:]
    back = jnp.dot(upstream, weight[2], preferred_element_type=jnp.float32)
    activated, slope = silu_parts(pre_gate)
    hidden = activated * pre_up
    gate_grad = jnp.sum(hidden * back, axis=1)
    scaled = scales[:, None] * back
    grad_gate_in = (scaled * pre_up * slope).astype(jnp.bfloat16)
    grad_up_in = (scaled * activated).astype(jnp.bfloat16)
    both = jnp.concatenate([grad_gate_in, grad_up_in], axis=1)
    input_grad = lax.dot_general(
        both, paired, (((1,), (1,)), ((), ())), preferred_element_type=jnp.float32
    )
    hidden_b = hidden.astype(jnp.bfloat16)
    scaled_up = (scales[:, None] * upstream.astype(jnp.float32)).astype(jnp.bfloat16)
    return (input_grad, gate_grad, grad_gate_in, grad_up_in, hidden_b, scaled_up)


def weight_terms(inputs, grad_gate_in, grad_up_in, scaled_up, hidden_b):
    return jnp.stack(
        [
            contract_rows(inputs, grad_gate_in),
            contract_rows(inputs, grad_up_in),
            contract_rows(scaled_up, hidden_b),
        ],
        axis=0,
    )


def shards(tokens, cotangent, expert_ids, gate_weights, expert_weights, shared_weights):
    tok_rows, model_width = tokens.shape
    top_count = expert_ids.shape[1]
    data_count = lax.axis_size("dp")
    expert_count = lax.axis_size("expert")
    devices = data_count * expert_count
    capacity = max(2, (6 * tok_rows * top_count + 5 * devices - 1) // (5 * devices))
    slot_total = devices * capacity
    pair_count = tok_rows * top_count
    row_ids = jnp.arange(tok_rows, dtype=jnp.int32)
    earlier_mask = (row_ids[:, None] > row_ids[None, :]).astype(jnp.bfloat16)
    padded_tokens = jnp.concatenate([tokens, jnp.zeros((1, model_width), jnp.bfloat16)], axis=0)
    padded_cotangent = jnp.concatenate(
        [cotangent, jnp.zeros((1, model_width), jnp.bfloat16)], axis=0
    )
    matches = expert_ids[:, :, None] == jnp.arange(devices, dtype=jnp.int32)
    per_token = jnp.sum(matches, axis=1).astype(jnp.bfloat16)
    before = jnp.dot(earlier_mask, per_token, preferred_element_type=jnp.float32)
    slot_index = jnp.sum(jnp.where(matches, before[:, None, :], 0.0), axis=2).astype(jnp.int32)
    position = expert_ids * capacity + slot_index
    slot_table = (
        jnp.full((slot_total,), pair_count, jnp.int32)
        .at[position.reshape(-1)]
        .set(jnp.arange(pair_count, dtype=jnp.int32))
    )
    token_index = slot_table // top_count
    padded_gates = jnp.concatenate(
        [gate_weights.reshape(-1), jnp.zeros((1,), jnp.bfloat16)], axis=0
    )
    send_tokens = padded_tokens[token_index].reshape(
        data_count, expert_count, capacity, model_width
    )
    send_cotangent = padded_cotangent[token_index].reshape(
        data_count, expert_count, capacity, model_width
    )
    send_gates = padded_gates[slot_table].reshape(data_count, expert_count, capacity)
    arrived = (
        lax.all_to_all(
            lax.all_to_all(send_tokens, "dp", split_axis=0, concat_axis=0, tiled=True),
            "expert",
            split_axis=1,
            concat_axis=1,
            tiled=True,
        ),
        lax.all_to_all(
            lax.all_to_all(send_cotangent, "dp", split_axis=0, concat_axis=0, tiled=True),
            "expert",
            split_axis=1,
            concat_axis=1,
            tiled=True,
        ),
        lax.all_to_all(
            lax.all_to_all(send_gates, "dp", split_axis=0, concat_axis=0, tiled=True),
            "expert",
            split_axis=1,
            concat_axis=1,
            tiled=True,
        ),
    )
    arrived_tokens = arrived[0].reshape(slot_total, model_width)
    routed = expert_grads(
        arrived_tokens,
        arrived[1].reshape(slot_total, model_width),
        arrived[2].reshape(slot_total).astype(jnp.float32),
        expert_weights[0],
    )
    grad_experts = weight_terms(arrived_tokens, routed[2], routed[3], routed[5], routed[4]).astype(
        jnp.bfloat16
    )[None]
    outgoing_input = (
        routed[0].astype(jnp.bfloat16).reshape(data_count, expert_count, capacity, model_width)
    )
    outgoing_gate = routed[1].astype(jnp.bfloat16).reshape(data_count, expert_count, capacity)
    returned = (
        lax.all_to_all(
            lax.all_to_all(outgoing_input, "dp", split_axis=0, concat_axis=0, tiled=True),
            "expert",
            split_axis=1,
            concat_axis=1,
            tiled=True,
        ),
        lax.all_to_all(
            lax.all_to_all(outgoing_gate, "dp", split_axis=0, concat_axis=0, tiled=True),
            "expert",
            split_axis=1,
            concat_axis=1,
            tiled=True,
        ),
    )
    flat_back = returned[0].reshape(slot_total, model_width)
    routed_sum = jnp.sum(flat_back[position].astype(jnp.float32), axis=1)
    grad_gates = returned[1].reshape(slot_total)[position]
    shared = expert_grads(tokens, cotangent, jnp.ones((tok_rows,), jnp.float32), shared_weights)
    grad_tokens = (routed_sum + shared[0]).astype(jnp.bfloat16)
    kept_rows = model_width // data_count
    shared_units = shared_weights.shape[2]
    upstream_cols = shared[5]
    kept = lax.psum_scatter(
        jnp.concatenate(
            [
                contract_rows(tokens, shared[2]),
                contract_rows(tokens, shared[3]),
                contract_rows(upstream_cols, shared[4]),
            ],
            axis=1,
        ),
        "dp",
        scatter_dimension=0,
        tiled=True,
    )
    totals = lax.psum(kept, "expert")
    grad_shared = jnp.transpose(totals.reshape(kept_rows, 3, shared_units), (1, 0, 2))
    return (grad_tokens, grad_gates, grad_experts, grad_shared)


def solution(mesh):
    placed = (
        P(("dp", "expert"), None),
        P(("dp", "expert"), None),
        P(("dp", "expert"), None),
        P(("dp", "expert"), None),
        P(("dp", "expert"), None, None, None),
        P(),
    )
    return jax.shard_map(
        shards,
        mesh=mesh,
        in_specs=placed,
        out_specs=(
            P(("dp", "expert"), None),
            P(("dp", "expert"), None),
            P(("dp", "expert"), None, None, None),
            P(None, "dp", None),
        ),
        check_vma=False,
    )
```

profile of v0, /device:TPU:0, one launch (start us, length us, event | category | flops | bytes accessed | tf_op | source)
XLA Modules:
  0.0 506.0 jit_solution(18286118189874244357)
XLA Ops:
  9.8 5.2 %scatter_custom_fusion = s32[1536]{0:T(1024)S(1)} fusion(s32[1280]{0:T(1024)S(1)} %fusion.35, s32[1280]{0:T(1024)S(1)} %iota.14, s32[]{:T(128)} %constant.14.clone.1), kind=kCustom, calls=%fused_computation.78 | custom fusion | bytes 6148 | tf_op jit(solution)/shard_map/scatter | solution.py:74
  16.1 9.5 %gather_fusion = bf16[1536]{0:T(1024)(128)(2,1)S(1)} fusion(bf16[1281]{0:T(1024)(128)(2,1)S(1)} %pad_maximum_fusion.14, s32[2048]{0:T(1024)S(1)} %get-tuple-element.42), kind=kCustom, calls=%fused_computation | custom fusion | bytes 12288 | tf_op jit(solution)/shard_map/gather | solution.py:86
  25.8 7.9 %all_to_all.50 = bf16[4,2,192]{2,1,0:T(2,128)(2,1)S(1)} all-to-all(bf16[4,2,192]{2,1,0:T(2,128)(2,1)S(1)} %reshape.207), channel_id=1, replica_groups=mesh['dp'=4,'expert'=8] {'dp'}, dimensions={0} | all-to-all | bytes 6144 | tf_op jit(solution)/shard_map/all_to_all | solution.py:103
  34.3 5.8 %all-to-all-start.1 = ((bf16[4,8,48]{2,0,1:T(4,128)(2,1)}), bf16[4,8,48]{2,0,1:T(4,128)(2,1)S(1)}, u32[]{:S(2)}, u32[]{:S(2)}) async-start(bf16[4,8,48]{2,0,1:T(4,128)(2,1)} %copy.88), calls=%async_computation.1 | async-start | bytes 16384 | tf_op jit(solution)/shard_map/all_to_all | solution.py:102
  40.1 5.8 %gather_fusion.2 = bf16[1536,1024]{1,0:T(8,128)(2,1)} fusion(bf16[129,1024]{1,0:T(8,128)(2,1)S(1)} %concatenate.34, s32[2048]{0:T(1024)S(1)} %get-tuple-element.41), kind=kCustom, calls=%fused_computation.2 | custom fusion | bytes 6297600 | tf_op jit(solution)/shard_map/gather | solution.py:80
  51.3 5.8 %gather_fusion.1 = bf16[1536,1024]{1,0:T(8,128)(2,1)} fusion(bf16[129,1024]{1,0:T(8,128)(2,1)S(1)} %concatenate.33, s32[2048]{0:T(1024)S(1)} %get-tuple-element.41), kind=kCustom, calls=%fused_computation.1 | custom fusion | bytes 6297600 | tf_op jit(solution)/shard_map/gather | solution.py:83
  57.1 30.1 %all-to-all-done.4 = bf16[4,8,48,1024]{3,2,1,0:T(8,128)(2,1)S(1)} async-done(((bf16[4,8,48,1024]{3,2,1,0:T(8,128)(2,1)}), bf16[4,8,48,1024]{3,2,1,0:T(8,128)(2,1)S(1)}, u32[]{:S(2)}, u32[]{:S(2)}) %all-to-all-start.4) | async-done | bytes 3145760 | tf_op jit(solution)/shard_map/all_to_all | solution.py:89
  96.6 32.8 %all-to-all-done.2 = bf16[4,8,48,1024]{3,2,1,0:T(8,128)(2,1)S(1)} async-done(((bf16[4,8,48,1024]{3,2,1,0:T(8,128)(2,1)}), bf16[4,8,48,1024]{3,2,1,0:T(8,128)(2,1)S(1)}, u32[]{:S(2)}, u32[]{:S(2)}) %all-to-all-start.2) | async-done | bytes 3145760 | tf_op jit(solution)/shard_map/all_to_all | solution.py:96
  131.1 5.3 %all-to-all-start.5 = ((bf16[4,8,48,1024]{3,2,0,1:T(8,128)(2,1)}), bf16[4,8,48,1024]{3,2,0,1:T(8,128)(2,1)S(1)}, u32[]{:S(2)}, u32[]{:S(2)}) async-start(bf16[4,8,48,1024]{3,2,0,1:T(8,128)(2,1)} %copy.92), calls=%async_computation.5 | async-start | bytes 6291456 | tf_op jit(solution)/shard_map/all_to_all | solution.py:88
  143.1 63.7 %all-to-all-done.5 = bf16[4,8,48,1024]{3,2,0,1:T(8,128)(2,1)S(1)} async-done(((bf16[4,8,48,1024]{3,2,0,1:T(8,128)(2,1)}), bf16[4,8,48,1024]{3,2,0,1:T(8,128)(2,1)S(1)}, u32[]{:S(2)}, u32[]{:S(2)}) %all-to-all-start.5) | async-done | bytes 3145760 | tf_op jit(solution)/shard_map/all_to_all | solution.py:88
  206.8 4.5 all-to-all-start.3
  223.3 58.2 %all-to-all-done.3 = bf16[4,8,48,1024]{3,2,0,1:T(8,128)(2,1)} async-done(((bf16[4,8,48,1024]{3,2,0,1:T(8,128)(2,1)}), bf16[4,8,48,1024]{3,2,0,1:T(8,128)(2,1)}, u32[]{:S(2)}, u32[]{:S(2)}) %all-to-all-start.3) | async-done | bytes 3145760 | tf_op jit(solution)/shard_map/all_to_all | solution.py:95
  287.6 6.9 %multiply_convert_fusion.3 = (bf16[1536,512]{0,1:T(8,128)(2,1)}, bf16[1536,512]{0,1:T(8,128)(2,1)}, bf16[1536]{0:T(1024)(128)(2,1)S(1)}) fusion(f32[1536,1024]{0,1:T(8,128)S(1)} %fusion.17, f32[1536]{0:T(1024)S(1)} %reshape.147, bf16[1536,1024]{1,0:T(8,128)(2,1)S(1)} %bitcast.60, bf16[1,3,1024,512]{3,2,1,0:T(8,128)(2,1)} %param.10), kind=kOutput, calls=%fused_computation.17 | convolution fusion | flops 1623980544 | bytes 13640704 | tf_op jit(solution)/shard_map/dot_general | solution.py:24
  298.6 6.9 %convolution_convert_fusion = bf16[1536,1024]{1,0:T(8,128)(2,1)} fusion(bf16[1536,512]{0,1:T(8,128)(2,1)} %get-tuple-element.31, bf16[1536,512]{0,1:T(8,128)(2,1)} %get-tuple-element.30, bf16[1024,512]{1,0:T(8,128)(2,1)S(1)} %copy-done.17, bf16[1024,512]{1,0:T(8,128)(2,1)S(1)} %copy-done.15), kind=kOutput, calls=%fused_computation.8 | convolution fusion | flops 3233284096 | bytes 8388608 | tf_op jit(solution)/shard_map/dot_general | solution.py:32
  309.9 36.2 %all-to-all-done.6 = bf16[4,8,48,1024]{3,2,1,0:T(8,128)(2,1)S(1)} async-done(((bf16[4,8,48,1024]{3,2,1,0:T(8,128)(2,1)}), bf16[4,8,48,1024]{3,2,1,0:T(8,128)(2,1)S(1)}, u32[]{:S(2)}, u32[]{:S(2)}) %all-to-all-start.6) | async-done | bytes 3145760 | tf_op jit(solution)/shard_map/all_to_all | solution.py:126
  351.8 4.5 all-to-all-done.9
  356.3 4.4 all-to-all-start.7
  372.0 5.6 %fusion.10 = bf16[1,1,1024,512]{3,2,1,0:T(8,128)(2,1)S(1)} fusion(bf16[1536,1024]{1,0:T(8,128)(2,1)S(1)} %bitcast.61, f32[1536]{0:T(1024)S(1)} %reshape.147, f32[1536,1024]{0,1:T(8,128)} %copy-done.22), kind=kOutput, calls=%fused_computation.30 | convolution fusion | flops 1620574208 | bytes 10491904 | tf_op jit(solution)/shard_map/dot_general | solution.py:13
  379.6 8.0 %gather_fusion.4 = bf16[1280]{0:T(1024)(128)(2,1)S(1)} fusion(bf16[1536]{0:T(1024)(128)(2,1)S(1)} %reshape.145, s32[2048]{0:T(1024)S(1)} %pad_clamp_fusion), kind=kCustom, calls=%fused_computation.4 | custom fusion | bytes 10240 | tf_op jit(solution)/shard_map/gather | solution.py:142
  388.5 62.5 %all-to-all-done.7 = bf16[4,8,48,1024]{3,2,0,1:T(8,128)(2,1)} async-done(((bf16[4,8,48,1024]{3,2,0,1:T(8,128)(2,1)}), bf16[4,8,48,1024]{3,2,0,1:T(8,128)(2,1)}, u32[]{:S(2)}, u32[]{:S(2)}) %all-to-all-start.7) | async-done | bytes 3145760 | tf_op jit(solution)/shard_map/all_to_all | solution.py:125
  453.3 5.1 %gather_fusion.3 = bf16[1280,1024]{1,0:T(8,128)(2,1)} fusion(bf16[1536,1024]{1,0:T(8,128)(2,1)S(1)} %bitcast.53, s32[2048]{0:T(1024)S(1)} %pad_clamp_fusion), kind=kCustom, calls=%fused_computation.3 | custom fusion | bytes 5248000 | tf_op jit(solution)/shard_map/gather | solution.py:141
  458.4 6.3 %reshape.203 = f32[128,10,1024]{2,1,0:T(8,128)} reshape(bf16[1280,1024]{1,0:T(8,128)(2,1)} %gather_fusion.3) | data formatting | bytes 7864320 | tf_op jit(solution)/shard_map/convert_element_type | solution.py:141
  464.8 5.6 %reduce_sum.38 = f32[128,1024]{1,0:T(8,128)S(1)} reduce(f32[128,10,1024]{2,1,0:T(8,128)} %reshape.203, f32[]{:T(128)} %constant.17.clone.1), dimensions={1}, to_apply=%region_3.4 | reduce | flops 1179648 | bytes 5767172 | tf_op jit(solution)/shard_map/reduce_sum | solution.py:141
  471.9 24.6 %all-reduce.4.cloned.1.call-done = f32[3,256,512]{2,1,0:T(8,128)} async-done(((f32[3,256,512]{2,1,0:T(8,128)}), f32[3,256,512]{2,1,0:T(8,128)}) %all-reduce.4.cloned.1.call-update) | async-done | bytes 1572880 | tf_op jit(solution)/shard_map/psum | solution.py:161
  (111 shorter events, 80.4 us)
Async XLA Ops:
  7.2 32.9 %copy-start.7 = (bf16[128,1024]{1,0:T(8,128)(2,1)S(1)}, bf16[128,1024]{1,0:T(8,128)(2,1)}, u32[]{:S(2)}) copy-start(bf16[128,1024]{1,0:T(8,128)(2,1)} %param.6) | copy-start | bytes 786436
  34.3 12.3 %all-to-all-start.1 = ((bf16[4,8,48]{2,0,1:T(4,128)(2,1)}), bf16[4,8,48]{2,0,1:T(4,128)(2,1)S(1)}, u32[]{:S(2)}, u32[]{:S(2)}) async-start(bf16[4,8,48]{2,0,1:T(4,128)(2,1)} %copy.88), calls=%async_computation.1 | async-start | bytes 16384 | tf_op jit(solution)/shard_map/all_to_all | solution.py:102
  46.6 40.6 %all-to-all-start.4 = ((bf16[4,8,48,1024]{3,2,1,0:T(8,128)(2,1)}), bf16[4,8,48,1024]{3,2,1,0:T(8,128)(2,1)S(1)}, u32[]{:S(2)}, u32[]{:S(2)}) async-start(bf16[4,8,48,1024]{3,2,1,0:T(8,128)(2,1)} %bitcast.54), calls=%async_computation.4 | async-start | bytes 6291456 | tf_op jit(solution)/shard_map/all_to_all | solution.py:89
  88.9 40.6 %all-to-all-start.2 = ((bf16[4,8,48,1024]{3,2,1,0:T(8,128)(2,1)}), bf16[4,8,48,1024]{3,2,1,0:T(8,128)(2,1)S(1)}, u32[]{:S(2)}, u32[]{:S(2)}) async-start(bf16[4,8,48,1024]{3,2,1,0:T(8,128)(2,1)} %bitcast.55), calls=%async_computation.2 | async-start | bytes 6291456 | tf_op jit(solution)/shard_map/all_to_all | solution.py:96
  131.1 75.7 %all-to-all-start.5 = ((bf16[4,8,48,1024]{3,2,0,1:T(8,128)(2,1)}), bf16[4,8,48,1024]{3,2,0,1:T(8,128)(2,1)S(1)}, u32[]{:S(2)}, u32[]{:S(2)}) async-start(bf16[4,8,48,1024]{3,2,0,1:T(8,128)(2,1)} %copy.92), calls=%async_computation.5 | async-start | bytes 6291456 | tf_op jit(solution)/shard_map/all_to_all | solution.py:88
  136.4 4.5 copy-start.1
  206.8 74.6 %all-to-all-start.3 = ((bf16[4,8,48,1024]{3,2,0,1:T(8,128)(2,1)}), bf16[4,8,48,1024]{3,2,0,1:T(8,128)(2,1)}, u32[]{:S(2)}, u32[]{:S(2)}) async-start(bf16[4,8,48,1024]{3,2,0,1:T(8,128)(2,1)} %copy.90), calls=%async_computation.3 | async-start | bytes 6291456 | tf_op jit(solution)/shard_map/all_to_all | solution.py:95
  211.3 154.2 %reduce-scatter.2.cloned.1.call-start = ((), (), s32[]{:S(2)}) async-start(), calls=%async_computation.11 | async-start | bytes 7864320 | tf_op jit(solution)/shard_map/reduce_scatter | solution.py:148
  223.3 60.5 %copy-start.3 = (bf16[4,8,48,1024]{3,2,1,0:T(8,128)(2,1)S(1)}, bf16[4,8,48,1024]{3,2,1,0:T(8,128)(2,1)}, u32[]{:S(2)}) copy-start(bf16[4,8,48,1024]{3,2,1,0:T(8,128)(2,1)} %copy.93) | copy-start | bytes 9437188
  283.8 3.8 copy-start.5
  287.6 6.9 %copy-start.22 = (f32[1536,1024]{0,1:T(8,128)}, f32[1536,1024]{0,1:T(8,128)S(1)}, u32[]{:S(2)}) copy-start(f32[1536,1024]{0,1:T(8,128)S(1)} %fusion.17) | copy-start | bytes 18874372
  287.6 11.0 %copy-start.15 = (bf16[1024,512]{1,0:T(8,128)(2,1)S(1)}, bf16[1024,512]{1,0:T(8,128)(2,1)}, u32[]{:S(2)}) copy-start(bf16[1024,512]{1,0:T(8,128)(2,1)} %get-tuple-element.35) | copy-start | bytes 3145732
  287.6 11.0 %copy-start.17 = (bf16[1024,512]{1,0:T(8,128)(2,1)S(1)}, bf16[1024,512]{1,0:T(8,128)(2,1)}, u32[]{:S(2)}) copy-start(bf16[1024,512]{1,0:T(8,128)(2,1)} %get-tuple-element.36) | copy-start | bytes 3145732
  295.3 10.2 %all-to-all-start.8 = ((bf16[4,2,192]{2,1,0:T(2,128)(2,1)}), bf16[4,2,192]{2,1,0:T(2,128)(2,1)S(1)}, u32[]{:S(2)}, u32[]{:S(2)}) async-start(bf16[4,2,192]{2,1,0:T(2,128)(2,1)} %reshape.209), calls=%async_computation.8 | async-start | bytes 8192 | tf_op jit(solution)/shard_map/all_to_all | solution.py:133
  305.5 40.6 %all-to-all-start.6 = ((bf16[4,8,48,1024]{3,2,1,0:T(8,128)(2,1)}), bf16[4,8,48,1024]{3,2,1,0:T(8,128)(2,1)S(1)}, u32[]{:S(2)}, u32[]{:S(2)}) async-start(bf16[4,8,48,1024]{3,2,1,0:T(8,128)(2,1)} %bitcast.62), calls=%async_computation.6 | async-start | bytes 6291456 | tf_op jit(solution)/shard_map/all_to_all | solution.py:126
  346.1 10.1 %all-to-all-start.9 = ((bf16[4,8,48]{2,0,1:T(4,128)(2,1)}), bf16[4,8,48]{2,0,1:T(4,128)(2,1)S(1)}, u32[]{:S(2)}, u32[]{:S(2)}) async-start(bf16[4,8,48]{2,0,1:T(4,128)(2,1)} %copy.98), calls=%async_computation.9 | async-start | bytes 16384 | tf_op jit(solution)/shard_map/all_to_all | solution.py:132
  351.8 9.5 %copy-start.4 = (bf16[4,8,48,1024]{3,2,1,0:T(8,128)(2,1)S(1)}, bf16[4,8,48,1024]{3,2,1,0:T(8,128)(2,1)}, u32[]{:S(2)}) copy-start(bf16[4,8,48,1024]{3,2,1,0:T(8,128)(2,1)} %copy.93) | copy-start | bytes 9437188
  356.3 94.7 %all-to-all-start.7 = ((bf16[4,8,48,1024]{3,2,0,1:T(8,128)(2,1)}), bf16[4,8,48,1024]{3,2,0,1:T(8,128)(2,1)}, u32[]{:S(2)}, u32[]{:S(2)}) async-start(bf16[4,8,48,1024]{3,2,0,1:T(8,128)(2,1)} %copy.94), calls=%async_computation.7 | async-start | bytes 6291456 | tf_op jit(solution)/shard_map/all_to_all | solution.py:125
  360.7 135.7 %all-reduce.4.cloned.1.call-start = ((), (), s32[]{:S(2)}) async-start(), calls=%async_computation.12 | async-start | bytes 3145728 | tf_op jit(solution)/shard_map/psum | solution.py:161
  368.5 3.4 copy-start.6
  371.9 5.6 %copy-start.18 = (bf16[1,1,1024,512]{3,2,1,0:T(8,128)(2,1)S(1)}, bf16[1,1,1024,512]{3,2,1,0:T(8,128)(2,1)}, u32[]{:S(2)}) copy-start(bf16[1,1,1024,512]{3,2,1,0:T(8,128)(2,1)} %fusion.13) | copy-start | bytes 3145732
  464.8 5.6 %copy-start.11 = (bf16[1024,512]{1,0:T(8,128)(2,1)S(1)}, bf16[1024,512]{1,0:T(8,128)(2,1)}, u32[]{:S(2)}) copy-start(bf16[1024,512]{1,0:T(8,128)(2,1)} %copy-done.10) | copy-start | bytes 3145732
  464.8 5.6 %copy-start.13 = (bf16[1024,512]{1,0:T(8,128)(2,1)S(1)}, bf16[1024,512]{1,0:T(8,128)(2,1)}, u32[]{:S(2)}) copy-start(bf16[1024,512]{1,0:T(8,128)(2,1)} %copy-done.12) | copy-start | bytes 3145732
  464.8 5.6 %copy-start.21 = (bf16[128,512]{1,0:T(8,128)(2,1)S(1)}, bf16[128,512]{1,0:T(8,128)(2,1)}, u32[]{:S(2)}) copy-start(bf16[128,512]{1,0:T(8,128)(2,1)} %copy-done.20) | copy-start | bytes 393220
  (10 other events, 16.7 us)
Sparse Core Ops, SparseCore 0:
  218.3 58.2 reduce-scatter.1
  368.6 127.7 all-reduce.3
where the time goes:
time: 507 us; the launch traced here: 506 us
  waiting for transfers between devices  313 us (62%)
  local copies, waits for them, and re-layouts  82.2 us (16%)
  starting transfers between devices  38.4 us (8%)
  matrix products  36.7 us (7%)
  between operations  14.5 us (3%)
  other arithmetic  13.1 us (3%)
  blocking collectives  7.85 us (2%)
    all_to_all x1, waiting for transfers between devices, shards(): lax.all_to_all(lax.all_to_all(send_tokens, 'dp', split_axis=0, concat_axi...  63.7 us
    all_to_all x1, waiting for transfers between devices, shards(): lax.all_to_all(lax.all_to_all(outgoing_input, 'dp', split_axis=0, concat_...  62.5 us
    all_to_all x1, waiting for transfers between devices, shards(): lax.all_to_all(lax.all_to_all(send_cotangent, 'dp', split_axis=0, concat_...  58.2 us
    all_to_all x1, waiting for transfers between devices, shards(): lax.all_to_all(outgoing_input, 'dp', split_axis=0, concat_axis=0, tiled=T...  36.2 us
    all_to_all x1, waiting for transfers between devices, shards(): lax.all_to_all(send_cotangent, 'dp', split_axis=0, concat_axis=0, tiled=T...  32.8 us
    all_to_all x1, waiting for transfers between devices, shards(): lax.all_to_all(send_tokens, 'dp', split_axis=0, concat_axis=0, tiled=True)  30.1 us
    psum x1, waiting for transfers between devices, shards(): totals = lax.psum(kept, 'expert')  24.6 us
    dot_general x6, matrix products, contract_rows(): lax.dot_general(left, right, (((0,), (0,)), ((), ())), preferred_element_...  14.6 us
  transfers between devices with their start and end apart: 11, of which 9 were waited for; matrix products, arithmetic and copies ran while one was open for 21% of the time, Pallas kernels for 0%

commit v1 on v0

--- a/solution.py
+++ b/solution.py
@@ -1,6 +1,10 @@
+import functools
+
 import jax
 import jax.numpy as jnp
 from jax import lax
+from jax.experimental import pallas as pl
+from jax.experimental.pallas import tpu as pltpu
 from jax.sharding import PartitionSpec as P
 
 
@@ -48,13 +52,17 @@
     )
 
 
+def capacity_of(tok_rows, top_count, devices):
+    return max(2, (6 * tok_rows * top_count + 5 * devices - 1) // (5 * devices))
+
+
 def shards(tokens, cotangent, expert_ids, gate_weights, expert_weights, shared_weights):
     tok_rows, model_width = tokens.shape
     top_count = expert_ids.shape[1]
     data_count = lax.axis_size("dp")
     expert_count = lax.axis_size("expert")
     devices = data_count * expert_count
-    capacity = max(2, (6 * tok_rows * top_count + 5 * devices - 1) // (5 * devices))
+    capacity = capacity_of(tok_rows, top_count, devices)
     slot_total = devices * capacity
     pair_count = tok_rows * top_count
     row_ids = jnp.arange(tok_rows, dtype=jnp.int32)
@@ -163,6 +171,307 @@
     return (grad_tokens, grad_gates, grad_experts, grad_shared)
 
 
+def strict_upper(rows):
+    r = lax.broadcasted_iota(jnp.int32, (rows, rows), 0)
+    c = lax.broadcasted_iota(jnp.int32, (rows, rows), 1)
+    return (r < c).astype(jnp.bfloat16)
+
+
+def dot32(left, right, dims=((1,), (0,))):
+    return lax.dot_general(left, right, (dims, ((), ())), preferred_element_type=jnp.float32)
+
+
+def route_kernel(n, cap, gates, *refs):
+    pieces, (w_own, w_sib) = refs[:n], refs[n : n + 2]
+    parts, (gate_out, xs, sy, gg, gu, hb) = refs[n + 2 : 2 * n + 2], refs[2 * n + 2 : 2 * n + 8]
+    onehot, yslot, gslot, ig = refs[2 * n + 8 :]
+    rows = gates.shape[2]
+    named = jnp.where(gates[...] > 0, 1.0, 0.0)
+    before = dot32(named.reshape(2 * n, rows).astype(jnp.bfloat16), strict_upper(rows))
+    before = before.reshape(n, 2, rows)
+    slot = lax.broadcasted_iota(jnp.int32, (cap, rows), 0).astype(jnp.float32)
+    for p in range(n):
+        for j in range(2):
+            hit = (before[p, j][None, :] == slot) & (named[p, j][None, :] > 0)
+            hit = jnp.where(hit, 1.0, 0.0)
+            onehot[p, j * cap : (j + 1) * cap] = hit.astype(jnp.bfloat16)
+            gslot[j, p * cap : (p + 1) * cap] = jnp.sum(
+                hit * gates[p, j].astype(jnp.float32)[None, :], axis=1, keepdims=True
+            )
+        picked_x = dot32(onehot[p], pieces[p][0]).astype(jnp.bfloat16)
+        picked_y = dot32(onehot[p], pieces[p][1])
+        for j in range(2):
+            here = slice(p * cap, (p + 1) * cap)
+            there = slice(j * cap, (j + 1) * cap)
+            xs[j, here] = picked_x[there]
+            yslot[j, here] = picked_y[there].astype(jnp.bfloat16)
+            sy[j, here] = (picked_y[there] * gslot[j, here]).astype(jnp.bfloat16)
+    hidden_units = w_own.shape[2]
+    tile = min(256, hidden_units)
+    for j, w in enumerate((w_own, w_sib)):
+        gate_grad = jnp.zeros((n * cap, 1), jnp.float32)
+        for f in range(0, hidden_units, tile):
+            cols = slice(f, f + tile)
+            pre_gate = dot32(xs[j], w[0, :, cols])
+            pre_up = dot32(xs[j], w[1, :, cols])
+            back = dot32(yslot[j], w[2, :, cols])
+            activated, slope = silu_parts(pre_gate)
+            hidden = activated * pre_up
+            gate_grad += jnp.sum(hidden * back, axis=1, keepdims=True)
+            scaled = gslot[j] * back
+            gg[j, :, cols] = (scaled * pre_up * slope).astype(jnp.bfloat16)
+            gu[j, :, cols] = (scaled * activated).astype(jnp.bfloat16)
+            hb[j, :, cols] = hidden.astype(jnp.bfloat16)
+        ig[j] = (
+            dot32(gg[j], w[0], ((1,), (1,))) + dot32(gu[j], w[1], ((1,), (1,)))
+        ).astype(jnp.bfloat16)
+        for p in range(n):
+            hit = onehot[p, j * cap : (j + 1) * cap].astype(jnp.float32)
+            gate_out[p, j : j + 1] = jnp.sum(
+                hit * gate_grad[p * cap : (p + 1) * cap], axis=0, keepdims=True
+            )
+    for p in range(n):
+        both = jnp.concatenate([ig[j, p * cap : (p + 1) * cap] for j in range(2)], axis=0)
+        parts[p][...] = dot32(onehot[p], both, ((0,), (0,))).astype(parts[p].dtype)
+
+
+def route(cap, gates, pieces, w_own, w_sib):
+    n, rows, width = len(pieces), pieces[0].shape[1], pieces[0].shape[2]
+    hidden_units = w_own.shape[2]
+    slots = n * cap
+    shape = jax.ShapeDtypeStruct
+    bf = jnp.bfloat16
+    out_shape = [shape((rows, width), jnp.float32)] + [shape((rows, width), bf)] * (n - 1)
+    out_shape += [shape((n, 2, rows), jnp.float32)]
+    out_shape += [shape((2, slots, width), bf)] * 2 + [shape((2, slots, hidden_units), bf)] * 3
+    flops = 2 * 2 * slots * width * hidden_units * 5
+    outs = pl.pallas_call(
+        functools.partial(route_kernel, n, cap),
+        out_shape=out_shape,
+        scratch_shapes=[
+            pltpu.VMEM((n, 2 * cap, rows), bf),
+            pltpu.VMEM((2, slots, width), bf),
+            pltpu.VMEM((2, slots, 1), jnp.float32),
+            pltpu.VMEM((2, slots, width), bf),
+        ],
+        cost_estimate=pl.CostEstimate(
+            flops=flops, bytes_accessed=4 * w_own.size + 2 * slots * width * 8, transcendentals=0
+        ),
+        name="route",
+    )(gates, *pieces, w_own, w_sib)
+    return outs[:n], outs[n], outs[n + 1 :]
+
+
+def common_kernel(n, first, last, where_ref, *refs):
+    pieces, w, refs = refs[:n], refs[n], refs[n + 1 :]
+    if not first:
+        total_in, refs = refs[0], refs[1:]
+    if first:
+        own_grad, refs = refs[0], refs[1:]
+    if last:
+        (mine, other), refs = refs[:2], refs[2:]
+    else:
+        total, refs = refs[0], refs[1:]
+    x, y, gg, gu, hb = refs
+    rows = pieces[0].shape[1]
+    for p in range(n):
+        x[p * rows : (p + 1) * rows] = pieces[p][0]
+        y[p * rows : (p + 1) * rows] = pieces[p][1]
+    hidden_units = w.shape[2]
+    tile = min(256, hidden_units)
+    for f in range(0, hidden_units, tile):
+        cols = slice(f, f + tile)
+        pre_gate = dot32(x[...], w[0, :, cols])
+        pre_up = dot32(x[...], w[1, :, cols])
+        back = dot32(y[...], w[2, :, cols])
+        activated, slope = silu_parts(pre_gate)
+        gg[:, cols] = (back * pre_up * slope).astype(jnp.bfloat16)
+        gu[:, cols] = (back * activated).astype(jnp.bfloat16)
+        hb[:, cols] = (activated * pre_up).astype(jnp.bfloat16)
+    if first:
+        own_grad[...] = dot32(gg[:rows], w[0], ((1,), (1,))) + dot32(gu[:rows], w[1], ((1,), (1,)))
+    kept = total_in.shape[1] if not first else total.shape[1]
+    keep = pl.ds(pl.multiple_of(where_ref[0] * kept, kept), kept)
+    xk, yk = x[:, keep], y[:, keep]
+    for i, (left, right) in enumerate(((xk, gg), (xk, gu), (yk, hb))):
+        term = dot32(left, right[...], ((0,), (0,)))
+        if not first:
+            term = term + total_in[i]
+        if last:
+            half = kept // 2
+
+            @pl.when(where_ref[1] == 0)
+            def _():
+                mine[i] = term[:half]
+                other[i] = term[half:]
+
+            @pl.when(where_ref[1] == 1)
+            def _():
+                mine[i] = term[half:]
+                other[i] = term[:half]
+        else:
+            total[i] = term
+
+
+def common(where_at, kept, pieces, w, total, last):
+    first = total is None
+    n, rows, width = len(pieces), pieces[0].shape[1], pieces[0].shape[2]
+    hidden_units = w.shape[2]
+    shape = jax.ShapeDtypeStruct
+    out_shape = [shape((rows, width), jnp.float32)] if first else []
+    if last:
+        out_shape += [shape((3, kept // 2, hidden_units), jnp.float32)] * 2
+    else:
+        out_shape += [shape((3, kept, hidden_units), jnp.float32)]
+    args = list(pieces) + [w] + ([] if first else [total])
+    flops = 2 * n * rows * hidden_units * 3 * (width + kept)
+    return pl.pallas_call(
+        functools.partial(common_kernel, n, first, last),
+        out_shape=out_shape,
+        in_specs=[pl.BlockSpec(memory_space=pltpu.SMEM)]
+        + [pl.BlockSpec(memory_space=pltpu.VMEM)] * len(args),
+        scratch_shapes=[pltpu.VMEM((n * rows, width), jnp.bfloat16)] * 2
+        + [pltpu.VMEM((n * rows, hidden_units), jnp.bfloat16)] * 3,
+        cost_estimate=pl.CostEstimate(
+            flops=flops, bytes_accessed=2 * w.size + n * rows * width * 4, transcendentals=0
+        ),
+        name="common",
+    )(where_at, *args)
+
+
+def weights_kernel(groups, j, received, *refs):
+    saved, refs = refs[: 5 * groups], refs[5 * groups :]
+    came, out = (refs[0], refs[1]) if received else (None, refs[0])
+    for i, (left, right) in enumerate(((0, 2), (0, 3), (1, 4))):
+        total = None
+        for g in range(groups):
+            term = dot32(saved[5 * g + left][j], saved[5 * g + right][j], ((0,), (0,)))
+            total = term if total is None else total + term
+        if received:
+            total = total + came[i].astype(jnp.float32)
+        out[i] = total.astype(jnp.bfloat16)
+
+
+def weights(saved, j, came):
+    groups = len(saved)
+    flat = [a for group in saved for a in group]
+    width, hidden_units = flat[0].shape[2], flat[2].shape[2]
+    slots = sum(group[0].shape[1] for group in saved)
+    args = flat + ([came] if came is not None else [])
+    return pl.pallas_call(
+        functools.partial(weights_kernel, groups, j, came is not None),
+        out_shape=jax.ShapeDtypeStruct((3, width, hidden_units), jnp.bfloat16),
+        in_specs=[pl.BlockSpec((1,) + a.shape[1:], lambda j=j: (j, 0, 0)) for a in flat]
+        if False
+        else [pl.BlockSpec(memory_space=pltpu.VMEM)] * len(args),
+        cost_estimate=pl.CostEstimate(
+            flops=6 * slots * width * hidden_units,
+            bytes_accessed=slots * (4 * width + 6 * hidden_units),
+            transcendentals=0,
+        ),
+        name="weights",
+    )(*args)
+
+
+def shared_rows(tokens, cotangent, expert_ids, gate_weights, expert_weights, shared_weights):
+    rows, width = tokens.shape
+    top_count = expert_ids.shape[1]
+    data_count, expert_count = lax.axis_size("dp"), lax.axis_size("expert")
+    devices = data_count * expert_count
+    cap = capacity_of(rows, top_count, devices)
+    planes = expert_count // 2
+    bf, f32 = jnp.bfloat16, jnp.float32
+    me_dp, me_ex = lax.axis_index("dp"), lax.axis_index("expert")
+    across_x = [(e, e ^ 1) for e in range(expert_count)]
+    around_z = [(e, (e + 2) % expert_count) for e in range(expert_count)]
+    across_y = [(d, d ^ 2) for d in range(data_count)]
+    across_core = [(d, d ^ 1) for d in range(data_count)]
+    px = lambda a: lax.ppermute(a, "expert", across_x)
+    pz = lambda a: lax.ppermute(a, "expert", around_z)
+    py = lambda a: lax.ppermute(a, "dp", across_y)
+    pc = lambda a: lax.ppermute(a, "dp", across_core)
+
+    w_own = expert_weights[0]
+    own = jnp.stack([tokens, cotangent])
+    w_sib = pc(w_own)
+
+    matches = expert_ids[:, :, None] == jnp.arange(devices, dtype=jnp.int32)
+    by_expert = jnp.sum(jnp.where(matches, gate_weights[:, :, None].astype(f32), 0.0), axis=1)
+    by_expert = by_expert.T.astype(bf).reshape(data_count // 2, 2, expert_count, rows)
+    outward = jnp.stack([by_expert, by_expert[:, ::-1]], axis=3).reshape(devices, 2, rows)
+    inward = lax.all_to_all(outward, ("dp", "expert"), 0, 0, tiled=True)
+    order = []
+    for s in range(planes):
+        plane = (me_ex // 2 + planes - s) % planes
+        for dy, dx in ((0, 0), (0, 1), (1, 0), (1, 1)):
+            source = (me_dp ^ (2 * dy)) * expert_count + plane * 2 + (me_ex % 2 ^ dx)
+            order.append(source)
+    pick = jnp.stack(order)[:, None] == jnp.arange(devices, dtype=jnp.int32)[None, :]
+    pick = pick.astype(bf)
+    gates = jnp.dot(pick, inward.reshape(devices, 2 * rows), preferred_element_type=f32)
+    gates = gates.reshape(planes, 4, 2, rows)
+
+    col, xs, ys, ds = [own], [], [], []
+    for s in range(planes):
+        if s:
+            col.append(pz(col[s - 1]))
+        xs.append(px(col[s]))
+        ys.append(py(col[s]))
+        if s < max(1, planes // 2):
+            ds.append(jnp.stack([px(ys[s][0]), py(xs[s][1])]))
+        else:
+            ds.append(pz(ds[s - 1]))
+
+    where_at = jnp.stack([me_dp // 2, me_dp % 2]).astype(jnp.int32)
+    kept = 2 * (width // data_count)
+    total, shared_grad, saved, gate_grads = None, None, [], []
+    carry, carry_d, final = None, None, None
+    half = width // 2
+    for s in range(planes):
+        pieces = (col[s], xs[s], ys[s], ds[s])
+        (c, x, y, d), gate_grad, keep = route(cap, gates[s], pieces, w_own, w_sib)
+        saved.append(keep)
+        gate_grads.append(gate_grad)
+        outs = common(where_at, kept, pieces, shared_weights, total, s == planes - 1)
+        if s == 0:
+            shared_grad, total = outs
+        elif s < planes - 1:
+            total = outs[0]
+        else:
+            mine, other = outs
+        if carry_d is not None:
+            d = (d.astype(f32) + carry_d.astype(f32)).astype(bf)
+        if 0 < s < planes - 1:
+            carry_d = pz(d)
+        else:
+            from_x, from_y = px(d[:, :half]), py(d[:, half:])
+            y = jnp.concatenate([(y[:, :half].astype(f32) + from_x.astype(f32)).astype(bf), y[:, half:]], axis=1)
+            x = jnp.concatenate([x[:, :half], (x[:, half:].astype(f32) + from_y.astype(f32)).astype(bf)], axis=1)
+        c = c + px(x).astype(f32) + py(y).astype(f32)
+        if s == 0:
+            final = c
+        else:
+            if carry is not None:
+                c = c + carry.astype(f32)
+            carry = pz(c.astype(bf))
+    if carry is not None:
+        final = final + carry.astype(f32)
+    grad_tokens = (final + shared_grad).astype(bf)
+
+    grad_shared = mine + pc(other)
+    came = pc(weights(saved, 1, None))
+    grad_experts = weights(saved, 0, came)[None]
+
+    back = jnp.stack(gate_grads).reshape(4 * planes, 2 * rows).astype(bf)
+    back = lax.dot_general(pick, back, (((0,), (0,)), ((), ())), preferred_element_type=f32)
+    back = lax.all_to_all(back.astype(bf).reshape(devices, 2, rows), ("dp", "expert"), 0, 0, tiled=True)
+    back = back.astype(f32).reshape(data_count // 2, 2, expert_count, 2, rows)
+    by_expert = back[:, :, :, 0] + back[:, ::-1, :, 1]
+    by_expert = by_expert.reshape(devices, rows).T
+    grad_gates = jnp.sum(jnp.where(matches, by_expert[:, None, :], 0.0), axis=2).astype(bf)
+    return (grad_tokens, grad_gates, grad_experts, grad_shared)
+
+
 def solution(mesh):
     placed = (
         P(("dp", "expert"), None),
@@ -172,8 +481,19 @@
         P(("dp", "expert"), None, None, None),
         P(),
     )
+    data_count, expert_count = mesh.shape["dp"], mesh.shape["expert"]
+
+    def body(tokens, cotangent, expert_ids, gate_weights, expert_weights, shared_weights):
+        rows = tokens.shape[0] * data_count * expert_count
+        slots = data_count * expert_count * capacity_of(
+            tokens.shape[0], expert_ids.shape[1], data_count * expert_count
+        )
+        share = data_count == 4 and expert_count % 4 == 0 and rows <= 4 * slots
+        plan = shared_rows if share else shards
+        return plan(tokens, cotangent, expert_ids, gate_weights, expert_weights, shared_weights)
+
     return jax.shard_map(
-        shards,
+        body,
         mesh=mesh,
         in_specs=placed,
         out_specs=(

time: 507 us -> 231 us (0.46)
  waiting for transfers between devices: 313 us -> 69.2 us
  Pallas kernels: 0 us -> 85.4 us
  local copies, waits for them, and re-layouts: 82.2 us -> 14.1 us
  matrix products: 36.7 us -> 0.45 us
  between operations: 14.5 us -> 1.08 us
  blocking collectives: 7.85 us -> 0 us
  other arithmetic: 13.1 us -> 20.8 us
    all_to_all x9 -> x2, waiting for transfers between devices: 289 us -> 0.01 us  [the longest x1 0.01 us: shared_rows(): inward = lax.all_to_all(outward, ('dp', 'expert'), 0, 0, tiled=True)]
    pallas_call x0 -> x10, Pallas kernels: none -> 85.4 us  [the longest x4 33.5 us: route(): pl.pallas_call(functools.partial(route_kernel, n, cap), out_shape=out_sha...]
    ppermute x0 -> x37, waiting for transfers between devices: none -> 69.2 us  [the longest x10 43.7 us: shared_rows(): pz = lambda a: lax.ppermute(a, 'expert', around_z)]
    dot_general x13 -> x2, matrix products: 36.7 us -> 0.45 us  [the longest x1 0.26 us: shared_rows(): lax.dot_general(pick, back, (((0,), (0,)), ((), ())), preferred_element_t...]
    gather x6 -> x0, local copies, waits for them, and re-layouts: 34.3 us -> none  [the longest x1 9.46 us: shards(): padded_gates[slot_table].reshape(data_count, expert_count, capacity)]
    ppermute x0 -> x37, starting transfers between devices: none -> 30.8 us  [the longest x12 12.7 us: shared_rows(): py = lambda a: lax.ppermute(a, 'dp', across_y)]
    all_to_all x9 -> x2, starting transfers between devices: 38 us -> 8.36 us  [the longest x1 4.37 us: shared_rows(): lax.all_to_all(back.astype(bf).reshape(devices, 2, rows), ('dp', 'expert'...]
    psum x1 -> x0, waiting for transfers between devices: 24.6 us -> none  [shards(): totals = lax.psum(kept, 'expert')]
  transfers between devices with their start and end apart: 11 -> 39, of which waited for: 9 -> 16; matrix products, arithmetic and copies ran while one was open for 21% -> 13% of each run, Pallas kernels for 0% -> 33%
where the time goes in v1:
time: 231 us; the launch traced here: 230 us
  Pallas kernels  85.4 us (37%)
  waiting for transfers between devices  69.2 us (30%)
  starting transfers between devices  39.2 us (17%)
  other arithmetic  20.8 us (9%)
  local copies, waits for them, and re-layouts  14.1 us (6%)
    ppermute x10, waiting for transfers between devices, shared_rows(): pz = lambda a: lax.ppermute(a, 'expert', around_z)  43.7 us
    pallas_call x4, Pallas kernels, route(): pl.pallas_call(functools.partial(route_kernel, n, cap), out_shape=out_sha...  33.5 us
    pallas_call x4, Pallas kernels, common(): pl.pallas_call(functools.partial(common_kernel, n, first, last), out_shap...  32.2 us
    pallas_call x2, Pallas kernels, weights(): pl.pallas_call(functools.partial(weights_kernel, groups, j, came is not N...  19.7 us
    ppermute x12, waiting for transfers between devices, shared_rows(): px = lambda a: lax.ppermute(a, 'expert', across_x)  14.3 us
    ppermute x12, starting transfers between devices, shared_rows(): py = lambda a: lax.ppermute(a, 'dp', across_y)  12.7 us
    ppermute x12, starting transfers between devices, shared_rows(): px = lambda a: lax.ppermute(a, 'expert', across_x)  12.3 us
    ppermute x12, waiting for transfers between devices, shared_rows(): py = lambda a: lax.ppermute(a, 'dp', across_y)  11.3 us
  transfers between devices with their start and end apart: 39, of which 16 were waited for; matrix products, arithmetic and copies ran while one was open for 13% of the time, Pallas kernels for 33%

profile of v1, /device:TPU:0, one launch (start us, length us, event | category | flops | bytes accessed | tf_op | source)
XLA Modules:
  0.0 230.2 jit_solution(14071588833332243670)
XLA Ops:
  2.5 3.1 %collective-permute-start.9 = (bf16[2,128,1024]{2,1,0:T(8,128)(2,1)}, bf16[2,128,1024]{2,1,0:T(8,128)(2,1)}, u32[]{:S(2)}, u32[]{:S(2)}) collective-permute-start(bf16[2,128,1024]{2,1,0:T(8,128)(2,1)} %pad_maximum_fusion.refs_0_), channel_id=1, source_target_pairs={{0,2},{1,3},{2,4},{3,5},{4,6},{5,7},{6,0},{7,1},{8,10},{9,11},{10,... | collective-permute-start | bytes 1572872 | tf_op jit(solution)/shard_map/ppermute | solution.py:390
  5.6 14.3 %collective-permute-done.9.refs_0_ = bf16[2,128,1024]{2,1,0:T(8,128)(2,1)} collective-permute-done((bf16[2,128,1024]{2,1,0:T(8,128)(2,1)}, bf16[2,128,1024]{2,1,0:T(8,128)(2,1)}, u32[]{:S(2)}, u32[]{:S(2)}) %collective-permute-start.9) | collective-permute-done | bytes 524320 | tf_op jit(solution)/shard_map/ppermute | solution.py:390
  25.9 4.0 %all-to-all-start = ((bf16[32,2,128]{2,1,0:T(2,128)(2,1)}), bf16[32,2,128]{2,1,0:T(2,128)(2,1)S(1)}, u32[]{:S(2)}, u32[]{:S(2)}) async-start(bf16[32,2,128]{2,1,0:T(2,128)(2,1)} %copy.24), calls=%async_computation | async-start | bytes 32768 | tf_op jit(solution)/shard_map/all_to_all | solution.py:402
  30.6 4.4 %collective-permute-done.16.refs_1_ = bf16[2,128,1024]{2,1,0:T(8,128)(2,1)} collective-permute-done((bf16[2,128,1024]{2,1,0:T(8,128)(2,1)}, bf16[2,128,1024]{2,1,0:T(8,128)(2,1)}, u32[]{:S(2)}, u32[]{:S(2)}) %collective-permute-start.16) | collective-permute-done | bytes 524320 | tf_op jit(solution)/shard_map/ppermute | solution.py:389
  36.0 9.6 %collective-permute-done.14.refs_2_ = bf16[2,128,1024]{2,1,0:T(8,128)(2,1)} collective-permute-done((bf16[2,128,1024]{2,1,0:T(8,128)(2,1)}, bf16[2,128,1024]{2,1,0:T(8,128)(2,1)}, u32[]{:S(2)}, u32[]{:S(2)}) %collective-permute-start.14) | collective-permute-done | bytes 524320 | tf_op jit(solution)/shard_map/ppermute | solution.py:391
  54.6 2.2 collective-permute-done.15
  65.4 7.8 %collective-permute-done.11.refs_0_ = bf16[2,128,1024]{2,1,0:T(8,128)(2,1)} collective-permute-done((bf16[2,128,1024]{2,1,0:T(8,128)(2,1)}, bf16[2,128,1024]{2,1,0:T(8,128)(2,1)}, u32[]{:S(2)}, u32[]{:S(2)}) %collective-permute-start.11) | collective-permute-done | bytes 524320 | tf_op jit(solution)/shard_map/ppermute | solution.py:390
  74.8 5.3 %collective-permute-done.18.refs_3_ = bf16[2,128,1024]{2,1,0:T(8,128)(2,1)} collective-permute-done((bf16[2,128,1024]{2,1,0:T(8,128)(2,1)}, bf16[2,128,1024]{2,1,0:T(8,128)(2,1)}, u32[]{:S(2)}, u32[]{:S(2)}) %collective-permute-start.18) | collective-permute-done | bytes 524320 | tf_op jit(solution)/shard_map/ppermute | solution.py:390
  80.1 7.6 %common.4 = (f32[128,1024]{1,0:T(8,128)}, f32[3,512,512]{2,1,0:T(8,128)}) custom-call(s32[2]{0:T(128)} %pad_add_fusion.where_ref, bf16[2,128,1024]{2,1,0:T(8,128)(2,1)} %pad_maximum_fusion.refs_0_, bf16[2,128,1024]{2,1,0:T(8,128)(2,1)} %collective-permute-done.refs_1_, bf16[2,128,1024]{2,1,0:T(8,128)(2,1)} %collective-permute-done.1.refs_2_, ...), custom_call_target="tpu_custom_call" | custom-call | flops 2415919104 | bytes 5242880 | tf_op jit(solution)/shard_map/common/pallas_call | solution.py:328
  87.8 7.9 %common.5.refs_5_ = f32[3,512,512]{2,1,0:T(8,128)} custom-call(s32[2]{0:T(128)} %pad_add_fusion.where_ref, bf16[2,128,1024]{2,1,0:T(8,128)(2,1)} %collective-permute-done.9.refs_0_, bf16[2,128,1024]{2,1,0:T(8,128)(2,1)} %collective-permute-done.16.refs_1_, bf16[2,128,1024]{2,1,0:T(8,128)(2,1)} %collective-permute-done.14.refs_2_, ...), custom_call_target="tpu_custom_call" | custom-call | flops 2415919104 | bytes 5242880 | tf_op jit(solution)/shard_map/common/pallas_call | solution.py:328
  95.7 7.9 %common.6.refs_5_ = f32[3,512,512]{2,1,0:T(8,128)} custom-call(s32[2]{0:T(128)} %pad_add_fusion.where_ref, bf16[2,128,1024]{2,1,0:T(8,128)(2,1)} %collective-permute-done.10.refs_0_, bf16[2,128,1024]{2,1,0:T(8,128)(2,1)} %collective-permute-done.20.refs_1_, bf16[2,128,1024]{2,1,0:T(8,128)(2,1)} %collective-permute-done.21.refs_2_, ...), custom_call_target="tpu_custom_call" | custom-call | flops 2415919104 | bytes 5242880 | tf_op jit(solution)/shard_map/common/pallas_call | solution.py:328
  103.6 8.7 %common.7 = (f32[3,256,512]{2,1,0:T(8,128)}, f32[3,256,512]{2,1,0:T(8,128)}) custom-call(s32[2]{0:T(128)} %pad_add_fusion.where_ref, bf16[2,128,1024]{2,1,0:T(8,128)(2,1)} %collective-permute-done.11.refs_0_, bf16[2,128,1024]{2,1,0:T(8,128)(2,1)} %collective-permute-done.12.refs_1_, bf16[2,128,1024]{2,1,0:T(8,128)(2,1)} %collective-permute-done.13.refs_2_, ...), custom_call_target="tpu_custom_call" | custom-call | flops 2415919104 | bytes 5242880 | tf_op jit(solution)/shard_map/common/pallas_call | solution.py:328
  114.0 8.3 %route.4 = (f32[128,1024]{1,0:T(8,128)}, bf16[128,1024]{1,0:T(8,128)(2,1)}, bf16[128,1024]{1,0:T(8,128)(2,1)}, bf16[128,1024]{1,0:T(8,128)(2,1)}, f32[4,2,128]{2...) custom-call(f32[4,2,128]{2,1,0:T(2,128)} %squeeze.29.gates, ...), custom_call_target="tpu_custom_call" | custom-call | flops 2013265920 | bytes 9437184 | tf_op jit(solution)/shard_map/route/pallas_call | solution.py:248
  125.5 8.3 %route.5 = (f32[128,1024]{1,0:T(8,128)}, bf16[128,1024]{1,0:T(8,128)(2,1)}, bf16[128,1024]{1,0:T(8,128)(2,1)}, bf16[128,1024]{1,0:T(8,128)(2,1)}, f32[4,2,128]{2...) custom-call(f32[4,2,128]{2,1,0:T(2,128)} %squeeze.33.gates, ...), custom_call_target="tpu_custom_call" | custom-call | flops 2013265920 | bytes 9437184 | tf_op jit(solution)/shard_map/route/pallas_call | solution.py:248
  134.5 8.5 %route.6 = (f32[128,1024]{1,0:T(8,128)}, bf16[128,1024]{1,0:T(8,128)(2,1)}, bf16[128,1024]{1,0:T(8,128)(2,1)}, bf16[128,1024]{1,0:T(8,128)(2,1)}, f32[4,2,128]{2...) custom-call(f32[4,2,128]{2,1,0:T(2,128)} %squeeze.36.gates, ...), custom_call_target="tpu_custom_call" | custom-call | flops 2013265920 | bytes 9437184 | tf_op jit(solution)/shard_map/route/pallas_call | solution.py:248
  143.6 8.3 %route.7 = (f32[128,1024]{1,0:T(8,128)}, bf16[128,1024]{1,0:T(8,128)(2,1)}, bf16[128,1024]{1,0:T(8,128)(2,1)}, bf16[128,1024]{1,0:T(8,128)(2,1)}, f32[4,2,128]{2...) custom-call(f32[4,2,128]{2,1,0:T(2,128)} %squeeze.37.gates, ...), custom_call_target="tpu_custom_call" | custom-call | flops 2013265920 | bytes 9437184 | tf_op jit(solution)/shard_map/route/pallas_call | solution.py:248
  154.7 4.4 %all-to-all-start.1 = ((bf16[32,2,128]{2,1,0:T(2,128)(2,1)}), bf16[32,2,128]{2,1,0:T(2,128)(2,1)S(1)}, u32[]{:S(2)}, u32[]{:S(2)}) async-start(bf16[32,2,128]{2,1,0:T(2,128)(2,1)} %reshape.50), calls=%async_computation.1 | async-start | bytes 32768 | tf_op jit(solution)/shard_map/all_to_all | solution.py:467
  159.1 9.4 %weights.2 = bf16[3,1024,512]{2,1,0:T(8,128)(2,1)} custom-call(bf16[2,192,1024]{2,1,0:T(8,128)(2,1)} %get-tuple-element.69.refs_0_, bf16[2,192,1024]{2,1,0:T(8,128)(2,1)} %get-tuple-element.70.refs_1_, bf16[2,192,512]{2,1,0:T(8,128)(2,1)} %get-tuple-element.71.refs_2_, bf16[2,192,512]{2,1,0:T(8,128)(2,1)} %get-tuple-element.72.refs_3_, ...), custom_call_target="tpu_custom_call" | custom-call | flops 2415919104 | bytes 5505024 | tf_op jit(solution)/shard_map/weights/pallas_call | solution.py:361
  188.8 5.2 %collective-permute-done.32 = bf16[128,1024]{1,0:T(8,128)(2,1)S(1)} collective-permute-done((bf16[128,1024]{1,0:T(8,128)(2,1)S(1)}, bf16[128,1024]{1,0:T(8,128)(2,1)S(1)}, u32[]{:S(2)}, u32[]{:S(2)}) %collective-permute-start.32) | collective-permute-done | bytes 262176 | tf_op jit(solution)/shard_map/ppermute | solution.py:390
  195.9 3.1 %collective-permute-done.26 = bf16[128,512]{1,0:T(8,128)(2,1)S(1)} collective-permute-done((bf16[128,512]{1,0:T(8,128)(2,1)S(1)}, bf16[128,512]{1,0:T(8,128)(2,1)S(1)}, u32[]{:S(2)}, u32[]{:S(2)}) %collective-permute-start.26) | collective-permute-done | bytes 131104 | tf_op jit(solution)/shard_map/ppermute | solution.py:389
  201.2 5.9 %collective-permute-done.33 = bf16[128,1024]{1,0:T(8,128)(2,1)S(1)} collective-permute-done((bf16[128,1024]{1,0:T(8,128)(2,1)S(1)}, bf16[128,1024]{1,0:T(8,128)(2,1)S(1)}, u32[]{:S(2)}, u32[]{:S(2)}) %collective-permute-start.33) | collective-permute-done | bytes 262176 | tf_op jit(solution)/shard_map/ppermute | solution.py:390
  209.0 2.9 %add.246 = f32[3,256,512]{2,1,0:T(8,128)} add(f32[3,256,512]{2,1,0:T(8,128)S(1)} %copy-done.2, f32[3,256,512]{2,1,0:T(8,128)} %collective-permute-done.36) | non-fusion elementwise | flops 393216 | bytes 4718592 | tf_op jit(solution)/shard_map/add | solution.py:461
  214.1 3.3 %collective-permute-done.34 = bf16[128,1024]{1,0:T(8,128)(2,1)S(1)} collective-permute-done((bf16[128,1024]{1,0:T(8,128)(2,1)S(1)}, bf16[128,1024]{1,0:T(8,128)(2,1)S(1)}, u32[]{:S(2)}, u32[]{:S(2)}) %collective-permute-start.34) | collective-permute-done | bytes 262176 | tf_op jit(solution)/shard_map/ppermute | solution.py:390
  219.9 10.3 %weights.3 = bf16[3,1024,512]{2,1,0:T(8,128)(2,1)} custom-call(bf16[2,192,1024]{2,1,0:T(8,128)(2,1)} %get-tuple-element.69.refs_0_, bf16[2,192,1024]{2,1,0:T(8,128)(2,1)} %get-tuple-element.70.refs_1_, bf16[2,192,512]{2,1,0:T(8,128)(2,1)} %get-tuple-element.71.refs_2_, bf16[2,192,512]{2,1,0:T(8,128)(2,1)} %get-tuple-element.72.refs_3_, ...), custom_call_target="tpu_custom_call" | custom-call | flops 2415919104 | bytes 5505024 | tf_op jit(solution)/shard_map/weights/pallas_call | solution.py:361
  (146 shorter events, 68.4 us)
Async XLA Ops:
  2.5 17.3 %collective-permute-start.9 = (bf16[2,128,1024]{2,1,0:T(8,128)(2,1)}, bf16[2,128,1024]{2,1,0:T(8,128)(2,1)}, u32[]{:S(2)}, u32[]{:S(2)}) collective-permute-start(bf16[2,128,1024]{2,1,0:T(8,128)(2,1)} %pad_maximum_fusion.refs_0_), channel_id=1, source_target_pairs={{0,2},{1,3},{2,4},{3,5},{4,6},{5,7},{6,0},{7,1},{8,10},{9,11},{10,... | collective-permute-start | bytes 1572872 | tf_op jit(solution)/shard_map/ppermute | solution.py:390
  5.6 106.8 %collective-permute-start.4 = (bf16[3,1024,512]{2,1,0:T(8,128)(2,1)}, bf16[3,1024,512]{2,1,0:T(8,128)(2,1)S(1)}, u32[]{:S(2)}, u32[]{:S(2)}) collective-permute-start(bf16[3,1024,512]{2,1,0:T(8,128)(2,1)} %bitcast.62), channel_id=1, source_target_pairs={{0,8},{8,0},{16,24},{24,16},{1,9},{9,1},{17,25},{25,17},{2,10},{10... | collective-permute-start | bytes 9437192 | tf_op jit(solution)/shard_map/ppermute | solution.py:392
  19.8 15.2 %collective-permute-start.16 = (bf16[2,128,1024]{2,1,0:T(8,128)(2,1)}, bf16[2,128,1024]{2,1,0:T(8,128)(2,1)}, u32[]{:S(2)}, u32[]{:S(2)}) collective-permute-start(bf16[2,128,1024]{2,1,0:T(8,128)(2,1)} %collective-permute-done.9.refs_0_), channel_id=1, source_target_pairs={{0,1},{1,0},{2,3},{3,2},{4,5},{5,4},{6,7},{7,6},{8,9},{9,8},{10,11... | collective-permute-start | bytes 1572872 | tf_op jit(solution)/shard_map/ppermute | solution.py:389
  21.3 26.8 %collective-permute-start.1 = (bf16[2,128,1024]{2,1,0:T(8,128)(2,1)}, bf16[2,128,1024]{2,1,0:T(8,128)(2,1)}, u32[]{:S(2)}, u32[]{:S(2)}) collective-permute-start(bf16[2,128,1024]{2,1,0:T(8,128)(2,1)} %pad_maximum_fusion.refs_0_), channel_id=1, source_target_pairs={{0,16},{8,24},{16,0},{24,8},{1,17},{9,25},{17,1},{25,9},{2,18},{10... | collective-permute-start | bytes 1572872 | tf_op jit(solution)/shard_map/ppermute | solution.py:391
  22.8 26.9 %collective-permute-start = (bf16[2,128,1024]{2,1,0:T(8,128)(2,1)}, bf16[2,128,1024]{2,1,0:T(8,128)(2,1)}, u32[]{:S(2)}, u32[]{:S(2)}) collective-permute-start(bf16[2,128,1024]{2,1,0:T(8,128)(2,1)} %pad_maximum_fusion.refs_0_), channel_id=1, source_target_pairs={{0,1},{1,0},{2,3},{3,2},{4,5},{5,4},{6,7},{7,6},{8,9},{9,8},{10,11... | collective-permute-start | bytes 1572872 | tf_op jit(solution)/shard_map/ppermute | solution.py:389
  24.1 21.6 %collective-permute-start.14 = (bf16[2,128,1024]{2,1,0:T(8,128)(2,1)}, bf16[2,128,1024]{2,1,0:T(8,128)(2,1)}, u32[]{:S(2)}, u32[]{:S(2)}) collective-permute-start(bf16[2,128,1024]{2,1,0:T(8,128)(2,1)} %collective-permute-done.9.refs_0_), channel_id=1, source_target_pairs={{0,16},{8,24},{16,0},{24,8},{1,17},{9,25},{17,1},{25,9},{2,18},{10... | collective-permute-start | bytes 1572872 | tf_op jit(solution)/shard_map/ppermute | solution.py:391
  25.9 34.4 %all-to-all-start = ((bf16[32,2,128]{2,1,0:T(2,128)(2,1)}), bf16[32,2,128]{2,1,0:T(2,128)(2,1)S(1)}, u32[]{:S(2)}, u32[]{:S(2)}) async-start(bf16[32,2,128]{2,1,0:T(2,128)(2,1)} %copy.24), calls=%async_computation | async-start | bytes 32768 | tf_op jit(solution)/shard_map/all_to_all | solution.py:402
  35.0 17.2 %collective-permute-start.10 = (bf16[2,128,1024]{2,1,0:T(8,128)(2,1)}, bf16[2,128,1024]{2,1,0:T(8,128)(2,1)}, u32[]{:S(2)}, u32[]{:S(2)}) collective-permute-start(bf16[2,128,1024]{2,1,0:T(8,128)(2,1)} %collective-permute-done.9.refs_0_), channel_id=1, source_target_pairs={{0,2},{1,3},{2,4},{3,5},{4,6},{5,7},{6,0},{7,1},{8,10},{9,11},{10,... | collective-permute-start | bytes 1572872 | tf_op jit(solution)/shard_map/ppermute | solution.py:390
  52.2 10.7 %collective-permute-start.3 = (bf16[128,1024]{1,0:T(8,128)(2,1)S(1)}, bf16[128,1024]{1,0:T(8,128)(2,1)}, u32[]{:S(2)}, u32[]{:S(2)}) collective-permute-start(bf16[128,1024]{1,0:T(8,128)(2,1)S(1)} %slice_bitcast_fusion.2), channel_id=1, source_target_pairs={{0,16},{8,24},{16,0},{24,8},{1,17},{9,25},{17,1},{25,9},{2,18},{10... | collective-permute-start | bytes 786440 | tf_op jit(solution)/shard_map/ppermute | solution.py:391
  52.8 20.8 %collective-permute-start.21 = (bf16[2,128,1024]{2,1,0:T(8,128)(2,1)}, bf16[2,128,1024]{2,1,0:T(8,128)(2,1)}, u32[]{:S(2)}, u32[]{:S(2)}) collective-permute-start(bf16[2,128,1024]{2,1,0:T(8,128)(2,1)} %collective-permute-done.10.refs_0_), channel_id=1, source_target_pairs={{0,16},{8,24},{16,0},{24,8},{1,17},{9,25},{17,1},{25,9},{2,18},{10... | collective-permute-start | bytes 1572872 | tf_op jit(solution)/shard_map/ppermute | solution.py:391
  56.8 16.3 %collective-permute-start.11 = (bf16[2,128,1024]{2,1,0:T(8,128)(2,1)}, bf16[2,128,1024]{2,1,0:T(8,128)(2,1)}, u32[]{:S(2)}, u32[]{:S(2)}) collective-permute-start(bf16[2,128,1024]{2,1,0:T(8,128)(2,1)} %collective-permute-done.10.refs_0_), channel_id=1, source_target_pairs={{0,2},{1,3},{2,4},{3,5},{4,6},{5,7},{6,0},{7,1},{8,10},{9,11},{10,... | collective-permute-start | bytes 1572872 | tf_op jit(solution)/shard_map/ppermute | solution.py:390
  60.3 19.8 %collective-permute-start.18 = (bf16[2,128,1024]{2,1,0:T(8,128)(2,1)}, bf16[2,128,1024]{2,1,0:T(8,128)(2,1)}, u32[]{:S(2)}, u32[]{:S(2)}) collective-permute-start(bf16[2,128,1024]{2,1,0:T(8,128)(2,1)} %pad_maximum_fusion.2.refs_3_), channel_id=1, source_target_pairs={{0,2},{1,3},{2,4},{3,5},{4,6},{5,7},{6,0},{7,1},{8,10},{9,11},{10,... | collective-permute-start | bytes 1572872 | tf_op jit(solution)/shard_map/ppermute | solution.py:390
  63.0 32.7 %collective-permute-start.20 = (bf16[2,128,1024]{2,1,0:T(8,128)(2,1)}, bf16[2,128,1024]{2,1,0:T(8,128)(2,1)}, u32[]{:S(2)}, u32[]{:S(2)}) collective-permute-start(bf16[2,128,1024]{2,1,0:T(8,128)(2,1)} %collective-permute-done.10.refs_0_), channel_id=1, source_target_pairs={{0,1},{1,0},{2,3},{3,2},{4,5},{5,4},{6,7},{7,6},{8,9},{9,8},{10,11... | collective-permute-start | bytes 1572872 | tf_op jit(solution)/shard_map/ppermute | solution.py:389
  73.1 30.5 %collective-permute-start.13 = (bf16[2,128,1024]{2,1,0:T(8,128)(2,1)}, bf16[2,128,1024]{2,1,0:T(8,128)(2,1)}, u32[]{:S(2)}, u32[]{:S(2)}) collective-permute-start(bf16[2,128,1024]{2,1,0:T(8,128)(2,1)} %collective-permute-done.11.refs_0_), channel_id=1, source_target_pairs={{0,16},{8,24},{16,0},{24,8},{1,17},{9,25},{17,1},{25,9},{2,18},{10... | collective-permute-start | bytes 1572872 | tf_op jit(solution)/shard_map/ppermute | solution.py:391
  73.6 30.0 %collective-permute-start.12 = (bf16[2,128,1024]{2,1,0:T(8,128)(2,1)}, bf16[2,128,1024]{2,1,0:T(8,128)(2,1)}, u32[]{:S(2)}, u32[]{:S(2)}) collective-permute-start(bf16[2,128,1024]{2,1,0:T(8,128)(2,1)} %collective-permute-done.11.refs_0_), channel_id=1, source_target_pairs={{0,1},{1,0},{2,3},{3,2},{4,5},{5,4},{6,7},{7,6},{8,9},{9,8},{10,11... | collective-permute-start | bytes 1572872 | tf_op jit(solution)/shard_map/ppermute | solution.py:389
  80.1 23.5 %collective-permute-start.19 = (bf16[2,128,1024]{2,1,0:T(8,128)(2,1)}, bf16[2,128,1024]{2,1,0:T(8,128)(2,1)}, u32[]{:S(2)}, u32[]{:S(2)}) collective-permute-start(bf16[2,128,1024]{2,1,0:T(8,128)(2,1)} %collective-permute-done.18.refs_3_), channel_id=1, source_target_pairs={{0,2},{1,3},{2,4},{3,5},{4,6},{5,7},{6,0},{7,1},{8,10},{9,11},{10,... | collective-permute-start | bytes 1572872 | tf_op jit(solution)/shard_map/ppermute | solution.py:390
  112.4 96.7 %collective-permute-start.36 = (f32[3,256,512]{2,1,0:T(8,128)}, f32[3,256,512]{2,1,0:T(8,128)}, u32[]{:S(2)}, u32[]{:S(2)}) collective-permute-start(f32[3,256,512]{2,1,0:T(8,128)} %get-tuple-element.91), channel_id=1, source_target_pairs={{0,8},{8,0},{16,24},{24,16},{1,9},{9,1},{17,25},{25,17},{2,10},{10... | collective-permute-start | bytes 4718600 | tf_op jit(solution)/shard_map/ppermute | solution.py:392
  124.8 49.0 %collective-permute-start.5 = (bf16[128,512]{1,0:T(8,128)(2,1)}, bf16[128,512]{1,0:T(8,128)(2,1)}, u32[]{:S(2)}, u32[]{:S(2)}) collective-permute-start(bf16[128,512]{1,0:T(8,128)(2,1)} %get-tuple-element.92), channel_id=1, source_target_pairs={{0,16},{8,24},{16,0},{24,8},{1,17},{9,25},{17,1},{25,9},{2,18},{10... | collective-permute-start | bytes 393224 | tf_op jit(solution)/shard_map/ppermute | solution.py:391
  152.7 19.9 %collective-permute-start.22 = (bf16[128,1024]{1,0:T(8,128)(2,1)}, bf16[128,1024]{1,0:T(8,128)(2,1)}, u32[]{:S(2)}, u32[]{:S(2)}) collective-permute-start(bf16[128,1024]{1,0:T(8,128)(2,1)} %get-tuple-element.56), channel_id=1, source_target_pairs={{0,2},{1,3},{2,4},{3,5},{4,6},{5,7},{6,0},{7,1},{8,10},{9,11},{10,... | collective-permute-start | bytes 786440 | tf_op jit(solution)/shard_map/ppermute | solution.py:390
  154.7 17.8 %all-to-all-start.1 = ((bf16[32,2,128]{2,1,0:T(2,128)(2,1)}), bf16[32,2,128]{2,1,0:T(2,128)(2,1)S(1)}, u32[]{:S(2)}, u32[]{:S(2)}) async-start(bf16[32,2,128]{2,1,0:T(2,128)(2,1)} %reshape.50), calls=%async_computation.1 | async-start | bytes 32768 | tf_op jit(solution)/shard_map/all_to_all | solution.py:467
  172.6 45.7 %collective-permute-start.35 = (bf16[3,1024,512]{2,1,0:T(8,128)(2,1)}, bf16[3,1024,512]{2,1,0:T(8,128)(2,1)S(1)}, u32[]{:S(2)}, u32[]{:S(2)}) collective-permute-start(bf16[3,1024,512]{2,1,0:T(8,128)(2,1)} %weights.2), channel_id=1, source_target_pairs={{0,8},{8,0},{16,24},{24,16},{1,9},{9,1},{17,25},{25,17},{2,10},{10... | collective-permute-start | bytes 9437192 | tf_op jit(solution)/shard_map/ppermute | solution.py:392
  173.8 10.6 %collective-permute-start.23 = (bf16[128,1024]{1,0:T(8,128)(2,1)S(1)}, bf16[128,1024]{1,0:T(8,128)(2,1)S(1)}, u32[]{:S(2)}, u32[]{:S(2)}) collective-permute-start(bf16[128,1024]{1,0:T(8,128)(2,1)S(1)} %add_convert_fusion.5), channel_id=1, source_target_pairs={{0,2},{1,3},{2,4},{3,5},{4,6},{5,7},{6,0},{7,1},{8,10},{9,11},{10,... | collective-permute-start | bytes 786440 | tf_op jit(solution)/shard_map/ppermute | solution.py:390
  185.8 14.8 %collective-permute-start.7 = (bf16[128,512]{1,0:T(8,128)(2,1)}, bf16[128,512]{1,0:T(8,128)(2,1)S(1)}, u32[]{:S(2)}, u32[]{:S(2)}) collective-permute-start(bf16[128,512]{1,0:T(8,128)(2,1)} %get-tuple-element.93), channel_id=1, source_target_pairs={{0,1},{1,0},{2,3},{3,2},{4,5},{5,4},{6,7},{7,6},{8,9},{9,8},{10,11... | collective-permute-start | bytes 393224 | tf_op jit(solution)/shard_map/ppermute | solution.py:389
  187.3 12.6 %collective-permute-start.24 = (bf16[128,512]{1,0:T(8,128)(2,1)S(1)}, bf16[128,512]{1,0:T(8,128)(2,1)S(1)}, u32[]{:S(2)}, u32[]{:S(2)}) collective-permute-start(bf16[128,512]{1,0:T(8,128)(2,1)S(1)} %get-tuple-element.94), channel_id=1, source_target_pairs={{0,16},{8,24},{16,0},{24,8},{1,17},{9,25},{17,1},{25,9},{2,18},{10... | collective-permute-start | bytes 393224 | tf_op jit(solution)/shard_map/ppermute | solution.py:391
  (30 other events, 315.5 us)

commit v2 on v0

--- a/solution.py
+++ b/solution.py
@@ -1,6 +1,10 @@
+import functools
+
 import jax
 import jax.numpy as jnp
 from jax import lax
+from jax.experimental import pallas as pl
+from jax.experimental.pallas import tpu as pltpu
 from jax.sharding import PartitionSpec as P
 
 
@@ -48,13 +52,17 @@
     )
 
 
+def capacity_of(tok_rows, top_count, devices):
+    return max(2, (6 * tok_rows * top_count + 5 * devices - 1) // (5 * devices))
+
+
 def shards(tokens, cotangent, expert_ids, gate_weights, expert_weights, shared_weights):
     tok_rows, model_width = tokens.shape
     top_count = expert_ids.shape[1]
     data_count = lax.axis_size("dp")
     expert_count = lax.axis_size("expert")
     devices = data_count * expert_count
-    capacity = max(2, (6 * tok_rows * top_count + 5 * devices - 1) // (5 * devices))
+    capacity = capacity_of(tok_rows, top_count, devices)
     slot_total = devices * capacity
     pair_count = tok_rows * top_count
     row_ids = jnp.arange(tok_rows, dtype=jnp.int32)
@@ -163,6 +171,406 @@
     return (grad_tokens, grad_gates, grad_experts, grad_shared)
 
 
+def strict_upper(rows):
+    r = lax.broadcasted_iota(jnp.int32, (rows, rows), 0)
+    c = lax.broadcasted_iota(jnp.int32, (rows, rows), 1)
+    return (r < c).astype(jnp.bfloat16)
+
+
+def dot32(left, right, dims=((1,), (0,))):
+    return lax.dot_general(left, right, (dims, ((), ())), preferred_element_type=jnp.float32)
+
+
+def route_kernel(s, n, cap, at_ref, gates_ref, *refs):
+    pieces, w_refs = refs[:n], refs[n : n + 2]
+    parts = refs[n + 2 : 2 * n + 2]
+    xs, sy, gg, gu, hb, onehot, yslot, ig = refs[2 * n + 2 :]
+    rows, width = gates_ref.shape[3], pieces[0].shape[1]
+    gates = gates_ref[s]
+    named = jnp.where(gates > 0, 1.0, 0.0)
+    before = dot32(named.reshape(2 * n, rows).astype(jnp.bfloat16), strict_upper(rows))
+    before = before.reshape(n, 2, rows)
+    slot = lax.broadcasted_iota(jnp.int32, (cap, rows), 0).astype(jnp.float32)
+    scales = [[], []]
+    for p in range(n):
+        for j in range(2):
+            hit = (before[p, j][None, :] == slot) & (named[p, j][None, :] > 0)
+            hit = jnp.where(hit, 1.0, 0.0)
+            onehot[p, j * cap : (j + 1) * cap] = hit.astype(jnp.bfloat16)
+            scales[j].append(jnp.sum(hit * gates[p, j][None, :], axis=1, keepdims=True))
+        picked_x = dot32(onehot[p], pieces[p][:rows]).astype(jnp.bfloat16)
+        picked_y = dot32(onehot[p], pieces[p][rows:])
+        for j in range(2):
+            here = slice(p * cap, (p + 1) * cap)
+            there = slice(j * cap, (j + 1) * cap)
+            xs[j, here] = picked_x[there]
+            yslot[j, here] = picked_y[there].astype(jnp.bfloat16)
+            sy[j, here] = (picked_y[there] * scales[j][p]).astype(jnp.bfloat16)
+    hidden_units = w_refs[0].shape[2]
+    tile = min(256, hidden_units)
+    grads = []
+    for j, w in enumerate(w_refs):
+        scale = jnp.concatenate(scales[j], axis=0)
+        gate_grad = jnp.zeros((n * cap, 1), jnp.float32)
+        for f in range(0, hidden_units, tile):
+            cols = slice(f, f + tile)
+            pre_gate = dot32(xs[j], w[0, :, cols])
+            pre_up = dot32(xs[j], w[1, :, cols])
+            back = dot32(yslot[j], w[2, :, cols])
+            activated, slope = silu_parts(pre_gate)
+            hidden = activated * pre_up
+            gate_grad += jnp.sum(hidden * back, axis=1, keepdims=True)
+            scaled = scale * back
+            gg[j, :, cols] = (scaled * pre_up * slope).astype(jnp.bfloat16)
+            gu[j, :, cols] = (scaled * activated).astype(jnp.bfloat16)
+            hb[j, :, cols] = hidden.astype(jnp.bfloat16)
+        ig[j] = (
+            dot32(gg[j], w[0], ((1,), (1,))) + dot32(gu[j], w[1], ((1,), (1,)))
+        ).astype(jnp.bfloat16)
+        grads.append(gate_grad)
+    extra = parts[0].shape[0] - rows
+    row = lax.broadcasted_iota(jnp.int32, (extra, width), 0)
+    block = lax.broadcasted_iota(jnp.int32, (extra, width), 1) // rows
+    for p in range(n):
+        tail = jnp.zeros((extra, width), jnp.float32)
+        for j in range(2):
+            here = slice(p * cap, (p + 1) * cap)
+            hit = onehot[p, j * cap : (j + 1) * cap].astype(jnp.float32)
+            line = jnp.sum(hit * grads[j][here], axis=0, keepdims=True)
+            line = jnp.concatenate([line] * (width // rows), axis=1)
+            mine = (row == at_ref[2 * j]) & (block == at_ref[2 * j + 1])
+            tail = tail + jnp.where(mine, line, 0.0)
+        both = jnp.concatenate([ig[j, here] for j in range(2)], axis=0)
+        parts[p][:rows] = dot32(onehot[p], both, ((0,), (0,))).astype(parts[p].dtype)
+        parts[p][rows:] = tail.astype(jnp.bfloat16).astype(parts[p].dtype)
+
+
+MIB = 1024 * 1024
+IN_SMEM = pl.BlockSpec(memory_space=pltpu.SMEM)
+IN_VMEM = pl.BlockSpec(memory_space=pltpu.VMEM)
+
+
+def route(s, cap, extra, at, gates, pieces, w_own, w_sib):
+    n, rows, width = len(pieces), gates.shape[3], pieces[0].shape[1]
+    hidden_units = w_own.shape[2]
+    slots = n * cap
+    shape, scratch = jax.ShapeDtypeStruct, pltpu.VMEM
+    bf = jnp.bfloat16
+    out_shape = [shape((rows + extra, width), jnp.float32)]
+    out_shape += [shape((rows + extra, width), bf)] * (n - 1)
+    out_shape += [shape((2, slots, width), bf)] * 2 + [shape((2, slots, hidden_units), bf)] * 3
+    outs = pl.pallas_call(
+        functools.partial(route_kernel, s, n, cap),
+        out_shape=out_shape,
+        in_specs=[IN_SMEM] + [IN_VMEM] * (n + 3),
+        out_specs=[IN_VMEM] * (n + 5),
+        scratch_shapes=[
+            scratch((n, 2 * cap, rows), bf),
+            scratch((2, slots, width), bf),
+            scratch((2, slots, width), bf),
+        ],
+        cost_estimate=pl.CostEstimate(
+            flops=20 * slots * width * hidden_units,
+            bytes_accessed=4 * w_own.size + 16 * slots * width,
+            transcendentals=0,
+        ),
+        compiler_params=pltpu.CompilerParams(vmem_limit_bytes=20 * MIB),
+        name="route",
+    )(at, gates, *pieces, w_own, w_sib)
+    return outs[:n], outs[n:]
+
+
+def common_kernel(n, first, last, where_ref, *refs):
+    pieces, w, refs = refs[:n], refs[n], refs[n + 1 :]
+    (own_grad,), refs = (refs[:1], refs[1:]) if first else ((None,), refs)
+    (total_in,), refs = ((None,), refs) if first else (refs[:1], refs[1:])
+    outs, (x, y, gg, gu, hb) = refs[:-5], refs[-5:]
+    rows = pieces[0].shape[0] // 2
+    for p in range(n):
+        x[p * rows : (p + 1) * rows] = pieces[p][:rows]
+        y[p * rows : (p + 1) * rows] = pieces[p][rows:]
+    hidden_units = w.shape[2]
+    tile = min(256, hidden_units)
+    chunk = 4 * rows
+    for r in range(0, n * rows, chunk):
+        at = slice(r, r + chunk)
+        for f in range(0, hidden_units, tile):
+            cols = slice(f, f + tile)
+            pre_gate = dot32(x[at], w[0, :, cols])
+            pre_up = dot32(x[at], w[1, :, cols])
+            back = dot32(y[at], w[2, :, cols])
+            activated, slope = silu_parts(pre_gate)
+            gg[at, cols] = (back * pre_up * slope).astype(jnp.bfloat16)
+            gu[at, cols] = (back * activated).astype(jnp.bfloat16)
+            hb[at, cols] = (activated * pre_up).astype(jnp.bfloat16)
+    if first:
+        own_grad[...] = dot32(gg[:rows], w[0], ((1,), (1,))) + dot32(gu[:rows], w[1], ((1,), (1,)))
+    kept = outs[0].shape[1] * (2 if last else 1)
+    half = kept // 2
+    for i, (left, right) in enumerate(((x, gg), (x, gu), (y, hb))):
+        if last:
+            core = where_ref[1]
+            for out, block in zip(outs, (core, 1 - core)):
+                keep = pl.ds(pl.multiple_of(where_ref[0] * kept + block * half, half), half)
+                term = dot32(left[:, keep], right[...], ((0,), (0,)))
+                out[i] = term + total_in[i, pl.ds(pl.multiple_of(block * half, half), half)]
+        else:
+            keep = pl.ds(pl.multiple_of(where_ref[0] * kept, kept), kept)
+            term = dot32(left[:, keep], right[...], ((0,), (0,)))
+            outs[0][i] = term if first else term + total_in[i]
+
+
+def common(where_at, kept, pieces, w, total, last=False):
+    first = total is None
+    n, rows, width = len(pieces), pieces[0].shape[0] // 2, pieces[0].shape[1]
+    hidden_units = w.shape[2]
+    shape, scratch = jax.ShapeDtypeStruct, pltpu.VMEM
+    bf, f32 = jnp.bfloat16, jnp.float32
+    out_shape = [shape((rows, width), f32)] if first else []
+    if last:
+        out_shape += [shape((3, kept // 2, hidden_units), f32)] * 2
+    else:
+        out_shape += [shape((3, kept, hidden_units), f32)]
+    args = list(pieces) + [w] + ([] if first else [total])
+    return pl.pallas_call(
+        functools.partial(common_kernel, n, first, last),
+        out_shape=out_shape,
+        in_specs=[IN_SMEM] + [IN_VMEM] * len(args),
+        out_specs=[IN_VMEM] * len(out_shape),
+        scratch_shapes=[scratch((n * rows, width), bf)] * 2
+        + [scratch((n * rows, hidden_units), bf)] * 3,
+        cost_estimate=pl.CostEstimate(
+            flops=6 * n * rows * hidden_units * (width + kept),
+            bytes_accessed=2 * w.size + n * rows * width * 4,
+            transcendentals=0,
+        ),
+        compiler_params=pltpu.CompilerParams(vmem_limit_bytes=24 * MIB),
+        name="common",
+    )(where_at, *args)
+
+
+def weights_kernel(groups, *refs):
+    saved, (own, sib, xs, sy, gg, gu, hb) = refs[: 5 * groups], refs[5 * groups :]
+    for j in (1, 0):
+        at = 0
+        for g in range(groups):
+            slots = saved[5 * g].shape[1]
+            for i, into in enumerate((xs, sy, gg, gu, hb)):
+                into[at : at + slots] = saved[5 * g + i][j]
+            at += slots
+        for i, (left, right) in enumerate(((xs, gg), (xs, gu), (sy, hb))):
+            out = (own, sib)[j]
+            out[i] = dot32(left[...], right[...], ((0,), (0,))).astype(out.dtype)
+
+
+def weights(saved):
+    groups = len(saved)
+    flat = [a for group in saved for a in group]
+    width, hidden_units = flat[0].shape[2], flat[2].shape[2]
+    slots = sum(group[0].shape[1] for group in saved)
+    bf, scratch = jnp.bfloat16, pltpu.VMEM
+    return pl.pallas_call(
+        functools.partial(weights_kernel, groups),
+        out_shape=[
+            jax.ShapeDtypeStruct((3, width, hidden_units), bf),
+            jax.ShapeDtypeStruct((3, width, hidden_units), bf),
+        ],
+        in_specs=[IN_VMEM] * len(flat),
+        out_specs=[IN_VMEM] * 2,
+        scratch_shapes=[scratch((slots, width), bf)] * 2 + [scratch((slots, hidden_units), bf)] * 3,
+        cost_estimate=pl.CostEstimate(
+            flops=12 * slots * width * hidden_units,
+            bytes_accessed=slots * (8 * width + 12 * hidden_units),
+            transcendentals=0,
+        ),
+        compiler_params=pltpu.CompilerParams(vmem_limit_bytes=32 * MIB),
+        name="weights",
+    )(*flat)
+
+
+def add_kernel(left, right, out):
+    total = left[...].astype(jnp.float32) + right[...].astype(jnp.float32)
+    out[...] = total.astype(out.dtype)
+
+
+def add(left, right, dtype):
+    block = pl.BlockSpec((1,) + left.shape[1:], lambda i: (i, 0, 0))
+    return pl.pallas_call(
+        add_kernel,
+        grid=(left.shape[0],),
+        out_shape=jax.ShapeDtypeStruct(left.shape, dtype),
+        in_specs=[block] * 2,
+        out_specs=block,
+        compiler_params=pltpu.CompilerParams(vmem_limit_bytes=12 * MIB),
+        name="add",
+    )(left, right)
+
+
+def join_kernel(left, right, out):
+    rows = left.shape[0]
+    out[:rows] = left[...]
+    out[rows:] = right[...]
+
+
+def join(left, right):
+    rows, width = left.shape
+    return pl.pallas_call(
+        join_kernel,
+        out_shape=jax.ShapeDtypeStruct((2 * rows, width), left.dtype),
+        in_specs=[IN_VMEM] * 2,
+        out_specs=IN_VMEM,
+        compiler_params=pltpu.CompilerParams(vmem_limit_bytes=4 * MIB),
+        name="join",
+    )(left, right)
+
+
+def finish_kernel(terms, ids_ref, *refs):
+    sums, own_grad, (tokens_out, gates_out) = refs[:terms], refs[terms], refs[terms + 1 :]
+    rows, top_count = ids_ref.shape
+    total = sums[0][...].astype(jnp.float32)
+    for ref in sums[1:]:
+        total = total + ref[...].astype(jnp.float32)
+    tokens_out[...] = (total[:rows] + own_grad[...]).astype(tokens_out.dtype)
+    blocks = total.shape[1] // rows
+    lines = [
+        total[r : r + 1, b * rows : (b + 1) * rows]
+        for r in range(rows, total.shape[0])
+        for b in range(blocks)
+    ]
+    by_expert = jnp.concatenate(lines, axis=0).T
+    expert = lax.broadcasted_iota(jnp.int32, by_expert.shape, 1)
+    picked = [
+        jnp.sum(jnp.where(ids_ref[:, k : k + 1] == expert, by_expert, 0.0), axis=1, keepdims=True)
+        for k in range(top_count)
+    ]
+    gates_out[...] = jnp.concatenate(picked, axis=1).astype(gates_out.dtype)
+
+
+def finish(expert_ids, sums, own_grad):
+    rows, top_count = expert_ids.shape
+    return pl.pallas_call(
+        functools.partial(finish_kernel, len(sums)),
+        out_shape=[
+            jax.ShapeDtypeStruct(own_grad.shape, jnp.bfloat16),
+            jax.ShapeDtypeStruct((rows, top_count), jnp.bfloat16),
+        ],
+        in_specs=[IN_VMEM] * (len(sums) + 2),
+        out_specs=[IN_VMEM] * 2,
+        compiler_params=pltpu.CompilerParams(vmem_limit_bytes=8 * MIB),
+        name="finish",
+    )(expert_ids, *sums, own_grad)
+
+
+def shared_rows(tokens, cotangent, expert_ids, gate_weights, expert_weights, shared_weights):
+    return shared_rows_body(
+        tokens, cotangent, expert_ids, gate_weights, expert_weights, shared_weights
+    )
+
+
+def shared_rows_body(tokens, cotangent, expert_ids, gate_weights, expert_weights, shared_weights):
+    rows, width = tokens.shape
+    top_count = expert_ids.shape[1]
+    data_count, expert_count = lax.axis_size("dp"), lax.axis_size("expert")
+    devices = data_count * expert_count
+    cap = capacity_of(rows, top_count, devices)
+    planes = expert_count // 2
+    bf, f32 = jnp.bfloat16, jnp.float32
+    me_dp, me_ex = lax.axis_index("dp"), lax.axis_index("expert")
+    routes = {
+        "x": ("expert", [(e, e ^ 1) for e in range(expert_count)]),
+        "+": ("expert", [(e, (e + 2) % expert_count) for e in range(expert_count)]),
+        "-": ("expert", [(e, (e - 2) % expert_count) for e in range(expert_count)]),
+        "--": ("expert", [(e, (e - 4) % expert_count) for e in range(expert_count)]),
+        "y": ("dp", [(d, d ^ 2) for d in range(data_count)]),
+        "core": ("dp", [(d, d ^ 1) for d in range(data_count)]),
+    }
+
+    def send(way, array):
+        return lax.ppermute(array, *routes[way])
+
+    w_own = expert_weights[0]
+    own = join(tokens, cotangent)
+    w_sib = send("core", w_own)
+
+    c, x, y, d = [own] + [None] * 3, [None] * 4, [None] * 4, [None] * 4
+    c[1] = send("+", c[0])
+    c[2] = send("+", c[1])
+    c[3] = send("-", c[0])
+    for s in range(planes):
+        x[s] = send("x", c[s])
+        y[s] = send("y", c[s])
+    d[0] = send("x", y[0])
+    d[1] = send("+", d[0])
+    d[2] = send("y", x[2])
+    d[3] = send("-", d[0])
+
+    matches = expert_ids[:, :, None] == jnp.arange(devices, dtype=jnp.int32)
+    by_expert = jnp.sum(jnp.where(matches, gate_weights[:, :, None].astype(f32), 0.0), axis=1)
+    by_expert = by_expert.T.astype(bf).reshape(data_count // 2, 2, expert_count, rows)
+    outward = jnp.stack([by_expert, by_expert[:, ::-1]], axis=3).reshape(devices, 2, rows)
+    inward = lax.all_to_all(outward, ("dp", "expert"), 0, 0, tiled=True)
+    order = []
+    for s in range(planes):
+        plane = (me_ex // 2 + planes - s) % planes
+        for dy, dx in ((0, 0), (0, 1), (1, 0), (1, 1)):
+            source = (me_dp ^ (2 * dy)) * expert_count + plane * 2 + (me_ex % 2 ^ dx)
+            order.append(source)
+    pick = jnp.stack(order)[:, None] == jnp.arange(devices, dtype=jnp.int32)[None, :]
+    pick = pick.astype(bf)
+    gates = jnp.dot(pick, inward.reshape(devices, 2 * rows), preferred_element_type=f32)
+    gates = gates.reshape(planes, 4, 2, rows)
+
+    extra = 8 * (-(-devices * rows // (8 * width)))
+    blocks = width // rows
+    me = me_dp * expert_count + me_ex
+    sibling = (me_dp ^ 1) * expert_count + me_ex
+    at = jnp.stack([me // blocks, me % blocks, sibling // blocks, sibling % blocks])
+    at = at.astype(jnp.int32)
+    part, saved = [None] * 4, [None] * 4
+    for s in (0, 2, 1, 3):
+        part[s], saved[s] = route(s, cap, extra, at, gates, (c[s], x[s], y[s], d[s]), w_own, w_sib)
+    pc, px, py, pd = zip(*part)
+
+    where_at = jnp.stack([me_dp // 2, me_dp % 2]).astype(jnp.int32)
+    kept = 2 * (width // data_count)
+    pieces = (c[0], x[0], y[0], c[1])
+    shared_grad, total = common(where_at, kept, pieces, shared_weights, None)
+    pieces = (d[0], y[1], c[2], y[2])
+    (total,) = common(where_at, kept, pieces, shared_weights, total)
+    pieces = (x[2], c[3], x[1], d[1], d[2], x[3], y[3], d[3])
+    mine, other = common(where_at, kept, pieces, shared_weights, total, last=True)
+
+    def plus(*terms):
+        total = terms[0].astype(f32)
+        for term in terms[1:]:
+            total = total + term.astype(f32)
+        return total
+
+    def home_x(array):
+        return send("x", array.astype(bf))
+
+    def home_y(array):
+        return send("y", array.astype(bf))
+
+    x2 = plus(px[2], send("y", pd[2]))
+    c2 = plus(pc[2], home_x(x2), home_y(py[2]))
+    c1 = plus(pc[1], home_x(px[1]), home_y(py[1]))
+    c3 = plus(pc[3], home_x(px[3]), home_y(py[3]))
+    d0 = plus(pd[0], send("-", pd[1]), send("+", pd[3]))
+    y0 = plus(py[0], send("x", d0.astype(bf)))
+    sums = (pc[0], home_x(px[0]), home_y(y0))
+    sums += (send("-", c1.astype(bf)), send("+", c3.astype(bf)))
+    sums += (send("--", c2.astype(bf)),)
+    grad_tokens, grad_gates = finish(expert_ids, sums, shared_grad)
+
+    mine_experts, for_sib = weights(saved)
+    came = send("core", for_sib)
+    came_shared = send("core", other)
+    grad_experts = add(mine_experts, came, bf)[None]
+    grad_shared = add(mine, came_shared, f32)
+    return (grad_tokens, grad_gates, grad_experts, grad_shared)
+
+
 def solution(mesh):
     placed = (
         P(("dp", "expert"), None),
@@ -172,8 +580,9 @@
         P(("dp", "expert"), None, None, None),
         P(),
     )
+    share = mesh.shape["dp"] == 4 and mesh.shape["expert"] == 8
     return jax.shard_map(
-        shards,
+        shared_rows if share else shards,
         mesh=mesh,
         in_specs=placed,
         out_specs=(

time: 507 us -> 217 us (0.43)
  waiting for transfers between devices: 313 us -> 90.7 us
  local copies, waits for them, and re-layouts: 82.2 us -> 27.9 us
  Pallas kernels: 0 us -> 54 us
  matrix products: 36.7 us -> 0.19 us
  between operations: 14.5 us -> 1.18 us
  other arithmetic: 13.1 us -> 5.05 us
  blocking collectives: 7.85 us -> 0 us
    all_to_all x9 -> x1, waiting for transfers between devices: 289 us -> 18.4 us  [shared_rows_body(): inward = lax.all_to_all(outward, ('dp', 'expert'), 0, 0, tiled=True)]
    ppermute x0 -> x33, waiting for transfers between devices: none -> 72.2 us  [send(): return lax.ppermute(array, *routes[way])]
    pallas_call x0 -> x12, Pallas kernels: none -> 54 us  [the longest x4 21.3 us: route(): pl.pallas_call(functools.partial(route_kernel, s, n, cap), out_shape=out_...]
    dot_general x13 -> x1, matrix products: 36.7 us -> 0.19 us  [shared_rows_body(): jnp.dot(pick, inward.reshape(devices, 2 * rows), preferred_element_type=f32)]
    all_to_all x9 -> x1, starting transfers between devices: 38 us -> 2.87 us  [shared_rows_body(): inward = lax.all_to_all(outward, ('dp', 'expert'), 0, 0, tiled=True)]
    ppermute x0 -> x33, starting transfers between devices: none -> 34.6 us  [send(): return lax.ppermute(array, *routes[way])]
    gather x6 -> x0, local copies, waits for them, and re-layouts: 34.3 us -> none  [the longest x1 9.46 us: shards(): padded_gates[slot_table].reshape(data_count, expert_count, capacity)]
    psum x1 -> x0, waiting for transfers between devices: 24.6 us -> none  [shards(): totals = lax.psum(kept, 'expert')]
  transfers between devices with their start and end apart: 11 -> 34, of which waited for: 9 -> 15; matrix products, arithmetic and copies ran while one was open for 21% -> 3% of each run, Pallas kernels for 0% -> 17%
where the time goes in v2:
time: 217 us; the launch traced here: 216 us
  waiting for transfers between devices  90.7 us (42%)
  Pallas kernels  54 us (25%)
  starting transfers between devices  37.5 us (17%)
  local copies, waits for them, and re-layouts  27.9 us (13%)
  other arithmetic  5.05 us (2%)
    ppermute x33, waiting for transfers between devices, send(): return lax.ppermute(array, *routes[way])  72.2 us
    ppermute x33, starting transfers between devices, send(): return lax.ppermute(array, *routes[way])  34.6 us
    unnamed x114, local copies, waits for them, and re-layouts  27.1 us
    pallas_call x4, Pallas kernels, route(): pl.pallas_call(functools.partial(route_kernel, s, n, cap), out_shape=out_...  21.3 us
    all_to_all x1, waiting for transfers between devices, shared_rows_body(): inward = lax.all_to_all(outward, ('dp', 'expert'), 0, 0, tiled=True)  18.4 us
    pallas_call x3, Pallas kernels, common(): pl.pallas_call(functools.partial(common_kernel, n, first, last), out_shap...  16.5 us
    pallas_call x1, Pallas kernels, weights(): pl.pallas_call(functools.partial(weights_kernel, groups), out_shape=[jax....  6.42 us
    pallas_call x2, Pallas kernels, add(): pl.pallas_call(add_kernel, grid=(left.shape[0],), out_shape=jax.ShapeDtyp...  6.38 us
  transfers between devices with their start and end apart: 34, of which 15 were waited for; matrix products, arithmetic and copies ran while one was open for 3% of the time, Pallas kernels for 17%

profile of v2, /device:TPU:0, one launch (start us, length us, event | category | flops | bytes accessed | tf_op | source)
XLA Modules:
  0.0 216.5 jit_solution(17499469143086989415)
XLA Ops:
  3.1 2.6 %collective-permute-start.5 = (bf16[256,1024]{1,0:T(8,128)(2,1)S(1)}, bf16[256,1024]{1,0:T(8,128)(2,1)}, u32[]{:S(2)}, u32[]{:S(2)}) collective-permute-start(bf16[256,1024]{1,0:T(8,128)(2,1)S(1)} %join.1.refs_0_), channel_id=1, source_target_pairs={{0,2},{1,3},{2,4},{3,5},{4,6},{5,7},{6,0},{7,1},{8,10},{9,11},{10,... | collective-permute-start | bytes 1572872 | tf_op jit(solution)/shard_map/ppermute | solution.py:489
  5.8 14.7 %collective-permute-done.5.refs_0_.refs_3_ = bf16[256,1024]{1,0:T(8,128)(2,1)} collective-permute-done((bf16[256,1024]{1,0:T(8,128)(2,1)S(1)}, bf16[256,1024]{1,0:T(8,128)(2,1)}, u32[]{:S(2)}, u32[]{:S(2)}) %collective-permute-start.5) | collective-permute-done | bytes 524320 | tf_op jit(solution)/shard_map/ppermute | solution.py:489
  20.5 3.8 %collective-permute-start.10 = (bf16[256,1024]{1,0:T(8,128)(2,1)S(1)}, bf16[256,1024]{1,0:T(8,128)(2,1)}, u32[]{:S(2)}, u32[]{:S(2)}) collective-permute-start(bf16[256,1024]{1,0:T(8,128)(2,1)S(1)} %join.1.refs_0_), channel_id=1, source_target_pairs={{0,6},{1,7},{2,0},{3,1},{4,2},{5,3},{6,4},{7,5},{8,14},{9,15},{10,... | collective-permute-start | bytes 1572872 | tf_op jit(solution)/shard_map/ppermute | solution.py:489
  28.1 9.3 %collective-permute-done.23.refs_0_.refs_2_ = bf16[256,1024]{1,0:T(8,128)(2,1)} collective-permute-done((bf16[256,1024]{1,0:T(8,128)(2,1)}, bf16[256,1024]{1,0:T(8,128)(2,1)}, u32[]{:S(2)}, u32[]{:S(2)}) %collective-permute-start.23) | collective-permute-done | bytes 524320 | tf_op jit(solution)/shard_map/ppermute | solution.py:489
  38.9 6.7 %collective-permute-done.10.refs_0_.refs_1_ = bf16[256,1024]{1,0:T(8,128)(2,1)} collective-permute-done((bf16[256,1024]{1,0:T(8,128)(2,1)S(1)}, bf16[256,1024]{1,0:T(8,128)(2,1)}, u32[]{:S(2)}, u32[]{:S(2)}) %collective-permute-start.10) | collective-permute-done | bytes 524320 | tf_op jit(solution)/shard_map/ppermute | solution.py:489
  53.5 2.9 %all-to-all-start = ((bf16[32,2,128]{2,1,0:T(2,128)(2,1)}), bf16[32,2,128]{2,1,0:T(2,128)(2,1)S(1)}, u32[]{:S(2)}, u32[]{:S(2)}) async-start(bf16[32,2,128]{2,1,0:T(2,128)(2,1)} %copy.47), calls=%async_computation | async-start | bytes 32768 | tf_op jit(solution)/shard_map/all_to_all | solution.py:511
  56.7 4.0 %collective-permute-done.7.refs_2_.refs_1_ = bf16[256,1024]{1,0:T(8,128)(2,1)} collective-permute-done((bf16[256,1024]{1,0:T(8,128)(2,1)}, bf16[256,1024]{1,0:T(8,128)(2,1)}, u32[]{:S(2)}, u32[]{:S(2)}) %collective-permute-start.7) | collective-permute-done | bytes 524320 | tf_op jit(solution)/shard_map/ppermute | solution.py:489
  63.0 18.4 %all-to-all-done = bf16[32,2,128]{2,1,0:T(2,128)(2,1)S(1)} async-done(((bf16[32,2,128]{2,1,0:T(2,128)(2,1)}), bf16[32,2,128]{2,1,0:T(2,128)(2,1)S(1)}, u32[]{:S(2)}, u32[]{:S(2)}) %all-to-all-start) | async-done | bytes 16416 | tf_op jit(solution)/shard_map/all_to_all | solution.py:511
  84.3 2.6 %collective-permute-start.13 = (bf16[256,1024]{1,0:T(8,128)(2,1)}, bf16[256,1024]{1,0:T(8,128)(2,1)S(1)}, u32[]{:S(2)}, u32[]{:S(2)}) collective-permute-start(bf16[256,1024]{1,0:T(8,128)(2,1)} %collective-permute-done.2.refs_3_.refs_0_), channel_id=1, source_target_pairs={{0,6},{1,7},{2,0},{3,1},{4,2},{5,3},{6,4},{7,5},{8,14},{9,15},{10,... | collective-permute-start | bytes 1572872 | tf_op jit(solution)/shard_map/ppermute | solution.py:489
  90.8 5.1 %route.4 = (f32[136,1024]{1,0:T(8,128)S(1)}, bf16[136,1024]{1,0:T(8,128)(2,1)S(1)}, bf16[136,1024]{1,0:T(8,128)(2,1)S(1)}, bf16[136,1024]{1,0:T(8,128)(2,1)S(1)}...) custom-call(s32[4]{0:T(128)S(1)} %pad_add_fusion.at_ref, ...), custom_call_target="tpu_custom_call" | custom-call | flops 2013265920 | bytes 9437184 | tf_op jit(solution)/shard_map/route/pallas_call | solution.py:262
  98.1 5.5 %route.7 = (f32[136,1024]{1,0:T(8,128)S(1)}, bf16[136,1024]{1,0:T(8,128)(2,1)S(1)}, bf16[136,1024]{1,0:T(8,128)(2,1)S(1)}, bf16[136,1024]{1,0:T(8,128)(2,1)S(1)}...) custom-call(s32[4]{0:T(128)S(1)} %pad_add_fusion.at_ref, ...), custom_call_target="tpu_custom_call" | custom-call | flops 2013265920 | bytes 9437184 | tf_op jit(solution)/shard_map/route/pallas_call | solution.py:262
  104.4 5.5 %route.5 = (f32[136,1024]{1,0:T(8,128)S(1)}, bf16[136,1024]{1,0:T(8,128)(2,1)S(1)}, bf16[136,1024]{1,0:T(8,128)(2,1)S(1)}, bf16[136,1024]{1,0:T(8,128)(2,1)S(1)}...) custom-call(s32[4]{0:T(128)S(1)} %pad_add_fusion.at_ref, ...), custom_call_target="tpu_custom_call" | custom-call | flops 2013265920 | bytes 9437184 | tf_op jit(solution)/shard_map/route/pallas_call | solution.py:262
  112.9 5.2 %route.6 = (f32[136,1024]{1,0:T(8,128)S(1)}, bf16[136,1024]{1,0:T(8,128)(2,1)S(1)}, bf16[136,1024]{1,0:T(8,128)(2,1)S(1)}, bf16[136,1024]{1,0:T(8,128)(2,1)S(1)}...) custom-call(s32[4]{0:T(128)S(1)} %pad_add_fusion.at_ref, ...), custom_call_target="tpu_custom_call" | custom-call | flops 2013265920 | bytes 9437184 | tf_op jit(solution)/shard_map/route/pallas_call | solution.py:262
  121.2 6.4 %weights.1 = (bf16[3,1024,512]{2,1,0:T(8,128)(2,1)S(1)}, bf16[3,1024,512]{2,1,0:T(8,128)(2,1)}) custom-call(bf16[2,192,1024]{2,1,0:T(8,128)(2,1)S(1)} %get-tuple-element.67.refs_0_, bf16[2,192,1024]{2,1,0:T(8,128)(2,1)S(1)} %get-tuple-element.68.refs_1_, bf16[2,192,512]{2,1,0:T(8,128)(2,1)S(1)} %get-tuple-element.69.refs_2_, ...), custom_call_target="tpu_custom_call" | custom-call | flops 4831838208 | bytes 11010048 | tf_op jit(solution)/shard_map/weights/pallas_call | solution.py:372
  131.4 4.6 %common.3 = (f32[128,1024]{1,0:T(8,128)S(1)}, f32[3,512,512]{2,1,0:T(8,128)S(1)}) custom-call(s32[2]{0:T(128)S(1)} %pad_add_fusion.1.where_ref, bf16[256,1024]{1,0:T(8,128)(2,1)S(1)} %copy-done.7, bf16[256,1024]{1,0:T(8,128)(2,1)S(1)} %copy-done.22, bf16[256,1024]{1,0:T(8,128)(2,1)} %collective-permute-done.1.refs_2_, ...), custom_call_target="tpu_custom_call" | custom-call | flops 2415919104 | bytes 5242880 | tf_op jit(solution)/shard_map/common/pallas_call | solution.py:335
  136.1 4.6 %common.4.refs_9_ = f32[3,512,512]{2,1,0:T(8,128)S(1)} custom-call(s32[2]{0:T(128)S(1)} %pad_add_fusion.1.where_ref, bf16[256,1024]{1,0:T(8,128)(2,1)} %collective-permute-done.2.refs_3_.refs_0_, bf16[256,1024]{1,0:T(8,128)(2,1)} %collective-permute-done.7.refs_2_.refs_1_, bf16[256,1024]{1,0:T(8,128)(2,1)} %collective-permute-done.23.refs_0_.refs_2_, ...), custom_call_target="tpu_custom_call" | custom-call | flops 2415919104 | bytes 5242880 | tf_op jit(solution)/shard_map/common/pallas_call | solution.py:335
  142.4 7.3 %common.5 = (f32[3,256,512]{2,1,0:T(8,128)S(1)}, f32[3,256,512]{2,1,0:T(8,128)S(1)}) custom-call(s32[2]{0:T(128)S(1)} %pad_add_fusion.1.where_ref, bf16[256,1024]{1,0:T(8,128)(2,1)} %collective-permute-done.24.refs_1_.refs_0_, bf16[256,1024]{1,0:T(8,128)(2,1)} %collective-permute-done.10.refs_0_.refs_1_, ...), custom_call_target="tpu_custom_call" | custom-call | flops 4831838208 | bytes 7340032 | tf_op jit(solution)/shard_map/common/pallas_call | solution.py:335
  154.0 11.0 %collective-permute-done.9 = bf16[136,1024]{1,0:T(8,128)(2,1)S(1)} collective-permute-done((bf16[136,1024]{1,0:T(8,128)(2,1)S(1)}, bf16[136,1024]{1,0:T(8,128)(2,1)S(1)}, u32[]{:S(2)}, u32[]{:S(2)}) %collective-permute-start.9) | collective-permute-done | bytes 278560 | tf_op jit(solution)/shard_map/ppermute | solution.py:489
  168.4 6.1 %collective-permute-done.20 = bf16[136,1024]{1,0:T(8,128)(2,1)S(1)} collective-permute-done((bf16[136,1024]{1,0:T(8,128)(2,1)S(1)}, bf16[136,1024]{1,0:T(8,128)(2,1)S(1)}, u32[]{:S(2)}, u32[]{:S(2)}) %collective-permute-start.20) | collective-permute-done | bytes 278560 | tf_op jit(solution)/shard_map/ppermute | solution.py:489
  177.3 3.1 %collective-permute-done.15 = bf16[136,1024]{1,0:T(8,128)(2,1)S(1)} collective-permute-done((bf16[136,1024]{1,0:T(8,128)(2,1)S(1)}, bf16[136,1024]{1,0:T(8,128)(2,1)S(1)}, u32[]{:S(2)}, u32[]{:S(2)}) %collective-permute-start.15) | collective-permute-done | bytes 278560 | tf_op jit(solution)/shard_map/ppermute | solution.py:489
  182.2 3.9 %collective-permute-done.28 = bf16[136,1024]{1,0:T(8,128)(2,1)S(1)} collective-permute-done((bf16[136,1024]{1,0:T(8,128)(2,1)S(1)}, bf16[136,1024]{1,0:T(8,128)(2,1)S(1)}, u32[]{:S(2)}, u32[]{:S(2)}) %collective-permute-start.28) | collective-permute-done | bytes 278560 | tf_op jit(solution)/shard_map/ppermute | solution.py:489
  196.6 9.0 %collective-permute-done.30.refs_5_ = bf16[136,1024]{1,0:T(8,128)(2,1)} collective-permute-done((bf16[136,1024]{1,0:T(8,128)(2,1)}, bf16[136,1024]{1,0:T(8,128)(2,1)}, u32[]{:S(2)}, u32[]{:S(2)}) %collective-permute-start.30) | collective-permute-done | bytes 278560 | tf_op jit(solution)/shard_map/ppermute | solution.py:489
  207.7 3.4 %finish.1 = (bf16[128,1024]{1,0:T(8,128)(2,1)}, bf16[128,10]{1,0:T(8,128)(2,1)S(1)}) custom-call(s32[128,10]{1,0:T(8,128)S(1)} %copy.53.ids_ref, f32[136,1024]{1,0:T(8,128)S(1)} %copy-done.13, bf16[136,1024]{1,0:T(8,128)(2,1)S(1)} %collective-permute-done.4.refs_1_, bf16[136,1024]{1,0:T(8,128)(2,1)} %collective-permute-done.16.refs_2_, ...), custom_call_target="tpu_custom_call" | custom-call | tf_op jit(solution)/shard_map/finish/pallas_call | solution.py:451
  211.8 4.7 %add.240 = bf16[3,1024,512]{2,1,0:T(8,128)(2,1)} custom-call(bf16[3,1024,512]{2,1,0:T(8,128)(2,1)S(1)} %copy-done.4, bf16[3,1024,512]{2,1,0:T(8,128)(2,1)} %collective-permute-done.31.right), custom_call_target="tpu_custom_call" | custom-call | tf_op jit(solution)/shard_map/add/pallas_call | solution.py:398
  (187 shorter events, 64.9 us)
Async XLA Ops:
  0.6 83.6 %collective-permute-start.3 = (bf16[3,1024,512]{2,1,0:T(8,128)(2,1)}, bf16[3,1024,512]{2,1,0:T(8,128)(2,1)S(1)}, u32[]{:S(2)}, u32[]{:S(2)}) collective-permute-start(bf16[3,1024,512]{2,1,0:T(8,128)(2,1)} %bitcast.52), channel_id=1, source_target_pairs={{0,8},{8,0},{16,24},{24,16},{1,9},{9,1},{17,25},{25,17},{2,10},{10... | collective-permute-start | bytes 9437192 | tf_op jit(solution)/shard_map/ppermute | solution.py:489
  3.1 17.3 %collective-permute-start.5 = (bf16[256,1024]{1,0:T(8,128)(2,1)S(1)}, bf16[256,1024]{1,0:T(8,128)(2,1)}, u32[]{:S(2)}, u32[]{:S(2)}) collective-permute-start(bf16[256,1024]{1,0:T(8,128)(2,1)S(1)} %join.1.refs_0_), channel_id=1, source_target_pairs={{0,2},{1,3},{2,4},{3,5},{4,6},{5,7},{6,0},{7,1},{8,10},{9,11},{10,... | collective-permute-start | bytes 1572872 | tf_op jit(solution)/shard_map/ppermute | solution.py:489
  20.5 16.9 %collective-permute-start.23 = (bf16[256,1024]{1,0:T(8,128)(2,1)}, bf16[256,1024]{1,0:T(8,128)(2,1)}, u32[]{:S(2)}, u32[]{:S(2)}) collective-permute-start(bf16[256,1024]{1,0:T(8,128)(2,1)} %collective-permute-done.5.refs_0_.refs_3_), channel_id=1, source_target_pairs={{0,2},{1,3},{2,4},{3,5},{4,6},{5,7},{6,0},{7,1},{8,10},{9,11},{10,... | collective-permute-start | bytes 1572872 | tf_op jit(solution)/shard_map/ppermute | solution.py:489
  20.5 25.1 %collective-permute-start.10 = (bf16[256,1024]{1,0:T(8,128)(2,1)S(1)}, bf16[256,1024]{1,0:T(8,128)(2,1)}, u32[]{:S(2)}, u32[]{:S(2)}) collective-permute-start(bf16[256,1024]{1,0:T(8,128)(2,1)S(1)} %join.1.refs_0_), channel_id=1, source_target_pairs={{0,6},{1,7},{2,0},{3,1},{4,2},{5,3},{6,4},{7,5},{8,14},{9,15},{10,... | collective-permute-start | bytes 1572872 | tf_op jit(solution)/shard_map/ppermute | solution.py:489
  24.3 22.6 %collective-permute-start.1 = (bf16[256,1024]{1,0:T(8,128)(2,1)S(1)}, bf16[256,1024]{1,0:T(8,128)(2,1)}, u32[]{:S(2)}, u32[]{:S(2)}) collective-permute-start(bf16[256,1024]{1,0:T(8,128)(2,1)S(1)} %join.1.refs_0_), channel_id=1, source_target_pairs={{0,16},{8,24},{16,0},{24,8},{1,17},{9,25},{17,1},{25,9},{2,18},{10... | collective-permute-start | bytes 1572872 | tf_op jit(solution)/shard_map/ppermute | solution.py:489
  25.8 23.2 %collective-permute-start = (bf16[256,1024]{1,0:T(8,128)(2,1)S(1)}, bf16[256,1024]{1,0:T(8,128)(2,1)S(1)}, u32[]{:S(2)}, u32[]{:S(2)}) collective-permute-start(bf16[256,1024]{1,0:T(8,128)(2,1)S(1)} %join.1.refs_0_), channel_id=1, source_target_pairs={{0,1},{1,0},{2,3},{3,2},{4,5},{5,4},{6,7},{7,6},{8,9},{9,8},{10,11... | collective-permute-start | bytes 1572872 | tf_op jit(solution)/shard_map/ppermute | solution.py:489
  37.4 14.0 %collective-permute-start.24 = (bf16[256,1024]{1,0:T(8,128)(2,1)}, bf16[256,1024]{1,0:T(8,128)(2,1)}, u32[]{:S(2)}, u32[]{:S(2)}) collective-permute-start(bf16[256,1024]{1,0:T(8,128)(2,1)} %collective-permute-done.23.refs_0_.refs_2_), channel_id=1, source_target_pairs={{0,1},{1,0},{2,3},{3,2},{4,5},{5,4},{6,7},{7,6},{8,9},{9,8},{10,11... | collective-permute-start | bytes 1572872 | tf_op jit(solution)/shard_map/ppermute | solution.py:489
  45.6 15.1 %collective-permute-start.7 = (bf16[256,1024]{1,0:T(8,128)(2,1)}, bf16[256,1024]{1,0:T(8,128)(2,1)}, u32[]{:S(2)}, u32[]{:S(2)}) collective-permute-start(bf16[256,1024]{1,0:T(8,128)(2,1)} %collective-permute-done.5.refs_0_.refs_3_), channel_id=1, source_target_pairs={{0,16},{8,24},{16,0},{24,8},{1,17},{9,25},{17,1},{25,9},{2,18},{10... | collective-permute-start | bytes 1572872 | tf_op jit(solution)/shard_map/ppermute | solution.py:489
  46.9 15.5 %collective-permute-start.2 = (bf16[256,1024]{1,0:T(8,128)(2,1)}, bf16[256,1024]{1,0:T(8,128)(2,1)}, u32[]{:S(2)}, u32[]{:S(2)}) collective-permute-start(bf16[256,1024]{1,0:T(8,128)(2,1)} %collective-permute-done.1.refs_2_), channel_id=1, source_target_pairs={{0,1},{1,0},{2,3},{3,2},{4,5},{5,4},{6,7},{7,6},{8,9},{9,8},{10,11... | collective-permute-start | bytes 1572872 | tf_op jit(solution)/shard_map/ppermute | solution.py:489
  49.9 31.8 %collective-permute-start.25 = (bf16[256,1024]{1,0:T(8,128)(2,1)}, bf16[256,1024]{1,0:T(8,128)(2,1)}, u32[]{:S(2)}, u32[]{:S(2)}) collective-permute-start(bf16[256,1024]{1,0:T(8,128)(2,1)} %collective-permute-done.23.refs_0_.refs_2_), channel_id=1, source_target_pairs={{0,16},{8,24},{16,0},{24,8},{1,17},{9,25},{17,1},{25,9},{2,18},{10... | collective-permute-start | bytes 1572872 | tf_op jit(solution)/shard_map/ppermute | solution.py:489
  51.3 31.4 %collective-permute-start.26 = (bf16[256,1024]{1,0:T(8,128)(2,1)}, bf16[256,1024]{1,0:T(8,128)(2,1)}, u32[]{:S(2)}, u32[]{:S(2)}) collective-permute-start(bf16[256,1024]{1,0:T(8,128)(2,1)} %collective-permute-done.24.refs_1_.refs_0_), channel_id=1, source_target_pairs={{0,16},{8,24},{16,0},{24,8},{1,17},{9,25},{17,1},{25,9},{2,18},{10... | collective-permute-start | bytes 1572872 | tf_op jit(solution)/shard_map/ppermute | solution.py:489
  53.5 27.9 %all-to-all-start = ((bf16[32,2,128]{2,1,0:T(2,128)(2,1)}), bf16[32,2,128]{2,1,0:T(2,128)(2,1)S(1)}, u32[]{:S(2)}, u32[]{:S(2)}) async-start(bf16[32,2,128]{2,1,0:T(2,128)(2,1)} %copy.47), calls=%async_computation | async-start | bytes 32768 | tf_op jit(solution)/shard_map/all_to_all | solution.py:511
  60.7 43.7 %collective-permute-start.6 = (bf16[256,1024]{1,0:T(8,128)(2,1)}, bf16[256,1024]{1,0:T(8,128)(2,1)}, u32[]{:S(2)}, u32[]{:S(2)}) collective-permute-start(bf16[256,1024]{1,0:T(8,128)(2,1)} %collective-permute-done.5.refs_0_.refs_3_), channel_id=1, source_target_pairs={{0,1},{1,0},{2,3},{3,2},{4,5},{5,4},{6,7},{7,6},{8,9},{9,8},{10,11... | collective-permute-start | bytes 1572872 | tf_op jit(solution)/shard_map/ppermute | solution.py:489
  62.4 42.0 %collective-permute-start.8 = (bf16[256,1024]{1,0:T(8,128)(2,1)}, bf16[256,1024]{1,0:T(8,128)(2,1)}, u32[]{:S(2)}, u32[]{:S(2)}) collective-permute-start(bf16[256,1024]{1,0:T(8,128)(2,1)} %collective-permute-done.2.refs_3_.refs_0_), channel_id=1, source_target_pairs={{0,2},{1,3},{2,4},{3,5},{4,6},{5,7},{6,0},{7,1},{8,10},{9,11},{10,... | collective-permute-start | bytes 1572872 | tf_op jit(solution)/shard_map/ppermute | solution.py:489
  81.6 31.3 %collective-permute-start.12 = (bf16[256,1024]{1,0:T(8,128)(2,1)}, bf16[256,1024]{1,0:T(8,128)(2,1)S(1)}, u32[]{:S(2)}, u32[]{:S(2)}) collective-permute-start(bf16[256,1024]{1,0:T(8,128)(2,1)} %collective-permute-done.10.refs_0_.refs_1_), channel_id=1, source_target_pairs={{0,16},{8,24},{16,0},{24,8},{1,17},{9,25},{17,1},{25,9},{2,18},{10... | collective-permute-start | bytes 1572872 | tf_op jit(solution)/shard_map/ppermute | solution.py:489
  82.8 30.1 %collective-permute-start.11 = (bf16[256,1024]{1,0:T(8,128)(2,1)}, bf16[256,1024]{1,0:T(8,128)(2,1)S(1)}, u32[]{:S(2)}, u32[]{:S(2)}) collective-permute-start(bf16[256,1024]{1,0:T(8,128)(2,1)} %collective-permute-done.10.refs_0_.refs_1_), channel_id=1, source_target_pairs={{0,1},{1,0},{2,3},{3,2},{4,5},{5,4},{6,7},{7,6},{8,9},{9,8},{10,11... | collective-permute-start | bytes 1572872 | tf_op jit(solution)/shard_map/ppermute | solution.py:489
  84.3 28.6 %collective-permute-start.13 = (bf16[256,1024]{1,0:T(8,128)(2,1)}, bf16[256,1024]{1,0:T(8,128)(2,1)S(1)}, u32[]{:S(2)}, u32[]{:S(2)}) collective-permute-start(bf16[256,1024]{1,0:T(8,128)(2,1)} %collective-permute-done.2.refs_3_.refs_0_), channel_id=1, source_target_pairs={{0,6},{1,7},{2,0},{3,1},{4,2},{5,3},{6,4},{7,5},{8,14},{9,15},{10,... | collective-permute-start | bytes 1572872 | tf_op jit(solution)/shard_map/ppermute | solution.py:489
  129.3 82.5 %collective-permute-start.31 = (bf16[3,1024,512]{2,1,0:T(8,128)(2,1)}, bf16[3,1024,512]{2,1,0:T(8,128)(2,1)}, u32[]{:S(2)}, u32[]{:S(2)}) collective-permute-start(bf16[3,1024,512]{2,1,0:T(8,128)(2,1)} %get-tuple-element.88), channel_id=1, source_target_pairs={{0,8},{8,0},{16,24},{24,16},{1,9},{9,1},{17,25},{25,17},{2,10},{10... | collective-permute-start | bytes 9437192 | tf_op jit(solution)/shard_map/ppermute | solution.py:489
  149.8 40.2 %collective-permute-start.32 = (f32[3,256,512]{2,1,0:T(8,128)S(1)}, f32[3,256,512]{2,1,0:T(8,128)S(1)}, u32[]{:S(2)}, u32[]{:S(2)}) collective-permute-start(f32[3,256,512]{2,1,0:T(8,128)S(1)} %get-tuple-element.91), channel_id=1, source_target_pairs={{0,8},{8,0},{16,24},{24,16},{1,9},{9,1},{17,25},{25,17},{2,10},{10... | collective-permute-start | bytes 4718600 | tf_op jit(solution)/shard_map/ppermute | solution.py:489
  149.9 15.0 %collective-permute-start.9 = (bf16[136,1024]{1,0:T(8,128)(2,1)S(1)}, bf16[136,1024]{1,0:T(8,128)(2,1)S(1)}, u32[]{:S(2)}, u32[]{:S(2)}) collective-permute-start(bf16[136,1024]{1,0:T(8,128)(2,1)S(1)} %copy-done.48), channel_id=1, source_target_pairs={{0,6},{1,7},{2,0},{3,1},{4,2},{5,3},{6,4},{7,5},{8,14},{9,15},{10,... | collective-permute-start | bytes 835592 | tf_op jit(solution)/shard_map/ppermute | solution.py:489
  151.6 14.5 %collective-permute-start.14 = (bf16[136,1024]{1,0:T(8,128)(2,1)S(1)}, bf16[136,1024]{1,0:T(8,128)(2,1)S(1)}, u32[]{:S(2)}, u32[]{:S(2)}) collective-permute-start(bf16[136,1024]{1,0:T(8,128)(2,1)S(1)} %copy-done.50), channel_id=1, source_target_pairs={{0,2},{1,3},{2,4},{3,5},{4,6},{5,7},{6,0},{7,1},{8,10},{9,11},{10,... | collective-permute-start | bytes 835592 | tf_op jit(solution)/shard_map/ppermute | solution.py:489
  152.0 15.7 %collective-permute-start.27 = (bf16[136,1024]{1,0:T(8,128)(2,1)S(1)}, bf16[136,1024]{1,0:T(8,128)(2,1)S(1)}, u32[]{:S(2)}, u32[]{:S(2)}) collective-permute-start(bf16[136,1024]{1,0:T(8,128)(2,1)S(1)} %copy-done.42), channel_id=1, source_target_pairs={{0,16},{8,24},{16,0},{24,8},{1,17},{9,25},{17,1},{25,9},{2,18},{10... | collective-permute-start | bytes 835592 | tf_op jit(solution)/shard_map/ppermute | solution.py:489
  182.2 13.7 %collective-permute-start.19 = (bf16[136,1024]{1,0:T(8,128)(2,1)}, bf16[136,1024]{1,0:T(8,128)(2,1)}, u32[]{:S(2)}, u32[]{:S(2)}) collective-permute-start(bf16[136,1024]{1,0:T(8,128)(2,1)} %add_convert_fusion.3), channel_id=1, source_target_pairs={{0,6},{1,7},{2,0},{3,1},{4,2},{5,3},{6,4},{7,5},{8,14},{9,15},{10,... | collective-permute-start | bytes 835592 | tf_op jit(solution)/shard_map/ppermute | solution.py:489
  191.3 14.4 %collective-permute-start.30 = (bf16[136,1024]{1,0:T(8,128)(2,1)}, bf16[136,1024]{1,0:T(8,128)(2,1)}, u32[]{:S(2)}, u32[]{:S(2)}) collective-permute-start(bf16[136,1024]{1,0:T(8,128)(2,1)} %add_convert_fusion), channel_id=1, source_target_pairs={{0,4},{1,5},{2,6},{3,7},{4,0},{5,1},{6,2},{7,3},{8,12},{9,13},{10,... | collective-permute-start | bytes 835592 | tf_op jit(solution)/shard_map/ppermute | solution.py:489
  (66 other events, 564.6 us)

commit v3 on v2

--- a/solution.py
+++ b/solution.py
@@ -181,12 +181,12 @@
     return lax.dot_general(left, right, (dims, ((), ())), preferred_element_type=jnp.float32)
 
 
-def route_kernel(s, n, cap, at_ref, gates_ref, *refs):
+def route_kernel(group, n, cap, at_ref, gates_ref, *refs):
     pieces, w_refs = refs[:n], refs[n : n + 2]
     parts = refs[n + 2 : 2 * n + 2]
     xs, sy, gg, gu, hb, onehot, yslot, ig = refs[2 * n + 2 :]
     rows, width = gates_ref.shape[3], pieces[0].shape[1]
-    gates = gates_ref[s]
+    gates = jnp.concatenate([gates_ref[s] for s in group], axis=0)
     named = jnp.where(gates > 0, 1.0, 0.0)
     before = dot32(named.reshape(2 * n, rows).astype(jnp.bfloat16), strict_upper(rows))
     before = before.reshape(n, 2, rows)
@@ -250,17 +250,17 @@
 IN_VMEM = pl.BlockSpec(memory_space=pltpu.VMEM)
 
 
-def route(s, cap, extra, at, gates, pieces, w_own, w_sib):
+def route(group, cap, extra, at, gates, pieces, w_own, w_sib):
     n, rows, width = len(pieces), gates.shape[3], pieces[0].shape[1]
     hidden_units = w_own.shape[2]
     slots = n * cap
     shape, scratch = jax.ShapeDtypeStruct, pltpu.VMEM
     bf = jnp.bfloat16
-    out_shape = [shape((rows + extra, width), jnp.float32)]
-    out_shape += [shape((rows + extra, width), bf)] * (n - 1)
+    kinds = [bf if p % 4 else jnp.float32 for p in range(n)]
+    out_shape = [shape((rows + extra, width), kind) for kind in kinds]
     out_shape += [shape((2, slots, width), bf)] * 2 + [shape((2, slots, hidden_units), bf)] * 3
     outs = pl.pallas_call(
-        functools.partial(route_kernel, s, n, cap),
+        functools.partial(route_kernel, group, n, cap),
         out_shape=out_shape,
         in_specs=[IN_SMEM] + [IN_VMEM] * (n + 3),
         out_specs=[IN_VMEM] * (n + 5),
@@ -274,7 +274,7 @@
             bytes_accessed=4 * w_own.size + 16 * slots * width,
             transcendentals=0,
         ),
-        compiler_params=pltpu.CompilerParams(vmem_limit_bytes=20 * MIB),
+        compiler_params=pltpu.CompilerParams(vmem_limit_bytes=14 * MIB),
         name="route",
     )(at, gates, *pieces, w_own, w_sib)
     return outs[:n], outs[n:]
@@ -293,7 +293,7 @@
     tile = min(256, hidden_units)
     chunk = 4 * rows
     for r in range(0, n * rows, chunk):
-        at = slice(r, r + chunk)
+        at = slice(r, min(r + chunk, n * rows))
         for f in range(0, hidden_units, tile):
             cols = slice(f, f + tile)
             pre_gate = dot32(x[at], w[0, :, cols])
@@ -313,7 +313,8 @@
             for out, block in zip(outs, (core, 1 - core)):
                 keep = pl.ds(pl.multiple_of(where_ref[0] * kept + block * half, half), half)
                 term = dot32(left[:, keep], right[...], ((0,), (0,)))
-                out[i] = term + total_in[i, pl.ds(pl.multiple_of(block * half, half), half)]
+                term = term + total_in[i, pl.ds(pl.multiple_of(block * half, half), half)]
+                out[i] = term.astype(out.dtype)
         else:
             keep = pl.ds(pl.multiple_of(where_ref[0] * kept, kept), kept)
             term = dot32(left[:, keep], right[...], ((0,), (0,)))
@@ -328,7 +329,7 @@
     bf, f32 = jnp.bfloat16, jnp.float32
     out_shape = [shape((rows, width), f32)] if first else []
     if last:
-        out_shape += [shape((3, kept // 2, hidden_units), f32)] * 2
+        out_shape += [shape((3, kept // 2, hidden_units), dtype) for dtype in (f32, bf)]
     else:
         out_shape += [shape((3, kept, hidden_units), f32)]
     args = list(pieces) + [w] + ([] if first else [total])
@@ -344,7 +345,7 @@
             bytes_accessed=2 * w.size + n * rows * width * 4,
             transcendentals=0,
         ),
-        compiler_params=pltpu.CompilerParams(vmem_limit_bytes=24 * MIB),
+        compiler_params=pltpu.CompilerParams(vmem_limit_bytes=14 * MIB),
         name="common",
     )(where_at, *args)
 
@@ -383,33 +384,78 @@
             bytes_accessed=slots * (8 * width + 12 * hidden_units),
             transcendentals=0,
         ),
-        compiler_params=pltpu.CompilerParams(vmem_limit_bytes=32 * MIB),
+        compiler_params=pltpu.CompilerParams(vmem_limit_bytes=18 * MIB),
         name="weights",
     )(*flat)
 
 
-def add_kernel(left, right, out):
-    total = left[...].astype(jnp.float32) + right[...].astype(jnp.float32)
-    out[...] = total.astype(out.dtype)
-
-
-def add(left, right, dtype):
-    block = pl.BlockSpec((1,) + left.shape[1:], lambda i: (i, 0, 0))
+def sums_kernel(e_mine, s_mine, e_came, s_came, e_out, s_out, *scratch):
+    e_in, s_in, e_res, s_res, sem_in, sem_out = scratch
+    count = e_mine.shape[0]
+    parts = [(e_mine, e_came, e_in, e_res, e_out, i, i) for i in range(count)]
+    parts += [(s_mine, s_came, s_in, s_res, s_out, i, count + i) for i in range(count)]
+    bring = [
+        pltpu.make_async_copy(came.at[i], into.at[i], sem_in.at[k])
+        for _, came, into, _, _, i, k in parts
+    ]
+    for copy in bring:
+        copy.start()
+    sends = []
+    for (mine, _, into, res, out, i, k), copy in zip(parts, bring):
+        copy.wait()
+        res[i] = (mine[i].astype(jnp.float32) + into[i].astype(jnp.float32)).astype(res.dtype)
+        sends.append(pltpu.make_async_copy(res.at[i], out.at[i], sem_out.at[k]))
+        sends[-1].start()
+    for copy in sends:
+        copy.wait()
+
+
+def last_sums(e_mine, s_mine, e_came, s_came):
+    shape, scratch, dma = jax.ShapeDtypeStruct, pltpu.VMEM, pltpu.SemaphoreType.DMA
+    bf, f32 = jnp.bfloat16, jnp.float32
+    count = e_mine.shape[0]
+    in_place = pl.BlockSpec(memory_space=pl.ANY)
     return pl.pallas_call(
-        add_kernel,
-        grid=(left.shape[0],),
-        out_shape=jax.ShapeDtypeStruct(left.shape, dtype),
-        in_specs=[block] * 2,
-        out_specs=block,
-        compiler_params=pltpu.CompilerParams(vmem_limit_bytes=12 * MIB),
-        name="add",
-    )(left, right)
-
-
-def join_kernel(left, right, out):
+        sums_kernel,
+        out_shape=[shape(e_mine.shape, bf), shape(s_mine.shape, f32)],
+        in_specs=[IN_VMEM] * 2 + [in_place] * 2,
+        out_specs=[in_place] * 2,
+        scratch_shapes=[scratch(e_came.shape, bf), scratch(s_came.shape, bf)]
+        + [scratch(e_mine.shape, bf), scratch(s_mine.shape, f32)]
+        + [dma((2 * count,)), dma((2 * count,))],
+        compiler_params=pltpu.CompilerParams(vmem_limit_bytes=16 * MIB),
+        name="sums",
+    )(e_mine, s_mine, e_came, s_came)
+
+
+def hold_kernel(array, out, sem):
+    copy = pltpu.make_async_copy(array, out, sem.at[0])
+    copy.start()
+    copy.wait()
+
+
+def hold(array):
+    return pl.pallas_call(
+        hold_kernel,
+        out_shape=jax.ShapeDtypeStruct(array.shape, array.dtype),
+        in_specs=[pl.BlockSpec(memory_space=pltpu.HBM)],
+        out_specs=IN_VMEM,
+        scratch_shapes=[pltpu.SemaphoreType.DMA((1,))],
+        compiler_params=pltpu.CompilerParams(vmem_limit_bytes=4 * MIB),
+        name="hold",
+    )(array)
+
+
+def join_kernel(left, right, out, sem):
     rows = left.shape[0]
-    out[:rows] = left[...]
-    out[rows:] = right[...]
+    copies = [
+        pltpu.make_async_copy(left, out.at[pl.ds(0, rows)], sem.at[0]),
+        pltpu.make_async_copy(right, out.at[pl.ds(rows, rows)], sem.at[1]),
+    ]
+    for copy in copies:
+        copy.start()
+    for copy in copies:
+        copy.wait()
 
 
 def join(left, right):
@@ -417,48 +463,52 @@
     return pl.pallas_call(
         join_kernel,
         out_shape=jax.ShapeDtypeStruct((2 * rows, width), left.dtype),
-        in_specs=[IN_VMEM] * 2,
+        in_specs=[pl.BlockSpec(memory_space=pltpu.HBM)] * 2,
         out_specs=IN_VMEM,
-        compiler_params=pltpu.CompilerParams(vmem_limit_bytes=4 * MIB),
+        scratch_shapes=[pltpu.SemaphoreType.DMA((2,))],
+        compiler_params=pltpu.CompilerParams(vmem_limit_bytes=60 * MIB),
         name="join",
     )(left, right)
 
 
 def finish_kernel(terms, ids_ref, *refs):
     sums, own_grad, (tokens_out, gates_out) = refs[:terms], refs[terms], refs[terms + 1 :]
-    rows, top_count = ids_ref.shape
+    top_count, rows = ids_ref.shape
     total = sums[0][...].astype(jnp.float32)
     for ref in sums[1:]:
         total = total + ref[...].astype(jnp.float32)
     tokens_out[...] = (total[:rows] + own_grad[...]).astype(tokens_out.dtype)
     blocks = total.shape[1] // rows
-    lines = [
-        total[r : r + 1, b * rows : (b + 1) * rows]
-        for r in range(rows, total.shape[0])
-        for b in range(blocks)
-    ]
-    by_expert = jnp.concatenate(lines, axis=0).T
-    expert = lax.broadcasted_iota(jnp.int32, by_expert.shape, 1)
+    by_expert = jnp.concatenate(
+        [
+            total[r : r + 1, b * rows : (b + 1) * rows]
+            for r in range(rows, total.shape[0])
+            for b in range(blocks)
+        ],
+        axis=0,
+    )
+    expert = lax.broadcasted_iota(jnp.int32, by_expert.shape, 0)
     picked = [
-        jnp.sum(jnp.where(ids_ref[:, k : k + 1] == expert, by_expert, 0.0), axis=1, keepdims=True)
+        jnp.sum(jnp.where(ids_ref[k : k + 1] == expert, by_expert, 0.0), axis=0, keepdims=True)
         for k in range(top_count)
     ]
-    gates_out[...] = jnp.concatenate(picked, axis=1).astype(gates_out.dtype)
+    gates_out[...] = jnp.concatenate(picked, axis=0).astype(gates_out.dtype)
 
 
 def finish(expert_ids, sums, own_grad):
     rows, top_count = expert_ids.shape
-    return pl.pallas_call(
+    tokens, gates = pl.pallas_call(
         functools.partial(finish_kernel, len(sums)),
         out_shape=[
             jax.ShapeDtypeStruct(own_grad.shape, jnp.bfloat16),
-            jax.ShapeDtypeStruct((rows, top_count), jnp.bfloat16),
+            jax.ShapeDtypeStruct((top_count, rows), jnp.bfloat16),
         ],
         in_specs=[IN_VMEM] * (len(sums) + 2),
         out_specs=[IN_VMEM] * 2,
         compiler_params=pltpu.CompilerParams(vmem_limit_bytes=8 * MIB),
         name="finish",
-    )(expert_ids, *sums, own_grad)
+    )(expert_ids.T, *sums, own_grad)
+    return tokens, gates.T
 
 
 def shared_rows(tokens, cotangent, expert_ids, gate_weights, expert_weights, shared_weights):
@@ -480,7 +530,6 @@
         "x": ("expert", [(e, e ^ 1) for e in range(expert_count)]),
         "+": ("expert", [(e, (e + 2) % expert_count) for e in range(expert_count)]),
         "-": ("expert", [(e, (e - 2) % expert_count) for e in range(expert_count)]),
-        "--": ("expert", [(e, (e - 4) % expert_count) for e in range(expert_count)]),
         "y": ("dp", [(d, d ^ 2) for d in range(data_count)]),
         "core": ("dp", [(d, d ^ 1) for d in range(data_count)]),
     }
@@ -491,6 +540,7 @@
     w_own = expert_weights[0]
     own = join(tokens, cotangent)
     w_sib = send("core", w_own)
+    w_sib = hold(w_sib)
 
     c, x, y, d = [own] + [None] * 3, [None] * 4, [None] * 4, [None] * 4
     c[1] = send("+", c[0])
@@ -502,7 +552,7 @@
     d[0] = send("x", y[0])
     d[1] = send("+", d[0])
     d[2] = send("y", x[2])
-    d[3] = send("-", d[0])
+    d[3] = send("x", y[3])
 
     matches = expert_ids[:, :, None] == jnp.arange(devices, dtype=jnp.int32)
     by_expert = jnp.sum(jnp.where(matches, gate_weights[:, :, None].astype(f32), 0.0), axis=1)
@@ -526,18 +576,26 @@
     sibling = (me_dp ^ 1) * expert_count + me_ex
     at = jnp.stack([me // blocks, me % blocks, sibling // blocks, sibling % blocks])
     at = at.astype(jnp.int32)
-    part, saved = [None] * 4, [None] * 4
-    for s in (0, 2, 1, 3):
-        part[s], saved[s] = route(s, cap, extra, at, gates, (c[s], x[s], y[s], d[s]), w_own, w_sib)
+    part, saved = [None] * 4, []
+    for group in ((0,), (2,), (1, 3)):
+        pieces = [piece for s in group for piece in (c[s], x[s], y[s], d[s])]
+        sums, keep = route(group, cap, extra, at, gates, pieces, w_own, w_sib)
+        saved.append(keep)
+        for i, s in enumerate(group):
+            part[s] = sums[4 * i : 4 * i + 4]
     pc, px, py, pd = zip(*part)
 
     where_at = jnp.stack([me_dp // 2, me_dp % 2]).astype(jnp.int32)
     kept = 2 * (width // data_count)
     pieces = (c[0], x[0], y[0], c[1])
     shared_grad, total = common(where_at, kept, pieces, shared_weights, None)
-    pieces = (d[0], y[1], c[2], y[2])
+    pieces = (d[0], y[1], x[1], c[2])
     (total,) = common(where_at, kept, pieces, shared_weights, total)
-    pieces = (x[2], c[3], x[1], d[1], d[2], x[3], y[3], d[3])
+    pieces = (c[3], x[2], y[2])
+    (total,) = common(where_at, kept, pieces, shared_weights, total)
+    pieces = (d[1], x[3], y[3])
+    (total,) = common(where_at, kept, pieces, shared_weights, total)
+    pieces = (d[2], d[3])
     mine, other = common(where_at, kept, pieces, shared_weights, total, last=True)
 
     def plus(*terms):
@@ -552,22 +610,23 @@
     def home_y(array):
         return send("y", array.astype(bf))
 
-    x2 = plus(px[2], send("y", pd[2]))
-    c2 = plus(pc[2], home_x(x2), home_y(py[2]))
-    c1 = plus(pc[1], home_x(px[1]), home_y(py[1]))
-    c3 = plus(pc[3], home_x(px[3]), home_y(py[3]))
-    d0 = plus(pd[0], send("-", pd[1]), send("+", pd[3]))
-    y0 = plus(py[0], send("x", d0.astype(bf)))
-    sums = (pc[0], home_x(px[0]), home_y(y0))
-    sums += (send("-", c1.astype(bf)), send("+", c3.astype(bf)))
-    sums += (send("--", c2.astype(bf)),)
+    part_x, part_y = list(px), list(py)
+    for s in range(planes):
+        if s in (0, 3):
+            part_y[s] = plus(py[s], send("x", pd[s]))
+        else:
+            part_x[s] = plus(px[s], send("y", pd[s]))
+    arrived = [(pc[s], home_x(part_x[s]), home_y(part_y[s])) for s in range(planes)]
+    c3 = arrived[3] + (send("+", plus(*arrived[2]).astype(bf)),)
+    sums = arrived[0] + (send("-", plus(*arrived[1]).astype(bf)),)
+    sums += (send("+", plus(*c3).astype(bf)),)
     grad_tokens, grad_gates = finish(expert_ids, sums, shared_grad)
 
     mine_experts, for_sib = weights(saved)
     came = send("core", for_sib)
     came_shared = send("core", other)
-    grad_experts = add(mine_experts, came, bf)[None]
-    grad_shared = add(mine, came_shared, f32)
+    grad_experts, grad_shared = last_sums(mine_experts, mine, came, came_shared)
+    grad_experts = grad_experts[None]
     return (grad_tokens, grad_gates, grad_experts, grad_shared)
 
 

time: 217 us -> 201 us (0.926)
  local copies, waits for them, and re-layouts: 27.9 us -> 16.4 us
  starting transfers between devices: 37.5 us -> 43.6 us
  Pallas kernels: 54 us -> 50 us
  waiting for transfers between devices: 90.7 us -> 86.9 us
  other arithmetic: 5.05 us -> 2.21 us
    all_to_all x1, waiting for transfers between devices: 18.4 us -> 0.01 us  [shared_rows_body(): inward = lax.all_to_all(outward, ('dp', 'expert'), 0, 0, tiled=True)]
    ppermute x33, waiting for transfers between devices: 72.2 us -> 86.9 us  [send(): return lax.ppermute(array, *routes[way])]
    unnamed x114 -> x80, local copies, waits for them, and re-layouts: 27.1 us -> 15.5 us
    ppermute x33, starting transfers between devices: 34.6 us -> 40.7 us  [send(): return lax.ppermute(array, *routes[way])]
    pallas_call x6 -> x5, Pallas kernels: 27.7 us -> 22.2 us  [the longest x3 18.2 us: route(): pl.pallas_call(functools.partial(route_kernel, group, n, cap), out_shape=...]
    pallas_call x3 -> x5, Pallas kernels: 16.5 us -> 19.8 us  [common(): pl.pallas_call(functools.partial(common_kernel, n, first, last), out_shap...]
    pallas_call x1, Pallas kernels: 3.36 us -> 0.87 us  [finish(): pl.pallas_call(functools.partial(finish_kernel, len(sums)), out_shape=[ja...]
    convert_element_type x4 -> x3, other arithmetic: 2.64 us -> 0.36 us  [the longest x1 0.16 us: shared_rows_body(): sums += (send('+', plus(*c3).astype(bf)),)]
  transfers between devices with their start and end apart: 34 -> 34, of which waited for: 15 -> 16; matrix products, arithmetic and copies ran while one was open for 3% -> 2% of each run, Pallas kernels for 17% -> 16%
where the time goes in v3:
time: 201 us
  waiting for transfers between devices  86.9 us (43%)
  Pallas kernels  50 us (25%)
  starting transfers between devices  43.6 us (22%)
  local copies, waits for them, and re-layouts  16.4 us (8%)
  other arithmetic  2.21 us (1%)
    ppermute x33, waiting for transfers between devices, send(): return lax.ppermute(array, *routes[way])  86.9 us
    ppermute x33, starting transfers between devices, send(): return lax.ppermute(array, *routes[way])  40.7 us
    pallas_call x5, Pallas kernels, common(): pl.pallas_call(functools.partial(common_kernel, n, first, last), out_shap...  19.8 us
    pallas_call x3, Pallas kernels, route(): pl.pallas_call(functools.partial(route_kernel, group, n, cap), out_shape=...  18.2 us
    unnamed x80, local copies, waits for them, and re-layouts  15.5 us
    pallas_call x1, Pallas kernels, weights(): pl.pallas_call(functools.partial(weights_kernel, groups), out_shape=[jax....  5.28 us
  transfers between devices with their start and end apart: 34, of which 16 were waited for; matrix products, arithmetic and copies ran while one was open for 2% of the time, Pallas kernels for 16%

profile of v3, /device:TPU:0, one launch (start us, length us, event | category | flops | bytes accessed | tf_op | source)
XLA Modules:
  0.0 200.6 jit_solution(15449919898333489870)
XLA Ops:
  3.1 2.6 %collective-permute-start.7 = (bf16[256,1024]{1,0:T(8,128)(2,1)}, bf16[256,1024]{1,0:T(8,128)(2,1)}, u32[]{:S(2)}, u32[]{:S(2)}) collective-permute-start(bf16[256,1024]{1,0:T(8,128)(2,1)} %join.1.refs_0_), channel_id=1, source_target_pairs={{0,2},{1,3},{2,4},{3,5},{4,6},{5,7},{6,0},{7,1},{8,10},{9,11},{10,... | collective-permute-start | bytes 1572872 | tf_op jit(solution)/shard_map/ppermute | solution.py:538
  5.7 14.9 %collective-permute-done.7.refs_0_.refs_3_ = bf16[256,1024]{1,0:T(8,128)(2,1)} collective-permute-done((bf16[256,1024]{1,0:T(8,128)(2,1)}, bf16[256,1024]{1,0:T(8,128)(2,1)}, u32[]{:S(2)}, u32[]{:S(2)}) %collective-permute-start.7) | collective-permute-done | bytes 524320 | tf_op jit(solution)/shard_map/ppermute | solution.py:538
  20.6 3.8 %collective-permute-start.11 = (bf16[256,1024]{1,0:T(8,128)(2,1)}, bf16[256,1024]{1,0:T(8,128)(2,1)}, u32[]{:S(2)}, u32[]{:S(2)}) collective-permute-start(bf16[256,1024]{1,0:T(8,128)(2,1)} %join.1.refs_0_), channel_id=1, source_target_pairs={{0,6},{1,7},{2,0},{3,1},{4,2},{5,3},{6,4},{7,5},{8,14},{9,15},{10,... | collective-permute-start | bytes 1572872 | tf_op jit(solution)/shard_map/ppermute | solution.py:538
  27.5 10.1 %collective-permute-done.22.refs_0_.refs_3_ = bf16[256,1024]{1,0:T(8,128)(2,1)} collective-permute-done((bf16[256,1024]{1,0:T(8,128)(2,1)}, bf16[256,1024]{1,0:T(8,128)(2,1)}, u32[]{:S(2)}, u32[]{:S(2)}) %collective-permute-start.22) | collective-permute-done | bytes 524320 | tf_op jit(solution)/shard_map/ppermute | solution.py:538
  39.1 6.9 %collective-permute-done.11.refs_4_.refs_0_ = bf16[256,1024]{1,0:T(8,128)(2,1)} collective-permute-done((bf16[256,1024]{1,0:T(8,128)(2,1)}, bf16[256,1024]{1,0:T(8,128)(2,1)}, u32[]{:S(2)}, u32[]{:S(2)}) %collective-permute-start.11) | collective-permute-done | bytes 524320 | tf_op jit(solution)/shard_map/ppermute | solution.py:538
  54.3 2.8 %all-to-all-start = ((bf16[32,2,128]{2,1,0:T(2,128)(2,1)}), bf16[32,2,128]{2,1,0:T(2,128)(2,1)S(1)}, u32[]{:S(2)}, u32[]{:S(2)}) async-start(bf16[32,2,128]{2,1,0:T(2,128)(2,1)} %copy.35), calls=%async_computation | async-start | bytes 32768 | tf_op jit(solution)/shard_map/all_to_all | solution.py:561
  57.5 3.6 %collective-permute-done.13.refs_6_.refs_2_ = bf16[256,1024]{1,0:T(8,128)(2,1)} collective-permute-done((bf16[256,1024]{1,0:T(8,128)(2,1)}, bf16[256,1024]{1,0:T(8,128)(2,1)}, u32[]{:S(2)}, u32[]{:S(2)}) %collective-permute-start.13) | collective-permute-done | bytes 524320 | tf_op jit(solution)/shard_map/ppermute | solution.py:538
  63.9 8.5 %collective-permute-done.24.refs_2_ = bf16[256,1024]{1,0:T(8,128)(2,1)} collective-permute-done((bf16[256,1024]{1,0:T(8,128)(2,1)}, bf16[256,1024]{1,0:T(8,128)(2,1)}, u32[]{:S(2)}, u32[]{:S(2)}) %collective-permute-start.24) | collective-permute-done | bytes 524320 | tf_op jit(solution)/shard_map/ppermute | solution.py:538
  73.7 10.0 %collective-permute-done.25.refs_3_.refs_0_ = bf16[256,1024]{1,0:T(8,128)(2,1)} collective-permute-done((bf16[256,1024]{1,0:T(8,128)(2,1)}, bf16[256,1024]{1,0:T(8,128)(2,1)}, u32[]{:S(2)}, u32[]{:S(2)}) %collective-permute-start.25) | collective-permute-done | bytes 524320 | tf_op jit(solution)/shard_map/ppermute | solution.py:538
  88.3 4.9 %route.3 = (f32[136,1024]{1,0:T(8,128)S(1)}, bf16[136,1024]{1,0:T(8,128)(2,1)S(1)}, bf16[136,1024]{1,0:T(8,128)(2,1)S(1)}, bf16[136,1024]{1,0:T(8,128)(2,1)S(1)}...) custom-call(s32[4]{0:T(128)S(1)} %pad_add_fusion.at_ref, ...), custom_call_target="tpu_custom_call" | custom-call | flops 2013265920 | bytes 9437184 | tf_op jit(solution)/shard_map/route/pallas_call | solution.py:262
  95.4 5.2 %route.5 = (f32[136,1024]{1,0:T(8,128)S(1)}, bf16[136,1024]{1,0:T(8,128)(2,1)S(1)}, bf16[136,1024]{1,0:T(8,128)(2,1)S(1)}, bf16[136,1024]{1,0:T(8,128)(2,1)S(1)}...) custom-call(s32[4]{0:T(128)S(1)} %pad_add_fusion.at_ref, ...), custom_call_target="tpu_custom_call" | custom-call | flops 2013265920 | bytes 9437184 | tf_op jit(solution)/shard_map/route/pallas_call | solution.py:262
  103.6 8.1 %route.4 = (f32[136,1024]{1,0:T(8,128)S(1)}, bf16[136,1024]{1,0:T(8,128)(2,1)S(1)}, bf16[136,1024]{1,0:T(8,128)(2,1)S(1)}, bf16[136,1024]{1,0:T(8,128)(2,1)S(1)}...) custom-call(s32[4]{0:T(128)S(1)} %pad_add_fusion.at_ref, ...), custom_call_target="tpu_custom_call" | custom-call | flops 4026531840 | bytes 12582912 | tf_op jit(solution)/shard_map/route/pallas_call | solution.py:262
  115.6 5.3 %weights.1 = (bf16[3,1024,512]{2,1,0:T(8,128)(2,1)S(1)}, bf16[3,1024,512]{2,1,0:T(8,128)(2,1)}) custom-call(bf16[2,192,1024]{2,1,0:T(8,128)(2,1)S(1)} %get-tuple-element.64.refs_0_, bf16[2,192,1024]{2,1,0:T(8,128)(2,1)S(1)} %get-tuple-element.65.refs_1_, bf16[2,192,512]{2,1,0:T(8,128)(2,1)S(1)} %get-tuple-element.66.refs_2_, ...), custom_call_target="tpu_custom_call" | custom-call | flops 4831838208 | bytes 11010048 | tf_op jit(solution)/shard_map/weights/pallas_call | solution.py:373
  124.8 4.6 %common.5 = (f32[128,1024]{1,0:T(8,128)S(1)}, f32[3,512,512]{2,1,0:T(8,128)S(1)}) custom-call(s32[2]{0:T(128)S(1)} %pad_add_fusion.1.where_ref, bf16[256,1024]{1,0:T(8,128)(2,1)S(1)} %copy-done.5, bf16[256,1024]{1,0:T(8,128)(2,1)S(1)} %copy-done.16, bf16[256,1024]{1,0:T(8,128)(2,1)} %collective-permute-done.1.refs_2_, ...), custom_call_target="tpu_custom_call" | custom-call | flops 2415919104 | bytes 5242880 | tf_op jit(solution)/shard_map/common/pallas_call | solution.py:336
  129.4 4.3 %common.6.refs_4_ = f32[3,512,512]{2,1,0:T(8,128)S(1)} custom-call(s32[2]{0:T(128)S(1)} %pad_add_fusion.1.where_ref, bf16[256,1024]{1,0:T(8,128)(2,1)} %collective-permute-done.2.refs_3_.refs_0_, bf16[256,1024]{1,0:T(8,128)(2,1)} %collective-permute-done.9.refs_2_.refs_1_, bf16[256,1024]{1,0:T(8,128)(2,1)} %collective-permute-done.8.refs_1_.refs_2_, ...), custom_call_target="tpu_custom_call" | custom-call | flops 2415919104 | bytes 5242880 | tf_op jit(solution)/shard_map/common/pallas_call | solution.py:336
  133.7 3.8 %common.7.refs_4_ = f32[3,512,512]{2,1,0:T(8,128)S(1)} custom-call(s32[2]{0:T(128)S(1)} %pad_add_fusion.1.where_ref, bf16[256,1024]{1,0:T(8,128)(2,1)} %collective-permute-done.11.refs_4_.refs_0_, bf16[256,1024]{1,0:T(8,128)(2,1)} %collective-permute-done.23.refs_1_, bf16[256,1024]{1,0:T(8,128)(2,1)} %collective-permute-done.24.refs_2_, ...), custom_call_target="tpu_custom_call" | custom-call | flops 1811939328 | bytes 4718592 | tf_op jit(solution)/shard_map/common/pallas_call | solution.py:336
  139.2 4.0 %common.8.refs_3_ = f32[3,512,512]{2,1,0:T(8,128)S(1)} custom-call(s32[2]{0:T(128)S(1)} %pad_add_fusion.1.where_ref, bf16[256,1024]{1,0:T(8,128)(2,1)} %collective-permute-done.10.refs_3_.refs_0_, bf16[256,1024]{1,0:T(8,128)(2,1)} %collective-permute-done.12.refs_5_.refs_1_, bf16[256,1024]{1,0:T(8,128)(2,1)} %collective-permute-done.13.refs_6_.refs_2_, ...), custom_call_target="tpu_custom_call" | custom-call | flops 1811939328 | bytes 4718592 | tf_op jit(solution)/shard_map/common/pallas_call | solution.py:336
  143.8 3.1 %common.9 = (f32[3,256,512]{2,1,0:T(8,128)S(1)}, bf16[3,256,512]{2,1,0:T(8,128)(2,1)S(1)}) custom-call(s32[2]{0:T(128)S(1)} %pad_add_fusion.1.where_ref, bf16[256,1024]{1,0:T(8,128)(2,1)} %collective-permute-done.25.refs_3_.refs_0_, bf16[256,1024]{1,0:T(8,128)(2,1)} %collective-permute-done.14.refs_7_.refs_1_, bf16[3,1024,512]{2,1,0:T(8,128)(2,1)S(1)} %copy-done, ...), custom_call_target="tpu_custom_call" | custom-call | flops 1207959552 | bytes 4194304 | tf_op jit(solution)/shard_map/common/pallas_call | solution.py:336
  153.7 8.8 %collective-permute-done.20 = bf16[136,1024]{1,0:T(8,128)(2,1)S(1)} collective-permute-done((bf16[136,1024]{1,0:T(8,128)(2,1)S(1)}, bf16[136,1024]{1,0:T(8,128)(2,1)S(1)}, u32[]{:S(2)}, u32[]{:S(2)}) %collective-permute-start.20) | collective-permute-done | bytes 278560 | tf_op jit(solution)/shard_map/ppermute | solution.py:538
  164.6 3.9 %collective-permute-done.27 = bf16[136,1024]{1,0:T(8,128)(2,1)S(1)} collective-permute-done((bf16[136,1024]{1,0:T(8,128)(2,1)S(1)}, bf16[136,1024]{1,0:T(8,128)(2,1)S(1)}, u32[]{:S(2)}, u32[]{:S(2)}) %collective-permute-start.27) | collective-permute-done | bytes 278560 | tf_op jit(solution)/shard_map/ppermute | solution.py:538
  174.5 4.8 %collective-permute-done.16 = bf16[136,1024]{1,0:T(8,128)(2,1)S(1)} collective-permute-done((bf16[136,1024]{1,0:T(8,128)(2,1)S(1)}, bf16[136,1024]{1,0:T(8,128)(2,1)S(1)}, u32[]{:S(2)}, u32[]{:S(2)}) %collective-permute-start.16) | collective-permute-done | bytes 278560 | tf_op jit(solution)/shard_map/ppermute | solution.py:538
  181.5 2.9 %collective-permute-start.18 = (bf16[136,1024]{1,0:T(8,128)(2,1)S(1)}, bf16[136,1024]{1,0:T(8,128)(2,1)S(1)}, u32[]{:S(2)}, u32[]{:S(2)}) collective-permute-start(bf16[136,1024]{1,0:T(8,128)(2,1)S(1)} %add_convert_fusion.4), channel_id=1, source_target_pairs={{0,6},{1,7},{2,0},{3,1},{4,2},{5,3},{6,4},{7,5},{8,14},{9,15},{10,... | collective-permute-start | bytes 835592 | tf_op jit(solution)/shard_map/ppermute | solution.py:538
  190.9 4.9 %collective-permute-done.30.refs_4_ = bf16[136,1024]{1,0:T(8,128)(2,1)S(1)} collective-permute-done((bf16[136,1024]{1,0:T(8,128)(2,1)S(1)}, bf16[136,1024]{1,0:T(8,128)(2,1)S(1)}, u32[]{:S(2)}, u32[]{:S(2)}) %collective-permute-start.30) | collective-permute-done | bytes 278560 | tf_op jit(solution)/shard_map/ppermute | solution.py:538
  196.7 3.7 %sums.1 = (bf16[3,1024,512]{2,1,0:T(8,128)(2,1)}, f32[3,256,512]{2,1,0:T(8,128)}) custom-call(bf16[3,1024,512]{2,1,0:T(8,128)(2,1)S(1)} %copy-done.3, f32[3,256,512]{2,1,0:T(8,128)S(1)} %get-tuple-element.81.s_mine, bf16[3,1024,512]{2,1,0:T(8,128)(2,1)} %collective-permute-done.31.e_came, bf16[3,256,512]{2,1,0:T(8,128)(2,1)S(1)} %collective-permute-done.32.s_came), custom_call_target="tpu_custom_call" | custom-call | tf_op jit(solution)/shard_map/sums/pallas_call | solution.py:418
  (155 shorter events, 63.6 us)
Async XLA Ops:
  0.6 84.3 %collective-permute-start.3 = (bf16[3,1024,512]{2,1,0:T(8,128)(2,1)}, bf16[3,1024,512]{2,1,0:T(8,128)(2,1)S(1)}, u32[]{:S(2)}, u32[]{:S(2)}) collective-permute-start(bf16[3,1024,512]{2,1,0:T(8,128)(2,1)} %bitcast.54), channel_id=1, source_target_pairs={{0,8},{8,0},{16,24},{24,16},{1,9},{9,1},{17,25},{25,17},{2,10},{10... | collective-permute-start | bytes 9437192 | tf_op jit(solution)/shard_map/ppermute | solution.py:538
  3.1 17.6 %collective-permute-start.7 = (bf16[256,1024]{1,0:T(8,128)(2,1)}, bf16[256,1024]{1,0:T(8,128)(2,1)}, u32[]{:S(2)}, u32[]{:S(2)}) collective-permute-start(bf16[256,1024]{1,0:T(8,128)(2,1)} %join.1.refs_0_), channel_id=1, source_target_pairs={{0,2},{1,3},{2,4},{3,5},{4,6},{5,7},{6,0},{7,1},{8,10},{9,11},{10,... | collective-permute-start | bytes 1572872 | tf_op jit(solution)/shard_map/ppermute | solution.py:538
  20.6 16.9 %collective-permute-start.22 = (bf16[256,1024]{1,0:T(8,128)(2,1)}, bf16[256,1024]{1,0:T(8,128)(2,1)}, u32[]{:S(2)}, u32[]{:S(2)}) collective-permute-start(bf16[256,1024]{1,0:T(8,128)(2,1)} %collective-permute-done.7.refs_0_.refs_3_), channel_id=1, source_target_pairs={{0,2},{1,3},{2,4},{3,5},{4,6},{5,7},{6,0},{7,1},{8,10},{9,11},{10,... | collective-permute-start | bytes 1572872 | tf_op jit(solution)/shard_map/ppermute | solution.py:538
  20.6 25.3 %collective-permute-start.11 = (bf16[256,1024]{1,0:T(8,128)(2,1)}, bf16[256,1024]{1,0:T(8,128)(2,1)}, u32[]{:S(2)}, u32[]{:S(2)}) collective-permute-start(bf16[256,1024]{1,0:T(8,128)(2,1)} %join.1.refs_0_), channel_id=1, source_target_pairs={{0,6},{1,7},{2,0},{3,1},{4,2},{5,3},{6,4},{7,5},{8,14},{9,15},{10,... | collective-permute-start | bytes 1572872 | tf_op jit(solution)/shard_map/ppermute | solution.py:538
  24.5 22.8 %collective-permute-start.1 = (bf16[256,1024]{1,0:T(8,128)(2,1)}, bf16[256,1024]{1,0:T(8,128)(2,1)}, u32[]{:S(2)}, u32[]{:S(2)}) collective-permute-start(bf16[256,1024]{1,0:T(8,128)(2,1)} %join.1.refs_0_), channel_id=1, source_target_pairs={{0,16},{8,24},{16,0},{24,8},{1,17},{9,25},{17,1},{25,9},{2,18},{10... | collective-permute-start | bytes 1572872 | tf_op jit(solution)/shard_map/ppermute | solution.py:538
  26.0 22.8 %collective-permute-start = (bf16[256,1024]{1,0:T(8,128)(2,1)}, bf16[256,1024]{1,0:T(8,128)(2,1)S(1)}, u32[]{:S(2)}, u32[]{:S(2)}) collective-permute-start(bf16[256,1024]{1,0:T(8,128)(2,1)} %join.1.refs_0_), channel_id=1, source_target_pairs={{0,1},{1,0},{2,3},{3,2},{4,5},{5,4},{6,7},{7,6},{8,9},{9,8},{10,11... | collective-permute-start | bytes 1572872 | tf_op jit(solution)/shard_map/ppermute | solution.py:538
  37.6 14.2 %collective-permute-start.23 = (bf16[256,1024]{1,0:T(8,128)(2,1)}, bf16[256,1024]{1,0:T(8,128)(2,1)}, u32[]{:S(2)}, u32[]{:S(2)}) collective-permute-start(bf16[256,1024]{1,0:T(8,128)(2,1)} %collective-permute-done.22.refs_0_.refs_3_), channel_id=1, source_target_pairs={{0,1},{1,0},{2,3},{3,2},{4,5},{5,4},{6,7},{7,6},{8,9},{9,8},{10,11... | collective-permute-start | bytes 1572872 | tf_op jit(solution)/shard_map/ppermute | solution.py:538
  45.9 15.1 %collective-permute-start.13 = (bf16[256,1024]{1,0:T(8,128)(2,1)}, bf16[256,1024]{1,0:T(8,128)(2,1)}, u32[]{:S(2)}, u32[]{:S(2)}) collective-permute-start(bf16[256,1024]{1,0:T(8,128)(2,1)} %collective-permute-done.11.refs_4_.refs_0_), channel_id=1, source_target_pairs={{0,16},{8,24},{16,0},{24,8},{1,17},{9,25},{17,1},{25,9},{2,18},{10... | collective-permute-start | bytes 1572872 | tf_op jit(solution)/shard_map/ppermute | solution.py:538
  47.3 15.2 %collective-permute-start.2 = (bf16[256,1024]{1,0:T(8,128)(2,1)}, bf16[256,1024]{1,0:T(8,128)(2,1)}, u32[]{:S(2)}, u32[]{:S(2)}) collective-permute-start(bf16[256,1024]{1,0:T(8,128)(2,1)} %collective-permute-done.1.refs_2_), channel_id=1, source_target_pairs={{0,1},{1,0},{2,3},{3,2},{4,5},{5,4},{6,7},{7,6},{8,9},{9,8},{10,11... | collective-permute-start | bytes 1572872 | tf_op jit(solution)/shard_map/ppermute | solution.py:538
  49.6 22.9 %collective-permute-start.24 = (bf16[256,1024]{1,0:T(8,128)(2,1)}, bf16[256,1024]{1,0:T(8,128)(2,1)}, u32[]{:S(2)}, u32[]{:S(2)}) collective-permute-start(bf16[256,1024]{1,0:T(8,128)(2,1)} %collective-permute-done.22.refs_0_.refs_3_), channel_id=1, source_target_pairs={{0,16},{8,24},{16,0},{24,8},{1,17},{9,25},{17,1},{25,9},{2,18},{10... | collective-permute-start | bytes 1572872 | tf_op jit(solution)/shard_map/ppermute | solution.py:538
  51.7 31.9 %collective-permute-start.25 = (bf16[256,1024]{1,0:T(8,128)(2,1)}, bf16[256,1024]{1,0:T(8,128)(2,1)}, u32[]{:S(2)}, u32[]{:S(2)}) collective-permute-start(bf16[256,1024]{1,0:T(8,128)(2,1)} %collective-permute-done.23.refs_1_), channel_id=1, source_target_pairs={{0,16},{8,24},{16,0},{24,8},{1,17},{9,25},{17,1},{25,9},{2,18},{10... | collective-permute-start | bytes 1572872 | tf_op jit(solution)/shard_map/ppermute | solution.py:538
  54.3 31.6 %all-to-all-start = ((bf16[32,2,128]{2,1,0:T(2,128)(2,1)}), bf16[32,2,128]{2,1,0:T(2,128)(2,1)S(1)}, u32[]{:S(2)}, u32[]{:S(2)}) async-start(bf16[32,2,128]{2,1,0:T(2,128)(2,1)} %copy.35), calls=%async_computation | async-start | bytes 32768 | tf_op jit(solution)/shard_map/all_to_all | solution.py:561
  61.1 42.5 %collective-permute-start.12 = (bf16[256,1024]{1,0:T(8,128)(2,1)}, bf16[256,1024]{1,0:T(8,128)(2,1)}, u32[]{:S(2)}, u32[]{:S(2)}) collective-permute-start(bf16[256,1024]{1,0:T(8,128)(2,1)} %collective-permute-done.11.refs_4_.refs_0_), channel_id=1, source_target_pairs={{0,1},{1,0},{2,3},{3,2},{4,5},{5,4},{6,7},{7,6},{8,9},{9,8},{10,11... | collective-permute-start | bytes 1572872 | tf_op jit(solution)/shard_map/ppermute | solution.py:538
  62.4 41.1 %collective-permute-start.9 = (bf16[256,1024]{1,0:T(8,128)(2,1)}, bf16[256,1024]{1,0:T(8,128)(2,1)}, u32[]{:S(2)}, u32[]{:S(2)}) collective-permute-start(bf16[256,1024]{1,0:T(8,128)(2,1)} %collective-permute-done.7.refs_0_.refs_3_), channel_id=1, source_target_pairs={{0,16},{8,24},{16,0},{24,8},{1,17},{9,25},{17,1},{25,9},{2,18},{10... | collective-permute-start | bytes 1572872 | tf_op jit(solution)/shard_map/ppermute | solution.py:538
  72.4 31.1 %collective-permute-start.8 = (bf16[256,1024]{1,0:T(8,128)(2,1)}, bf16[256,1024]{1,0:T(8,128)(2,1)}, u32[]{:S(2)}, u32[]{:S(2)}) collective-permute-start(bf16[256,1024]{1,0:T(8,128)(2,1)} %collective-permute-done.7.refs_0_.refs_3_), channel_id=1, source_target_pairs={{0,1},{1,0},{2,3},{3,2},{4,5},{5,4},{6,7},{7,6},{8,9},{9,8},{10,11... | collective-permute-start | bytes 1572872 | tf_op jit(solution)/shard_map/ppermute | solution.py:538
  83.7 19.9 %collective-permute-start.14 = (bf16[256,1024]{1,0:T(8,128)(2,1)}, bf16[256,1024]{1,0:T(8,128)(2,1)}, u32[]{:S(2)}, u32[]{:S(2)}) collective-permute-start(bf16[256,1024]{1,0:T(8,128)(2,1)} %collective-permute-done.13.refs_6_.refs_2_), channel_id=1, source_target_pairs={{0,1},{1,0},{2,3},{3,2},{4,5},{5,4},{6,7},{7,6},{8,9},{9,8},{10,11... | collective-permute-start | bytes 1572872 | tf_op jit(solution)/shard_map/ppermute | solution.py:538
  85.0 18.6 %collective-permute-start.10 = (bf16[256,1024]{1,0:T(8,128)(2,1)}, bf16[256,1024]{1,0:T(8,128)(2,1)}, u32[]{:S(2)}, u32[]{:S(2)}) collective-permute-start(bf16[256,1024]{1,0:T(8,128)(2,1)} %collective-permute-done.2.refs_3_.refs_0_), channel_id=1, source_target_pairs={{0,2},{1,3},{2,4},{3,5},{4,6},{5,7},{6,0},{7,1},{8,10},{9,11},{10,... | collective-permute-start | bytes 1572872 | tf_op jit(solution)/shard_map/ppermute | solution.py:538
  122.6 74.1 %collective-permute-start.31 = (bf16[3,1024,512]{2,1,0:T(8,128)(2,1)}, bf16[3,1024,512]{2,1,0:T(8,128)(2,1)}, u32[]{:S(2)}, u32[]{:S(2)}) collective-permute-start(bf16[3,1024,512]{2,1,0:T(8,128)(2,1)} %get-tuple-element.82), channel_id=1, source_target_pairs={{0,8},{8,0},{16,24},{24,16},{1,9},{9,1},{17,25},{25,17},{2,10},{10... | collective-permute-start | bytes 9437192 | tf_op jit(solution)/shard_map/ppermute | solution.py:538
  137.5 11.4 %collective-permute-start.26 = (bf16[136,1024]{1,0:T(8,128)(2,1)S(1)}, bf16[136,1024]{1,0:T(8,128)(2,1)S(1)}, u32[]{:S(2)}, u32[]{:S(2)}) collective-permute-start(bf16[136,1024]{1,0:T(8,128)(2,1)S(1)} %copy-done.35), channel_id=1, source_target_pairs={{0,16},{8,24},{16,0},{24,8},{1,17},{9,25},{17,1},{25,9},{2,18},{10... | collective-permute-start | bytes 835592 | tf_op jit(solution)/shard_map/ppermute | solution.py:538
  147.0 22.2 %collective-permute-start.5 = (bf16[136,1024]{1,0:T(8,128)(2,1)S(1)}, bf16[136,1024]{1,0:T(8,128)(2,1)S(1)}, u32[]{:S(2)}, u32[]{:S(2)}) collective-permute-start(bf16[136,1024]{1,0:T(8,128)(2,1)S(1)} %copy-done.27), channel_id=1, source_target_pairs={{0,1},{1,0},{2,3},{3,2},{4,5},{5,4},{6,7},{7,6},{8,9},{9,8},{10,11... | collective-permute-start | bytes 835592 | tf_op jit(solution)/shard_map/ppermute | solution.py:538
  147.6 16.4 %collective-permute-start.28 = (bf16[136,1024]{1,0:T(8,128)(2,1)S(1)}, bf16[136,1024]{1,0:T(8,128)(2,1)S(1)}, u32[]{:S(2)}, u32[]{:S(2)}) collective-permute-start(bf16[136,1024]{1,0:T(8,128)(2,1)S(1)} %copy-done.33), channel_id=1, source_target_pairs={{0,16},{8,24},{16,0},{24,8},{1,17},{9,25},{17,1},{25,9},{2,18},{10... | collective-permute-start | bytes 835592 | tf_op jit(solution)/shard_map/ppermute | solution.py:538
  148.9 13.6 %collective-permute-start.20 = (bf16[136,1024]{1,0:T(8,128)(2,1)S(1)}, bf16[136,1024]{1,0:T(8,128)(2,1)S(1)}, u32[]{:S(2)}, u32[]{:S(2)}) collective-permute-start(bf16[136,1024]{1,0:T(8,128)(2,1)S(1)} %copy-done.37), channel_id=1, source_target_pairs={{0,1},{1,0},{2,3},{3,2},{4,5},{5,4},{6,7},{7,6},{8,9},{9,8},{10,11... | collective-permute-start | bytes 835592 | tf_op jit(solution)/shard_map/ppermute | solution.py:538
  153.0 15.5 %collective-permute-start.27 = (bf16[136,1024]{1,0:T(8,128)(2,1)S(1)}, bf16[136,1024]{1,0:T(8,128)(2,1)S(1)}, u32[]{:S(2)}, u32[]{:S(2)}) collective-permute-start(bf16[136,1024]{1,0:T(8,128)(2,1)S(1)} %add_convert_fusion.2), channel_id=1, source_target_pairs={{0,1},{1,0},{2,3},{3,2},{4,5},{5,4},{6,7},{7,6},{8,9},{9,8},{10,11... | collective-permute-start | bytes 835592 | tf_op jit(solution)/shard_map/ppermute | solution.py:538
  174.5 22.2 %collective-permute-start.32 = (bf16[3,256,512]{2,1,0:T(8,128)(2,1)S(1)}, bf16[3,256,512]{2,1,0:T(8,128)(2,1)S(1)}, u32[]{:S(2)}, u32[]{:S(2)}) collective-permute-start(bf16[3,256,512]{2,1,0:T(8,128)(2,1)S(1)} %get-tuple-element.83), channel_id=1, source_target_pairs={{0,8},{8,0},{16,24},{24,16},{1,9},{9,1},{17,25},{25,17},{2,10},{10... | collective-permute-start | bytes 2359304 | tf_op jit(solution)/shard_map/ppermute | solution.py:538
  (50 other events, 479.7 us)

commit v4 on v3

--- a/solution.py
+++ b/solution.py
@@ -577,7 +577,7 @@
     at = jnp.stack([me // blocks, me % blocks, sibling // blocks, sibling % blocks])
     at = at.astype(jnp.int32)
     part, saved = [None] * 4, []
-    for group in ((0,), (2,), (1, 3)):
+    for group in ((0,), (1,), (2,), (3,)):
         pieces = [piece for s in group for piece in (c[s], x[s], y[s], d[s])]
         sums, keep = route(group, cap, extra, at, gates, pieces, w_own, w_sib)
         saved.append(keep)
@@ -593,9 +593,7 @@
     (total,) = common(where_at, kept, pieces, shared_weights, total)
     pieces = (c[3], x[2], y[2])
     (total,) = common(where_at, kept, pieces, shared_weights, total)
-    pieces = (d[1], x[3], y[3])
-    (total,) = common(where_at, kept, pieces, shared_weights, total)
-    pieces = (d[2], d[3])
+    pieces = (d[1], x[3], y[3], d[2], d[3])
     mine, other = common(where_at, kept, pieces, shared_weights, total, last=True)
 
     def plus(*terms):
@@ -612,7 +610,7 @@
 
     part_x, part_y = list(px), list(py)
     for s in range(planes):
-        if s in (0, 3):
+        if s % 2:
             part_y[s] = plus(py[s], send("x", pd[s]))
         else:
             part_x[s] = plus(px[s], send("y", pd[s]))

time: 201 us -> 199 us (0.990)
  waiting for transfers between devices: 86.9 us -> 84.1 us
    ppermute x33, waiting for transfers between devices: 86.9 us -> 65.5 us  [send(): return lax.ppermute(array, *routes[way])]
    all_to_all x1, waiting for transfers between devices: 0.01 us -> 18.6 us  [shared_rows_body(): inward = lax.all_to_all(outward, ('dp', 'expert'), 0, 0, tiled=True)]
    pallas_call x5 -> x4, Pallas kernels: 19.8 us -> 18 us  [common(): pl.pallas_call(functools.partial(common_kernel, n, first, last), out_shap...]
    pallas_call x3 -> x4, Pallas kernels: 18.2 us -> 19.8 us  [route(): pl.pallas_call(functools.partial(route_kernel, group, n, cap), out_shape=...]
    unnamed x80 -> x98, local copies, waits for them, and re-layouts: 15.5 us -> 15.6 us
  transfers between devices with their start and end apart: 34 -> 34, of which waited for: 16 -> 16; matrix products, arithmetic and copies ran while one was open for 2% -> 2% of each run, Pallas kernels for 16% -> 18%
where the time goes in v4:
time: 199 us; the launch traced here: 198 us
  waiting for transfers between devices  84.1 us (42%)
  Pallas kernels  51.1 us (26%)
  starting transfers between devices  43 us (22%)
  local copies, waits for them, and re-layouts  16.4 us (8%)
  other arithmetic  2.21 us (1%)
    ppermute x33, waiting for transfers between devices, send(): return lax.ppermute(array, *routes[way])  65.5 us
    ppermute x33, starting transfers between devices, send(): return lax.ppermute(array, *routes[way])  40.4 us
    pallas_call x4, Pallas kernels, route(): pl.pallas_call(functools.partial(route_kernel, group, n, cap), out_shape=...  19.8 us
    all_to_all x1, waiting for transfers between devices, shared_rows_body(): inward = lax.all_to_all(outward, ('dp', 'expert'), 0, 0, tiled=True)  18.6 us
    pallas_call x4, Pallas kernels, common(): pl.pallas_call(functools.partial(common_kernel, n, first, last), out_shap...  18 us
    unnamed x98, local copies, waits for them, and re-layouts  15.6 us
    pallas_call x1, Pallas kernels, weights(): pl.pallas_call(functools.partial(weights_kernel, groups), out_shape=[jax....  6.59 us
  transfers between devices with their start and end apart: 34, of which 16 were waited for; matrix products, arithmetic and copies ran while one was open for 2% of the time, Pallas kernels for 18%

profile of v4, /device:TPU:0, one launch (start us, length us, event | category | flops | bytes accessed | tf_op | source)
XLA Modules:
  0.0 198.5 jit_solution(7854848228636693871)
XLA Ops:
  3.1 2.6 %collective-permute-start.7 = (bf16[256,1024]{1,0:T(8,128)(2,1)}, bf16[256,1024]{1,0:T(8,128)(2,1)S(1)}, u32[]{:S(2)}, u32[]{:S(2)}) collective-permute-start(bf16[256,1024]{1,0:T(8,128)(2,1)} %join.1.refs_0_), channel_id=1, source_target_pairs={{0,2},{1,3},{2,4},{3,5},{4,6},{5,7},{6,0},{7,1},{8,10},{9,11},{10,... | collective-permute-start | bytes 1572872 | tf_op jit(solution)/shard_map/ppermute | solution.py:538
  5.7 14.8 %collective-permute-done.7.refs_0_.refs_3_ = bf16[256,1024]{1,0:T(8,128)(2,1)S(1)} collective-permute-done((bf16[256,1024]{1,0:T(8,128)(2,1)}, bf16[256,1024]{1,0:T(8,128)(2,1)S(1)}, u32[]{:S(2)}, u32[]{:S(2)}) %collective-permute-start.7) | collective-permute-done | bytes 524320 | tf_op jit(solution)/shard_map/ppermute | solution.py:538
  21.3 3.8 %collective-permute-start.15 = (bf16[256,1024]{1,0:T(8,128)(2,1)}, bf16[256,1024]{1,0:T(8,128)(2,1)}, u32[]{:S(2)}, u32[]{:S(2)}) collective-permute-start(bf16[256,1024]{1,0:T(8,128)(2,1)} %join.1.refs_0_), channel_id=1, source_target_pairs={{0,6},{1,7},{2,0},{3,1},{4,2},{5,3},{6,4},{7,5},{8,14},{9,15},{10,... | collective-permute-start | bytes 1572872 | tf_op jit(solution)/shard_map/ppermute | solution.py:538
  28.1 9.9 %collective-permute-done.22.refs_0_.refs_3_ = bf16[256,1024]{1,0:T(8,128)(2,1)} collective-permute-done((bf16[256,1024]{1,0:T(8,128)(2,1)S(1)}, bf16[256,1024]{1,0:T(8,128)(2,1)}, u32[]{:S(2)}, u32[]{:S(2)}) %collective-permute-start.22) | collective-permute-done | bytes 524320 | tf_op jit(solution)/shard_map/ppermute | solution.py:538
  39.5 7.1 %collective-permute-done.15.refs_0_ = bf16[256,1024]{1,0:T(8,128)(2,1)} collective-permute-done((bf16[256,1024]{1,0:T(8,128)(2,1)}, bf16[256,1024]{1,0:T(8,128)(2,1)}, u32[]{:S(2)}, u32[]{:S(2)}) %collective-permute-start.15) | collective-permute-done | bytes 524320 | tf_op jit(solution)/shard_map/ppermute | solution.py:538
  54.3 2.7 %all-to-all-start = ((bf16[32,2,128]{2,1,0:T(2,128)(2,1)}), bf16[32,2,128]{2,1,0:T(2,128)(2,1)S(1)}, u32[]{:S(2)}, u32[]{:S(2)}) async-start(bf16[32,2,128]{2,1,0:T(2,128)(2,1)} %copy.39), calls=%async_computation | async-start | bytes 32768 | tf_op jit(solution)/shard_map/all_to_all | solution.py:561
  57.4 4.4 %collective-permute-done.17.refs_2_ = bf16[256,1024]{1,0:T(8,128)(2,1)} collective-permute-done((bf16[256,1024]{1,0:T(8,128)(2,1)}, bf16[256,1024]{1,0:T(8,128)(2,1)}, u32[]{:S(2)}, u32[]{:S(2)}) %collective-permute-start.17) | collective-permute-done | bytes 524320 | tf_op jit(solution)/shard_map/ppermute | solution.py:538
  63.8 18.6 %all-to-all-done = bf16[32,2,128]{2,1,0:T(2,128)(2,1)S(1)} async-done(((bf16[32,2,128]{2,1,0:T(2,128)(2,1)}), bf16[32,2,128]{2,1,0:T(2,128)(2,1)S(1)}, u32[]{:S(2)}, u32[]{:S(2)}) %all-to-all-start) | async-done | bytes 16416 | tf_op jit(solution)/shard_map/all_to_all | solution.py:561
  87.2 4.9 %route.4 = (f32[136,1024]{1,0:T(8,128)S(1)}, bf16[136,1024]{1,0:T(8,128)(2,1)S(1)}, bf16[136,1024]{1,0:T(8,128)(2,1)S(1)}, bf16[136,1024]{1,0:T(8,128)(2,1)S(1)}...) custom-call(s32[4]{0:T(128)S(1)} %pad_add_fusion.at_ref, ...), custom_call_target="tpu_custom_call" | custom-call | flops 2013265920 | bytes 9437184 | tf_op jit(solution)/shard_map/route/pallas_call | solution.py:262
  92.9 5.4 %route.7 = (f32[136,1024]{1,0:T(8,128)S(1)}, bf16[136,1024]{1,0:T(8,128)(2,1)S(1)}, bf16[136,1024]{1,0:T(8,128)(2,1)S(1)}, bf16[136,1024]{1,0:T(8,128)(2,1)S(1)}...) custom-call(s32[4]{0:T(128)S(1)} %pad_add_fusion.at_ref, ...), custom_call_target="tpu_custom_call" | custom-call | flops 2013265920 | bytes 9437184 | tf_op jit(solution)/shard_map/route/pallas_call | solution.py:262
  101.3 5.2 %route.6 = (f32[136,1024]{1,0:T(8,128)S(1)}, bf16[136,1024]{1,0:T(8,128)(2,1)S(1)}, bf16[136,1024]{1,0:T(8,128)(2,1)S(1)}, bf16[136,1024]{1,0:T(8,128)(2,1)S(1)}...) custom-call(s32[4]{0:T(128)S(1)} %pad_add_fusion.at_ref, ...), custom_call_target="tpu_custom_call" | custom-call | flops 2013265920 | bytes 9437184 | tf_op jit(solution)/shard_map/route/pallas_call | solution.py:262
  108.1 4.3 %route.5 = (f32[136,1024]{1,0:T(8,128)S(1)}, bf16[136,1024]{1,0:T(8,128)(2,1)S(1)}, bf16[136,1024]{1,0:T(8,128)(2,1)S(1)}, bf16[136,1024]{1,0:T(8,128)(2,1)S(1)}...) custom-call(s32[4]{0:T(128)S(1)} %pad_add_fusion.at_ref, ...), custom_call_target="tpu_custom_call" | custom-call | flops 2013265920 | bytes 9437184 | tf_op jit(solution)/shard_map/route/pallas_call | solution.py:262
  115.5 6.6 %weights.1 = (bf16[3,1024,512]{2,1,0:T(8,128)(2,1)S(1)}, bf16[3,1024,512]{2,1,0:T(8,128)(2,1)}) custom-call(bf16[2,192,1024]{2,1,0:T(8,128)(2,1)S(1)} %get-tuple-element.69.refs_0_, bf16[2,192,1024]{2,1,0:T(8,128)(2,1)S(1)} %get-tuple-element.70.refs_1_, bf16[2,192,512]{2,1,0:T(8,128)(2,1)S(1)} %get-tuple-element.71.refs_2_, ...), custom_call_target="tpu_custom_call" | custom-call | flops 4831838208 | bytes 11010048 | tf_op jit(solution)/shard_map/weights/pallas_call | solution.py:373
  126.9 4.5 %common.4 = (f32[128,1024]{1,0:T(8,128)S(1)}, f32[3,512,512]{2,1,0:T(8,128)S(1)}) custom-call(s32[2]{0:T(128)S(1)} %pad_add_fusion.1.where_ref, bf16[256,1024]{1,0:T(8,128)(2,1)S(1)} %copy-done.9, bf16[256,1024]{1,0:T(8,128)(2,1)S(1)} %copy-done.23, bf16[256,1024]{1,0:T(8,128)(2,1)} %collective-permute-done.1.refs_2_, bf16[256,1024]{1,0:T(8,128)(2,1)S(1)} %copy-done.20, ...), custom_call_target="tpu_custom_call" | custom-call | flops 2415919104 | bytes 5242880 | tf_op jit(solution)/shard_map/common/pallas_call | solution.py:336
  131.5 4.0 %common.5.refs_4_ = f32[3,512,512]{2,1,0:T(8,128)S(1)} custom-call(s32[2]{0:T(128)S(1)} %pad_add_fusion.1.where_ref, bf16[256,1024]{1,0:T(8,128)(2,1)} %collective-permute-done.2.refs_3_.refs_0_, bf16[256,1024]{1,0:T(8,128)(2,1)S(1)} %copy-done.5, bf16[256,1024]{1,0:T(8,128)(2,1)S(1)} %copy-done.7, ...), custom_call_target="tpu_custom_call" | custom-call | flops 2415919104 | bytes 5242880 | tf_op jit(solution)/shard_map/common/pallas_call | solution.py:336
  135.5 3.8 %common.6.refs_6_ = f32[3,512,512]{2,1,0:T(8,128)S(1)} custom-call(s32[2]{0:T(128)S(1)} %pad_add_fusion.1.where_ref, bf16[256,1024]{1,0:T(8,128)(2,1)} %collective-permute-done.15.refs_0_, bf16[256,1024]{1,0:T(8,128)(2,1)} %collective-permute-done.23.refs_1_, bf16[256,1024]{1,0:T(8,128)(2,1)} %collective-permute-done.24.refs_2_, ...), custom_call_target="tpu_custom_call" | custom-call | flops 1811939328 | bytes 4718592 | tf_op jit(solution)/shard_map/common/pallas_call | solution.py:336
  140.5 5.6 %common.7 = (f32[3,256,512]{2,1,0:T(8,128)S(1)}, bf16[3,256,512]{2,1,0:T(8,128)(2,1)S(1)}) custom-call(s32[2]{0:T(128)S(1)} %pad_add_fusion.1.where_ref, bf16[256,1024]{1,0:T(8,128)(2,1)S(1)} %copy-done.25, bf16[256,1024]{1,0:T(8,128)(2,1)} %collective-permute-done.16.refs_1_, bf16[256,1024]{1,0:T(8,128)(2,1)} %collective-permute-done.17.refs_2_, ...), custom_call_target="tpu_custom_call" | custom-call | flops 3019898880 | bytes 5767168 | tf_op jit(solution)/shard_map/common/pallas_call | solution.py:336
  150.8 7.2 %collective-permute-done.12 = bf16[136,1024]{1,0:T(8,128)(2,1)S(1)} collective-permute-done((bf16[136,1024]{1,0:T(8,128)(2,1)S(1)}, bf16[136,1024]{1,0:T(8,128)(2,1)S(1)}, u32[]{:S(2)}, u32[]{:S(2)}) %collective-permute-start.12) | collective-permute-done | bytes 278560 | tf_op jit(solution)/shard_map/ppermute | solution.py:538
  166.2 3.7 %collective-permute-done.19 = bf16[136,1024]{1,0:T(8,128)(2,1)S(1)} collective-permute-done((bf16[136,1024]{1,0:T(8,128)(2,1)S(1)}, bf16[136,1024]{1,0:T(8,128)(2,1)S(1)}, u32[]{:S(2)}, u32[]{:S(2)}) %collective-permute-start.19) | collective-permute-done | bytes 278560 | tf_op jit(solution)/shard_map/ppermute | solution.py:538
  170.0 2.1 %collective-permute-start.29 = (bf16[136,1024]{1,0:T(8,128)(2,1)S(1)}, bf16[136,1024]{1,0:T(8,128)(2,1)S(1)}, u32[]{:S(2)}, u32[]{:S(2)}) collective-permute-start(bf16[136,1024]{1,0:T(8,128)(2,1)S(1)} %add_convert_fusion.1), channel_id=1, source_target_pairs={{0,2},{1,3},{2,4},{3,5},{4,6},{5,7},{6,0},{7,1},{8,10},{9,11},{10,... | collective-permute-start | bytes 835592 | tf_op jit(solution)/shard_map/ppermute | solution.py:538
  172.2 2.5 %collective-permute-done.11 = bf16[136,1024]{1,0:T(8,128)(2,1)S(1)} collective-permute-done((bf16[136,1024]{1,0:T(8,128)(2,1)S(1)}, bf16[136,1024]{1,0:T(8,128)(2,1)S(1)}, u32[]{:S(2)}, u32[]{:S(2)}) %collective-permute-start.11) | collective-permute-done | bytes 278560 | tf_op jit(solution)/shard_map/ppermute | solution.py:538
  180.4 3.3 %collective-permute-done.6.refs_2_ = bf16[136,1024]{1,0:T(8,128)(2,1)S(1)} collective-permute-done((bf16[136,1024]{1,0:T(8,128)(2,1)S(1)}, bf16[136,1024]{1,0:T(8,128)(2,1)S(1)}, u32[]{:S(2)}, u32[]{:S(2)}) %collective-permute-start.6) | collective-permute-done | bytes 278560 | tf_op jit(solution)/shard_map/ppermute | solution.py:538
  187.1 6.5 %collective-permute-done.30.refs_4_ = bf16[136,1024]{1,0:T(8,128)(2,1)S(1)} collective-permute-done((bf16[136,1024]{1,0:T(8,128)(2,1)S(1)}, bf16[136,1024]{1,0:T(8,128)(2,1)S(1)}, u32[]{:S(2)}, u32[]{:S(2)}) %collective-permute-start.30) | collective-permute-done | bytes 278560 | tf_op jit(solution)/shard_map/ppermute | solution.py:538
  194.5 3.7 %sums.1 = (bf16[3,1024,512]{2,1,0:T(8,128)(2,1)}, f32[3,256,512]{2,1,0:T(8,128)}) custom-call(bf16[3,1024,512]{2,1,0:T(8,128)(2,1)S(1)} %copy-done.3, f32[3,256,512]{2,1,0:T(8,128)S(1)} %get-tuple-element.91.s_mine, bf16[3,1024,512]{2,1,0:T(8,128)(2,1)} %collective-permute-done.31.e_came, bf16[3,256,512]{2,1,0:T(8,128)(2,1)S(1)} %collective-permute-done.32.s_came), custom_call_target="tpu_custom_call" | custom-call | tf_op jit(solution)/shard_map/sums/pallas_call | solution.py:418
  (173 shorter events, 59.6 us)
Async XLA Ops:
  0.6 62.4 %collective-permute-start.3 = (bf16[3,1024,512]{2,1,0:T(8,128)(2,1)}, bf16[3,1024,512]{2,1,0:T(8,128)(2,1)S(1)}, u32[]{:S(2)}, u32[]{:S(2)}) collective-permute-start(bf16[3,1024,512]{2,1,0:T(8,128)(2,1)} %bitcast.54), channel_id=1, source_target_pairs={{0,8},{8,0},{16,24},{24,16},{1,9},{9,1},{17,25},{25,17},{2,10},{10... | collective-permute-start | bytes 9437192 | tf_op jit(solution)/shard_map/ppermute | solution.py:538
  3.1 17.4 %collective-permute-start.7 = (bf16[256,1024]{1,0:T(8,128)(2,1)}, bf16[256,1024]{1,0:T(8,128)(2,1)S(1)}, u32[]{:S(2)}, u32[]{:S(2)}) collective-permute-start(bf16[256,1024]{1,0:T(8,128)(2,1)} %join.1.refs_0_), channel_id=1, source_target_pairs={{0,2},{1,3},{2,4},{3,5},{4,6},{5,7},{6,0},{7,1},{8,10},{9,11},{10,... | collective-permute-start | bytes 1572872 | tf_op jit(solution)/shard_map/ppermute | solution.py:538
  21.3 16.7 %collective-permute-start.22 = (bf16[256,1024]{1,0:T(8,128)(2,1)S(1)}, bf16[256,1024]{1,0:T(8,128)(2,1)}, u32[]{:S(2)}, u32[]{:S(2)}) collective-permute-start(bf16[256,1024]{1,0:T(8,128)(2,1)S(1)} %collective-permute-done.7.refs_0_.refs_3_), channel_id=1, source_target_pairs={{0,2},{1,3},{2,4},{3,5},{4,6},{5,7},{6,0},{7,1},{8,10},{9,11},{10,... | collective-permute-start | bytes 1572872 | tf_op jit(solution)/shard_map/ppermute | solution.py:538
  21.3 25.3 %collective-permute-start.15 = (bf16[256,1024]{1,0:T(8,128)(2,1)}, bf16[256,1024]{1,0:T(8,128)(2,1)}, u32[]{:S(2)}, u32[]{:S(2)}) collective-permute-start(bf16[256,1024]{1,0:T(8,128)(2,1)} %join.1.refs_0_), channel_id=1, source_target_pairs={{0,6},{1,7},{2,0},{3,1},{4,2},{5,3},{6,4},{7,5},{8,14},{9,15},{10,... | collective-permute-start | bytes 1572872 | tf_op jit(solution)/shard_map/ppermute | solution.py:538
  25.1 23.5 %collective-permute-start.1 = (bf16[256,1024]{1,0:T(8,128)(2,1)}, bf16[256,1024]{1,0:T(8,128)(2,1)}, u32[]{:S(2)}, u32[]{:S(2)}) collective-permute-start(bf16[256,1024]{1,0:T(8,128)(2,1)} %join.1.refs_0_), channel_id=1, source_target_pairs={{0,16},{8,24},{16,0},{24,8},{1,17},{9,25},{17,1},{25,9},{2,18},{10... | collective-permute-start | bytes 1572872 | tf_op jit(solution)/shard_map/ppermute | solution.py:538
  26.6 23.4 %collective-permute-start = (bf16[256,1024]{1,0:T(8,128)(2,1)}, bf16[256,1024]{1,0:T(8,128)(2,1)S(1)}, u32[]{:S(2)}, u32[]{:S(2)}) collective-permute-start(bf16[256,1024]{1,0:T(8,128)(2,1)} %join.1.refs_0_), channel_id=1, source_target_pairs={{0,1},{1,0},{2,3},{3,2},{4,5},{5,4},{6,7},{7,6},{8,9},{9,8},{10,11... | collective-permute-start | bytes 1572872 | tf_op jit(solution)/shard_map/ppermute | solution.py:538
  38.0 13.7 %collective-permute-start.23 = (bf16[256,1024]{1,0:T(8,128)(2,1)}, bf16[256,1024]{1,0:T(8,128)(2,1)}, u32[]{:S(2)}, u32[]{:S(2)}) collective-permute-start(bf16[256,1024]{1,0:T(8,128)(2,1)} %collective-permute-done.22.refs_0_.refs_3_), channel_id=1, source_target_pairs={{0,1},{1,0},{2,3},{3,2},{4,5},{5,4},{6,7},{7,6},{8,9},{9,8},{10,11... | collective-permute-start | bytes 1572872 | tf_op jit(solution)/shard_map/ppermute | solution.py:538
  46.6 15.2 %collective-permute-start.17 = (bf16[256,1024]{1,0:T(8,128)(2,1)}, bf16[256,1024]{1,0:T(8,128)(2,1)}, u32[]{:S(2)}, u32[]{:S(2)}) collective-permute-start(bf16[256,1024]{1,0:T(8,128)(2,1)} %collective-permute-done.15.refs_0_), channel_id=1, source_target_pairs={{0,16},{8,24},{16,0},{24,8},{1,17},{9,25},{17,1},{25,9},{2,18},{10... | collective-permute-start | bytes 1572872 | tf_op jit(solution)/shard_map/ppermute | solution.py:538
  48.6 34.3 %collective-permute-start.2 = (bf16[256,1024]{1,0:T(8,128)(2,1)}, bf16[256,1024]{1,0:T(8,128)(2,1)}, u32[]{:S(2)}, u32[]{:S(2)}) collective-permute-start(bf16[256,1024]{1,0:T(8,128)(2,1)} %collective-permute-done.1.refs_2_), channel_id=1, source_target_pairs={{0,1},{1,0},{2,3},{3,2},{4,5},{5,4},{6,7},{7,6},{8,9},{9,8},{10,11... | collective-permute-start | bytes 1572872 | tf_op jit(solution)/shard_map/ppermute | solution.py:538
  50.9 33.9 %collective-permute-start.24 = (bf16[256,1024]{1,0:T(8,128)(2,1)}, bf16[256,1024]{1,0:T(8,128)(2,1)}, u32[]{:S(2)}, u32[]{:S(2)}) collective-permute-start(bf16[256,1024]{1,0:T(8,128)(2,1)} %collective-permute-done.22.refs_0_.refs_3_), channel_id=1, source_target_pairs={{0,16},{8,24},{16,0},{24,8},{1,17},{9,25},{17,1},{25,9},{2,18},{10... | collective-permute-start | bytes 1572872 | tf_op jit(solution)/shard_map/ppermute | solution.py:538
  51.7 34.6 %collective-permute-start.25 = (bf16[256,1024]{1,0:T(8,128)(2,1)}, bf16[256,1024]{1,0:T(8,128)(2,1)}, u32[]{:S(2)}, u32[]{:S(2)}) collective-permute-start(bf16[256,1024]{1,0:T(8,128)(2,1)} %collective-permute-done.23.refs_1_), channel_id=1, source_target_pairs={{0,16},{8,24},{16,0},{24,8},{1,17},{9,25},{17,1},{25,9},{2,18},{10... | collective-permute-start | bytes 1572872 | tf_op jit(solution)/shard_map/ppermute | solution.py:538
  54.3 28.1 %all-to-all-start = ((bf16[32,2,128]{2,1,0:T(2,128)(2,1)}), bf16[32,2,128]{2,1,0:T(2,128)(2,1)S(1)}, u32[]{:S(2)}, u32[]{:S(2)}) async-start(bf16[32,2,128]{2,1,0:T(2,128)(2,1)} %copy.39), calls=%async_computation | async-start | bytes 32768 | tf_op jit(solution)/shard_map/all_to_all | solution.py:561
  61.8 39.5 %collective-permute-start.16 = (bf16[256,1024]{1,0:T(8,128)(2,1)}, bf16[256,1024]{1,0:T(8,128)(2,1)}, u32[]{:S(2)}, u32[]{:S(2)}) collective-permute-start(bf16[256,1024]{1,0:T(8,128)(2,1)} %collective-permute-done.15.refs_0_), channel_id=1, source_target_pairs={{0,1},{1,0},{2,3},{3,2},{4,5},{5,4},{6,7},{7,6},{8,9},{9,8},{10,11... | collective-permute-start | bytes 1572872 | tf_op jit(solution)/shard_map/ppermute | solution.py:538
  63.0 38.3 %collective-permute-start.18 = (bf16[256,1024]{1,0:T(8,128)(2,1)}, bf16[256,1024]{1,0:T(8,128)(2,1)}, u32[]{:S(2)}, u32[]{:S(2)}) collective-permute-start(bf16[256,1024]{1,0:T(8,128)(2,1)} %collective-permute-done.17.refs_2_), channel_id=1, source_target_pairs={{0,1},{1,0},{2,3},{3,2},{4,5},{5,4},{6,7},{7,6},{8,9},{9,8},{10,11... | collective-permute-start | bytes 1572872 | tf_op jit(solution)/shard_map/ppermute | solution.py:538
  83.7 24.4 %collective-permute-start.9 = (bf16[256,1024]{1,0:T(8,128)(2,1)S(1)}, bf16[256,1024]{1,0:T(8,128)(2,1)S(1)}, u32[]{:S(2)}, u32[]{:S(2)}) collective-permute-start(bf16[256,1024]{1,0:T(8,128)(2,1)S(1)} %copy-done.19), channel_id=1, source_target_pairs={{0,16},{8,24},{16,0},{24,8},{1,17},{9,25},{17,1},{25,9},{2,18},{10... | collective-permute-start | bytes 1572872 | tf_op jit(solution)/shard_map/ppermute | solution.py:538
  84.8 23.3 %collective-permute-start.8 = (bf16[256,1024]{1,0:T(8,128)(2,1)S(1)}, bf16[256,1024]{1,0:T(8,128)(2,1)S(1)}, u32[]{:S(2)}, u32[]{:S(2)}) collective-permute-start(bf16[256,1024]{1,0:T(8,128)(2,1)S(1)} %copy-done.19), channel_id=1, source_target_pairs={{0,1},{1,0},{2,3},{3,2},{4,5},{5,4},{6,7},{7,6},{8,9},{9,8},{10,11... | collective-permute-start | bytes 1572872 | tf_op jit(solution)/shard_map/ppermute | solution.py:538
  86.3 21.9 %collective-permute-start.10 = (bf16[256,1024]{1,0:T(8,128)(2,1)}, bf16[256,1024]{1,0:T(8,128)(2,1)S(1)}, u32[]{:S(2)}, u32[]{:S(2)}) collective-permute-start(bf16[256,1024]{1,0:T(8,128)(2,1)} %collective-permute-done.2.refs_3_.refs_0_), channel_id=1, source_target_pairs={{0,2},{1,3},{2,4},{3,5},{4,6},{5,7},{6,0},{7,1},{8,10},{9,11},{10,... | collective-permute-start | bytes 1572872 | tf_op jit(solution)/shard_map/ppermute | solution.py:538
  123.7 70.8 %collective-permute-start.31 = (bf16[3,1024,512]{2,1,0:T(8,128)(2,1)}, bf16[3,1024,512]{2,1,0:T(8,128)(2,1)}, u32[]{:S(2)}, u32[]{:S(2)}) collective-permute-start(bf16[3,1024,512]{2,1,0:T(8,128)(2,1)} %get-tuple-element.92), channel_id=1, source_target_pairs={{0,8},{8,0},{16,24},{24,16},{1,9},{9,1},{17,25},{25,17},{2,10},{10... | collective-permute-start | bytes 9437192 | tf_op jit(solution)/shard_map/ppermute | solution.py:538
  146.2 19.3 %collective-permute-start.4 = (bf16[136,1024]{1,0:T(8,128)(2,1)S(1)}, bf16[136,1024]{1,0:T(8,128)(2,1)S(1)}, u32[]{:S(2)}, u32[]{:S(2)}) collective-permute-start(bf16[136,1024]{1,0:T(8,128)(2,1)S(1)} %copy-done.36), channel_id=1, source_target_pairs={{0,16},{8,24},{16,0},{24,8},{1,17},{9,25},{17,1},{25,9},{2,18},{10... | collective-permute-start | bytes 835592 | tf_op jit(solution)/shard_map/ppermute | solution.py:538
  147.8 12.9 %collective-permute-start.28 = (bf16[136,1024]{1,0:T(8,128)(2,1)S(1)}, bf16[136,1024]{1,0:T(8,128)(2,1)S(1)}, u32[]{:S(2)}, u32[]{:S(2)}) collective-permute-start(bf16[136,1024]{1,0:T(8,128)(2,1)S(1)} %copy-done.42), channel_id=1, source_target_pairs={{0,16},{8,24},{16,0},{24,8},{1,17},{9,25},{17,1},{25,9},{2,18},{10... | collective-permute-start | bytes 835592 | tf_op jit(solution)/shard_map/ppermute | solution.py:538
  149.9 14.1 %collective-permute-start.27 = (bf16[136,1024]{1,0:T(8,128)(2,1)S(1)}, bf16[136,1024]{1,0:T(8,128)(2,1)S(1)}, u32[]{:S(2)}, u32[]{:S(2)}) collective-permute-start(bf16[136,1024]{1,0:T(8,128)(2,1)S(1)} %add_convert_fusion.2), channel_id=1, source_target_pairs={{0,1},{1,0},{2,3},{3,2},{4,5},{5,4},{6,7},{7,6},{8,9},{9,8},{10,11... | collective-permute-start | bytes 835592 | tf_op jit(solution)/shard_map/ppermute | solution.py:538
  158.0 11.9 %collective-permute-start.19 = (bf16[136,1024]{1,0:T(8,128)(2,1)S(1)}, bf16[136,1024]{1,0:T(8,128)(2,1)S(1)}, u32[]{:S(2)}, u32[]{:S(2)}) collective-permute-start(bf16[136,1024]{1,0:T(8,128)(2,1)S(1)} %copy-done.38), channel_id=1, source_target_pairs={{0,1},{1,0},{2,3},{3,2},{4,5},{5,4},{6,7},{7,6},{8,9},{9,8},{10,11... | collective-permute-start | bytes 835592 | tf_op jit(solution)/shard_map/ppermute | solution.py:538
  160.7 13.9 %collective-permute-start.11 = (bf16[136,1024]{1,0:T(8,128)(2,1)S(1)}, bf16[136,1024]{1,0:T(8,128)(2,1)S(1)}, u32[]{:S(2)}, u32[]{:S(2)}) collective-permute-start(bf16[136,1024]{1,0:T(8,128)(2,1)S(1)} %copy-done.40), channel_id=1, source_target_pairs={{0,1},{1,0},{2,3},{3,2},{4,5},{5,4},{6,7},{7,6},{8,9},{9,8},{10,11... | collective-permute-start | bytes 835592 | tf_op jit(solution)/shard_map/ppermute | solution.py:538
  174.6 19.9 %collective-permute-start.32 = (bf16[3,256,512]{2,1,0:T(8,128)(2,1)S(1)}, bf16[3,256,512]{2,1,0:T(8,128)(2,1)S(1)}, u32[]{:S(2)}, u32[]{:S(2)}) collective-permute-start(bf16[3,256,512]{2,1,0:T(8,128)(2,1)S(1)} %get-tuple-element.93), channel_id=1, source_target_pairs={{0,8},{8,0},{16,24},{24,16},{1,9},{9,1},{17,25},{25,17},{2,10},{10... | collective-permute-start | bytes 2359304 | tf_op jit(solution)/shard_map/ppermute | solution.py:538
  (59 other events, 520.5 us)
